TPU v7x, 128 devices: a whole 4x4x4 slice. The times are simulated.
128 devices in a mesh: wide: 8 (over x, y_hi), narrow: 16 (over y_lo, z, core).
Axes of the slice: x: 4, y: 4 (y_hi: 2, y_lo: 2; y = y_hi * 2 + y_lo), z: 4, core: 2. Of those that a mesh axis runs over, the one named last changes fastest.
Arguments:
- volume_field: float32 [2, 8, 128, 256, 512], P(None, None, 'wide', 'narrow'), may hold values from -6 to 6
- coefficients: bfloat16 [3, 128, 256, 512], P(None, 'wide', 'narrow'), may hold values from 0.25 to 1
- density: float32 [2, 8, 65536], P(None, None, 'narrow'), may hold values from -6 to 6
- boundary_matrix: bfloat16 [2, 4, 512, 65536], P(None, None, 'wide', 'narrow'), may hold values from -0.03125 to 0.03125
- upsample: int32 [128], P('narrow'), may hold values from 1 to 4, as said below
- trace_cell: int32 [8, 16, 256], P('wide', 'narrow'), may hold values from 0 to 255
- trace_row: int32 [8, 16, 256], P('wide', 'narrow'), may hold values from 0 to 511, as said below
- slot_counts: int32 [8, 16], P('wide', 'narrow'), may hold values from 192 to 256, as said below
Outputs:
- volume_out: float32 [2, 8, 128, 256, 512], P(None, None, 'wide', 'narrow')
- boundary_out: float32 [2, 8, 512], P(None, None, ('wide', 'narrow'))
Inputs may be any that keep to these rules, and one draw needn't show every extreme that they name: `trace_row`: live slots of one brick name rows of one owner (rows k * 4 to (k + 1) * 4 - 1) at most 4 times; in every draw one owner is named 4 times by the live slots of every brick. `slot_counts`: some brick has all 256 slots live. `upsample`: some panel group has factor 4 and some has factor 1.
All inputs are finite; a program needn't handle non-finite values.
Results may differ from a plain program's by a relative error of at most 0.0019.
Values sent between devices are 32-bit elements; how exact they have to be, the bound alone decides.
No kernel may reach another device: no remote copies, remote signals or barrier semaphores. Data moves between devices by JAX's collectives and lax.ppermute only.
A program may use at most 192 MiB of HBM per device.

v0:
```python
from functools import partial

import jax
import jax.numpy as jnp
from jax import lax
from jax.experimental import pallas as pl
from jax.experimental.pallas import tpu as pltpu
from jax.sharding import PartitionSpec as P


UMAX = 4
CALLS = 4
F32 = jnp.float32
BF16 = jnp.bfloat16
NT = (((1,), (1,)), ((), ()))
TN = (((0,), (0,)), ((), ()))


def split3(value):
    high = value.astype(BF16)
    rest = value - high.astype(F32)
    middle = rest.astype(BF16)
    low = (rest - middle.astype(F32)).astype(BF16)
    return high, middle, low


VMEM = pl.BlockSpec(memory_space=pltpu.VMEM)
ANY = pl.BlockSpec(memory_space=pl.ANY)
HBM = pl.BlockSpec(memory_space=pltpu.HBM)
LIMIT = pltpu.CompilerParams(vmem_limit_bytes=30 << 20)
SMEM = pl.BlockSpec(memory_space=pltpu.SMEM)


def near(value):
    return pltpu.with_memory_space_constraint(value, pltpu.VMEM)


def afar(value):
    return pltpu.with_memory_space_constraint(value, pltpu.HBM)


def sides_of(size_x):
    even = lax.axis_index("wide") % 2 == 0
    return jnp.where(even, size_x - 1, 0), jnp.where(even, 0, size_x - 1)


def run_all(copies):
    for copy in copies:
        copy.start()
    for copy in copies:
        copy.wait()


def faces_kernel(volume, upward, downward, same, sems):
    same_x, _ = sides_of(volume.shape[1])
    run_all(
        [
            pltpu.make_async_copy(volume.at[:, :, volume.shape[2] - 1], upward, sems.at[0]),
            pltpu.make_async_copy(volume.at[:, :, 0], downward, sems.at[1]),
            pltpu.make_async_copy(volume.at[:, same_x], same, sems.at[2]),
        ]
    )


def faces(volume):
    channels, size_x, size_y, size_z = volume.shape
    return pl.pallas_call(
        faces_kernel,
        in_specs=[HBM],
        out_specs=[VMEM] * 3,
        out_shape=[
            pltpu.VMEM((channels, size_x, size_z), F32),
            pltpu.VMEM((channels, size_x, size_z), F32),
            pltpu.VMEM((channels, size_y, size_z), F32),
        ],
        scratch_shapes=[pltpu.SemaphoreType.DMA((3,))],
        compiler_params=LIMIT,
        name="faces",
    )(afar(volume))


def pack_kernel(volume, before, after, corner, cross, sems):
    same_x, cross_x = sides_of(volume.shape[1])
    channels = volume.shape[0]
    run_all(
        [
            pltpu.make_async_copy(
                volume.at[:, cross_x], cross.at[pl.ds(0, channels)], sems.at[0]
            ),
            pltpu.make_async_copy(before.at[:, same_x], corner.at[0], sems.at[1]),
            pltpu.make_async_copy(after.at[:, same_x], corner.at[1], sems.at[2]),
            pltpu.make_async_copy(before.at[:, cross_x], cross.at[channels], sems.at[3]),
            pltpu.make_async_copy(after.at[:, cross_x], cross.at[channels + 1], sems.at[4]),
        ]
    )


def pack(volume, before, after):
    channels, _, size_y, size_z = volume.shape
    return pl.pallas_call(
        pack_kernel,
        in_specs=[HBM, VMEM, VMEM],
        out_specs=[VMEM] * 2,
        out_shape=[
            pltpu.VMEM((2, channels, size_z), F32),
            pltpu.VMEM((channels + 2, size_y, size_z), F32),
        ],
        scratch_shapes=[pltpu.SemaphoreType.DMA((5,))],
        compiler_params=LIMIT,
        name="pack",
    )(afar(volume), near(before), near(after))


def front_kernel(
    upsample, counts, volume, density, matrix, cells, rows, own, one, two, three, count_out,
    acc, top, sem,
):
    step = pl.program_id(0)
    steps = pl.num_programs(0)
    wide = lax.axis_index("wide")
    channels, size_x, size_y, size_z = volume.shape
    top_copy = pltpu.make_async_copy(volume.at[:, :, :, pl.ds(size_z - 128, 128)], top, sem)

    @pl.when(step == 0)
    def _():
        top_copy.start()
        acc[...] = jnp.zeros_like(acc)
        slots = cells.shape[1]
        cell_count, row_count = count_out.shape
        live = lax.broadcasted_iota(jnp.int32, (1, slots), 1) < counts[0, 0]
        cell_of = jnp.where(live, cells[...], -1)
        cell_hit = lax.broadcasted_iota(jnp.int32, (cell_count, slots), 0) == cell_of
        row_of = rows[...] ^ (wide * (row_count // 8))
        row_hit = lax.broadcasted_iota(jnp.int32, (row_count, slots), 0) == row_of
        cell_hit = jnp.where(cell_hit, 1.0, 0.0).astype(BF16)
        row_hit = jnp.where(row_hit, 1.0, 0.0).astype(BF16)
        counted = lax.dot_general(cell_hit, row_hit, NT, preferred_element_type=F32)
        count_out[...] = counted.astype(BF16)

    width = density.shape[1] // BLOCKS_A_STEP
    group = matrix.shape[2]
    lane = lax.broadcasted_iota(jnp.int32, (channels, width), 1)
    total = acc[...]
    for block in range(BLOCKS_A_STEP):
        columns = pl.ds(block * width, width)
        here = density[:, columns]
        following = jnp.where(lane == width - 1, here, pltpu.roll(here, width - 1, 1))
        factor = upsample[step * BLOCKS_A_STEP + block]
        inverse = jnp.where(
            factor == 1, 1.0, jnp.where(factor == 2, 0.5, jnp.where(factor == 3, 1.0 / 3.0, 0.25))
        )
        for level in range(UMAX):
            share = jnp.where(level < factor, inverse, 0.0)
            blend = level * inverse
            fine = ((1.0 - blend) * share) * here + (blend * share) * following
            both = matrix[:, level, :, columns].reshape(2 * group, width)
            total = total + lax.dot_general(
                fine.astype(BF16), both, NT, preferred_element_type=F32
            )
    acc[...] = total

    @pl.when(step == steps - 1)
    def _():
        waves = channels // 2
        turned = pltpu.roll(total, group, 1)
        bem = jnp.concatenate(
            [total[:waves] - turned[waves:], total[waves:] + turned[:waves]], axis=0
        )
        top_copy.wait()
        cell_count = size_x * size_y
        at = lax.broadcasted_iota(jnp.int32, (cell_count, 128), 1)
        tops = jnp.zeros((cell_count, 128), F32)
        for channel in range(channels):
            value = top[channel].reshape(cell_count, 128)
            tops = jnp.where(at == channel, pltpu.roll(value, (channel + 1) % 128, 1), tops)
        counted = count_out[...]
        traces = jnp.zeros((128, counted.shape[1]), F32)
        for piece in reversed(split3(tops)):
            traces = traces + lax.dot_general(piece, counted, TN, preferred_element_type=F32)
        for part, target in enumerate((own, one, two, three)):
            target[0] = bem
            target[1] = traces[:channels, part * 128 : (part + 1) * 128]


BLOCKS_A_STEP = 2


def front(upsample, counts, volume, density, matrix, cells, rows):
    blocks = upsample.shape[0]
    channels, columns = density.shape
    width = columns * BLOCKS_A_STEP // blocks
    group = matrix.shape[2]
    slots = cells.shape[1]
    message = pltpu.VMEM((2, channels, 128), F32)
    return pl.pallas_call(
        front_kernel,
        grid=(blocks // BLOCKS_A_STEP,),
        in_specs=[
            SMEM,
            SMEM,
            HBM,
            pl.BlockSpec((channels, width), lambda b: (0, b)),
            pl.BlockSpec((2, UMAX, group, width), lambda b: (0, 0, 0, b)),
            pl.BlockSpec((1, slots), lambda b: (0, 0)),
            pl.BlockSpec((1, slots), lambda b: (0, 0)),
        ],
        out_specs=[VMEM] * 5,
        out_shape=[message] * 4 + [pltpu.VMEM((256, 512), BF16)],
        scratch_shapes=[
            pltpu.VMEM((channels, 128), F32),
            pltpu.VMEM(volume.shape[:3] + (128,), F32),
            pltpu.SemaphoreType.DMA,
        ],
        compiler_params=LIMIT,
        name="front",
    )(upsample, counts, afar(volume), density, matrix, cells, rows)


def join_kernel(own, one, two, three, out):
    group = 64
    lane = lax.broadcasted_iota(jnp.int32, own.shape[1:], 1)
    out[0] = jnp.where(lane < group, own[0], pltpu.roll(one[0], group, 1))
    out[1] = jnp.where(lane < group, two[0], pltpu.roll(three[0], group, 1))
    out[2] = (own[1] + one[1]) + (two[1] + three[1])


def join(own, one, two, three):
    return pl.pallas_call(
        join_kernel,
        in_specs=[VMEM] * 4,
        out_specs=VMEM,
        out_shape=pltpu.VMEM((3,) + own.shape[1:], F32),
        compiler_params=LIMIT,
        name="join",
    )(*[near(value) for value in (own, one, two, three)])


def spread_kernel(own, one, two, three, out):
    group = 64
    lane = lax.broadcasted_iota(jnp.int32, own.shape[1:], 1)
    for pair in range(2):
        close = own[pair] + one[pair]
        distant = two[pair] + three[pair]
        out[2 * pair] = jnp.where(lane < group, close, pltpu.roll(distant, group, 1))
        out[2 * pair + 1] = jnp.where(lane < group, pltpu.roll(close, group, 1), distant)
    out[4] = (own[2] + one[2]) + pltpu.roll(two[2] + three[2], group, 1)


def spread(own, one, two, three):
    return pl.pallas_call(
        spread_kernel,
        in_specs=[VMEM] * 4,
        out_specs=VMEM,
        out_shape=pltpu.VMEM((5,) + own.shape[1:], F32),
        compiler_params=LIMIT,
        name="spread",
    )(*[near(value) for value in (own, one, two, three)])


def y_sum(value, before, after):
    half = value.shape[0] // 2
    low, high = value[:half], value[half:]
    at = lax.broadcasted_iota(jnp.int32, low.shape, 0)
    low_down, high_down = pltpu.roll(low, 1, 0), pltpu.roll(high, 1, 0)
    low_up, high_up = pltpu.roll(low, half - 1, 0), pltpu.roll(high, half - 1, 0)
    first, final_row = at == 0, at == half - 1
    low_sum = jnp.where(first, before, low_down) + jnp.where(final_row, high_up, low_up)
    high_sum = jnp.where(first, low_down, high_down) + jnp.where(final_row, after, high_up)
    return jnp.concatenate([low_sum, high_sum], axis=0)


def z_sum(value):
    tiles = value.shape[1] // 128
    pieces = [value[:, 128 * k : 128 * (k + 1)] for k in range(tiles)]
    at = lax.broadcasted_iota(jnp.int32, pieces[0].shape, 1)
    first, final_lane = at == 0, at == 127
    down = [pltpu.roll(piece, 1, 1) for piece in pieces]
    up = [pltpu.roll(piece, 127, 1) for piece in pieces]
    sums = []
    for k in range(tiles):
        below = down[k - 1] if k > 0 else 0.0
        above = up[k + 1] if k < tiles - 1 else 0.0
        sums.append(jnp.where(first, below, down[k]) + jnp.where(final_lane, above, up[k]))
    return jnp.concatenate(sums, axis=1)


def interior_kernel(volume, coefficients, before, after, *refs, first):
    out, planes, tops, scales, twice, mixed = refs[-6:]
    step = pl.program_id(0)
    _, _, size_x, size_y, size_z = volume.shape
    low = size_z - 128

    @pl.when(step == 0)
    def _():
        def prepare(x, carry):
            scale = coefficients[0, x].astype(F32)
            scales[0, x] = scale * (8.0 / 3.0) - coefficients[1, x].astype(F32)
            scales[1, x] = scale * (1.0 / 12.0)
            scales[2, x] = coefficients[2, x].astype(F32)
            return carry

        lax.fori_loop(0, size_x, prepare, 0)
        nothing = jnp.zeros((size_y, size_z), F32)
        for part in range(2):
            for x in (0, size_x + 1):
                twice[part, x] = nothing
                mixed[part, x] = nothing

    waves = before.shape[0] // 2
    wave = first + step

    def along(x, carry):
        for part in range(2):
            value = volume[part, 0, x]
            channel = part * waves + wave
            row = pl.ds(x, 1)
            total = y_sum(value, before[channel, row, :], after[channel, row, :])
            twice[part, x + 1] = total + total
            mixed[part, x + 1] = total + (value + value)
        return carry

    lax.fori_loop(0, size_x, along, 0)

    def across(x, carry):
        own = []
        for part in range(2):
            level = mixed[part, x] + mixed[part, x + 2] + twice[part, x + 1]
            nearby = z_sum(level) + (twice[part, x] + twice[part, x + 2])
            own.append(nearby)
        real, imag = volume[0, 0, x], volume[1, 0, x]
        diagonal, twelfth, absorb = scales[0, x], scales[1, x], scales[2, x]
        real_out = (diagonal * real - twelfth * own[0]) + absorb * imag
        imag_out = (diagonal * imag - twelfth * own[1]) - absorb * real
        out[0, 0, x] = real_out
        out[1, 0, x] = imag_out
        tops[0, step, x] = real_out[:, low:]
        tops[1, step, x] = imag_out[:, low:]
        return carry

    lax.fori_loop(0, size_x, across, 0)
    for part in range(2):
        planes[0, part, step] = out[part, 0, 0]
        planes[1, part, step] = out[part, 0, size_x - 1]


def interior(volume, coefficients, before, after, first, count, previous=None):
    parts, _, size_x, size_y, size_z = volume.shape
    whole = pl.BlockSpec((parts, 1, size_x, size_y, size_z), lambda i: (0, first + i, 0, 0, 0))
    fixed = pl.BlockSpec(coefficients.shape, lambda i: (0, 0, 0, 0))
    specs = [whole, fixed, VMEM, VMEM]
    operands = [afar(volume), coefficients, near(before), near(after)]
    aliases = {}
    if previous is not None:
        specs.append(ANY)
        operands.append(previous)
        aliases = {4: 0}
    work = pltpu.VMEM((parts, size_x + 2, size_y, size_z), F32)
    return pl.pallas_call(
        partial(interior_kernel, first=first),
        grid=(count,),
        in_specs=specs,
        out_specs=[whole, VMEM, VMEM],
        out_shape=[
            jax.ShapeDtypeStruct(volume.shape, F32),
            pltpu.VMEM((2, parts, count, size_y, size_z), F32),
            pltpu.VMEM((parts, count, size_x, size_y, 128), F32),
        ],
        scratch_shapes=[pltpu.VMEM((3, size_x, size_y, size_z), F32), work, work],
        input_output_aliases=aliases,
        compiler_params=LIMIT,
        name="interior",
    )(*operands)


def final_kernel(coefficients, same_plane, same_corner, cross_plane, small, counted, *refs):
    edges = refs[: 2 * CALLS]
    out, boundary, planes, tops, scales, sems, scale_sems = refs[2 * CALLS + 1 :]
    narrow = lax.axis_index("narrow")
    channels, size_x, size_y, size_z = out.shape
    places = sides_of(size_x)
    last = size_x - 1
    low = size_z - 128
    waves = channels // 2
    scale_copies = [
        pltpu.make_async_copy(coefficients.at[0, places[side]], scales.at[side], scale_sems.at[side])
        for side in range(2)
    ]
    for copy in scale_copies:
        copy.start()

    mine = pltpu.roll(small[0] - 0.25 * small[4], (128 - narrow * 4) % 128, 1)
    mine = mine.T
    boundary[0] = mine[:4, :waves]
    boundary[1] = mine[:4, waves:]
    rows = jnp.concatenate([small[k] for k in range(4)], axis=1)
    added = jnp.zeros((counted.shape[0], channels), F32)
    for piece in reversed(split3(rows)):
        added = added + lax.dot_general(counted[...], piece, NT, preferred_element_type=F32)
    added = jnp.concatenate([added, jnp.zeros((added.shape[0], 128 - channels), F32)], axis=1)
    at_top = lax.broadcasted_iota(jnp.int32, added.shape, 1) == 127
    for copy in scale_copies:
        copy.wait()

    copies = []
    count = waves // CALLS
    even = places[1] == 0
    for channel in range(channels):
        part, wave = divmod(channel, waves)
        source, source_top = edges[2 * (wave // count)], edges[2 * (wave // count) + 1]
        wave = wave % count
        lifted = jnp.where(at_top, pltpu.roll(added, 127 - channel, 1), 0.0)
        lifted = lifted.reshape(size_x, size_y, 128)
        for side in range(2):
            scale = scales[side].astype(F32) * (1.0 / 12.0)
            if side == 0:
                value = same_plane[channel]
                ends = [same_corner[k, pl.ds(channel, 1), :] for k in range(2)]
                begun = source[jnp.where(even, 1, 0), part, wave]
                raised = jnp.where(even, lifted[last], lifted[0])
            else:
                value = cross_plane[channel]
                ends = [cross_plane[channels + k, pl.ds(channel, 1), :] for k in range(2)]
                begun = source[jnp.where(even, 0, 1), part, wave]
                raised = jnp.where(even, lifted[0], lifted[last])
            total = y_sum(value, *ends)
            total2 = total + total
            nearby = z_sum(total + (value + value)) + total2
            result = begun - scale * nearby
            planes[side, channel, :, pl.ds(0, low)] = result[:, :low]
            planes[side, channel, :, pl.ds(low, 128)] = result[:, low:] + raised
            copy = pltpu.make_async_copy(
                planes.at[side, channel], out.at[channel, places[side]], sems.at[side, channel]
            )
            copy.start()
            copies.append(copy)
        tops[channel] = source_top[part, wave, pl.ds(1, size_x - 2)] + lifted[1:last]
        copy = pltpu.make_async_copy(
            tops.at[channel],
            out.at[channel, pl.ds(1, size_x - 2), :, pl.ds(low, 128)],
            sems.at[2, channel],
        )
        copy.start()
        copies.append(copy)
    for copy in copies:
        copy.wait()


def final(coefficients, wide_faces, small, counted, edges, started):
    channels, size_x, size_y, size_z = started.shape
    close = [near(v) for v in wide_faces + (small, counted) + tuple(edges)]
    return pl.pallas_call(
        final_kernel,
        in_specs=[HBM] + [VMEM] * len(close) + [ANY],
        out_specs=[ANY, VMEM],
        out_shape=[
            jax.ShapeDtypeStruct(started.shape, F32),
            jax.ShapeDtypeStruct((2, 4, channels // 2), F32),
        ],
        scratch_shapes=[
            pltpu.VMEM((2, channels, size_y, size_z), F32),
            pltpu.VMEM((channels, size_x - 2, size_y, 128), F32),
            pltpu.VMEM((2, size_y, size_z), BF16),
            pltpu.SemaphoreType.DMA((3, channels)),
            pltpu.SemaphoreType.DMA((2,)),
        ],
        input_output_aliases={len(close) + 1: 0},
        compiler_params=LIMIT,
        name="final",
    )(afar(coefficients), *close, started)


N_WIDE = 8
N_NARROW = 16
AXES = ("wide", "narrow")


def moved(value, rule):
    pairs = []
    for wide in range(N_WIDE):
        for narrow in range(N_NARROW):
            target = rule(wide, narrow)
            if target is not None and 0 <= target[0] < N_WIDE and 0 <= target[1] < N_NARROW:
                pairs.append((wide * N_NARROW + narrow, target[0] * N_NARROW + target[1]))
    return lax.ppermute(value, AXES, pairs)


def along_y(step):
    return lambda w, n: (w ^ (step >> 1), n ^ ((step & 1) * 8))


def on_device(
    volume_field,
    coefficients,
    density,
    boundary_matrix,
    upsample,
    trace_cell,
    trace_row,
    slot_counts,
):
    parts, waves, size_x, size_y, size_z = volume_field.shape
    channels = parts * waves
    volume = volume_field.reshape(channels, size_x, size_y, size_z)

    upward, downward, same_out = faces(volume)
    before = moved(upward, lambda w, n: (w, n + 1))
    after = moved(downward, lambda w, n: (w, n - 1))
    same_plane = moved(same_out, lambda w, n: (w ^ 1, n))

    own, one, two, three, counted = front(
        upsample,
        slot_counts,
        volume,
        density.reshape(channels, density.shape[2]),
        boundary_matrix,
        trace_cell.reshape(1, -1),
        trace_row.reshape(1, -1),
    )
    got = [
        moved(message, lambda w, n, s=step: (w ^ (2 * s), n))
        for step, message in ((1, one), (2, two), (3, three))
    ]
    corner_out, cross_out = pack(volume, before, after)
    small = join(own, *got)

    count = waves // CALLS
    started, edges = None, []

    def some_waves(call, started):
        return interior(
            volume_field, coefficients, before, after, call * count, count, started
        )

    started, *more = some_waves(0, started)
    edges += more
    got = [moved(small, along_y(step)) for step in range(1, 4)]
    same_corner = moved(corner_out, lambda w, n: (w ^ 1, n))
    cross_plane = moved(cross_out, lambda w, n: (w + (1 if w % 2 else -1), n))
    small = spread(small, *got)
    for call, step in enumerate((2, 4, 1)):
        started, *more = some_waves(call + 1, started)
        edges += more
        small = small + moved(small, lambda w, n, s=step: (w, n ^ s))

    volume_out, boundary = final(
        coefficients,
        (same_plane, same_corner, cross_plane),
        small,
        counted,
        edges,
        started.reshape(volume.shape),
    )
    return volume_out.reshape(volume_field.shape), boundary.transpose(0, 2, 1)


def solution(mesh):
    return jax.shard_map(
        on_device,
        mesh=mesh,
        in_specs=(
            P(None, None, "wide", "narrow", None),
            P(None, "wide", "narrow", None),
            P(None, None, "narrow"),
            P(None, None, "wide", "narrow"),
            P("narrow"),
            P("wide", "narrow", None),
            P("wide", "narrow", None),
            P("wide", "narrow"),
        ),
        out_specs=(P(None, None, "wide", "narrow", None), P(None, None, ("wide", "narrow"))),
        check_vma=False,
    )
```

profile of v0, /device:TPU:1, one launch (start us, length us, event | category | flops | bytes accessed | tf_op | source)
XLA Modules:
  0.0 93.0 jit_solution(12019040476390860695)
XLA Ops:
  0.7 1.6 %faces.1 = (f32[16,16,512]{2,1,0:T(8,128)S(1)}, f32[16,16,512]{2,1,0:T(8,128)S(1)}, f32[16,16,512]{2,1,0:T(8,128)S(1)}) custom-call(f32[16,16,16,512]{3,2,1,0:T(8,128)} %bitcast.10), custom_call_target="tpu_custom_call" | custom-call | tf_op jit(solution)/shard_map/faces/pallas_call | solution.py:67
  2.3 5.1 %collective-permute-start.1 = (f32[16,16,512]{2,1,0:T(8,128)S(1)}, f32[16,16,512]{2,1,0:T(8,128)S(1)}, u32[]{:S(2)}, u32[]{:S(2)}) collective-permute-start(f32[16,16,512]{2,1,0:T(8,128)S(1)} %get-tuple-element.27), channel_id=1, source_target_pairs={{0,1},{1,2},{2,3},{3,4},{4,5},{5,6},{6,7},{7,8},{8,9},{9,10},{10,1... | collective-permute-start | bytes 1572872 | tf_op jit(solution)/shard_map/ppermute | solution.py:484
  7.3 1.9 %collective-permute-start.2 = (f32[16,16,512]{2,1,0:T(8,128)S(1)}, f32[16,16,512]{2,1,0:T(8,128)S(1)}, u32[]{:S(2)}, u32[]{:S(2)}) collective-permute-start(f32[16,16,512]{2,1,0:T(8,128)S(1)} %get-tuple-element.28), channel_id=1, source_target_pairs={{1,0},{2,1},{3,2},{4,3},{5,4},{6,5},{7,6},{8,7},{9,8},{10,9},{11,1... | collective-permute-start | bytes 1572872 | tf_op jit(solution)/shard_map/ppermute | solution.py:484
  9.3 4.2 %collective-permute-done.1.before = f32[16,16,512]{2,1,0:T(8,128)S(1)} collective-permute-done((f32[16,16,512]{2,1,0:T(8,128)S(1)}, f32[16,16,512]{2,1,0:T(8,128)S(1)}, u32[]{:S(2)}, u32[]{:S(2)}) %collective-permute-start.1) | collective-permute-done | bytes 524320 | tf_op jit(solution)/shard_map/ppermute | solution.py:484
  13.4 4.4 %collective-permute-done.2.after = f32[16,16,512]{2,1,0:T(8,128)S(1)} collective-permute-done((f32[16,16,512]{2,1,0:T(8,128)S(1)}, f32[16,16,512]{2,1,0:T(8,128)S(1)}, u32[]{:S(2)}, u32[]{:S(2)}) %collective-permute-start.2) | collective-permute-done | bytes 524320 | tf_op jit(solution)/shard_map/ppermute | solution.py:484
  17.8 1.1 %pack.1 = (f32[2,16,512]{2,1,0:T(8,128)S(1)}, f32[18,16,512]{2,1,0:T(8,128)S(1)}) custom-call(f32[16,16,16,512]{3,2,1,0:T(8,128)} %bitcast.11, f32[16,16,512]{2,1,0:T(8,128)S(1)} %collective-permute-done.1.before, f32[16,16,512]{2,1,0:T(8,128)S(1)} %collective-permute-done.2.after), custom_call_target="tpu_custom_call" | custom-call | tf_op jit(solution)/shard_map/pack/pallas_call | solution.py:100
  19.8 5.2 %collective-permute-start = (f32[16,16,512]{2,1,0:T(8,128)S(1)}, f32[16,16,512]{2,1,0:T(8,128)S(1)}, u32[]{:S(2)}, u32[]{:S(2)}) collective-permute-start(f32[16,16,512]{2,1,0:T(8,128)S(1)} %get-tuple-element.26), channel_id=1, source_target_pairs={{0,16},{1,17},{2,18},{3,19},{4,20},{5,21},{6,22},{7,23},{8,24},{9,... | collective-permute-start | bytes 1572872 | tf_op jit(solution)/shard_map/ppermute | solution.py:484
  25.7 3.9 %front.1 = (f32[2,16,128]{2,1,0:T(8,128)S(1)}, f32[2,16,128]{2,1,0:T(8,128)S(1)}, f32[2,16,128]{2,1,0:T(8,128)S(1)}, f32[2,16,128]{2,1,0:T(8,128)S(1)}, bf16[256,512]{1,0:T(8,128)(2,1)S(1)}) custom-call(s32[8]{0:T(128)S(1)} %copy-done.5, s32[1,1]{1,0:T(1,128)S(6)} %copy.18.counts, f32[16,16,16,512]{3,2,1,0:T(8,128)} %bitcast.12, f32[16,4096]{1,0:T(8,128)S(1)} %bitcast.7, ...), custom_call_target="tpu_custom_call" | custom-call | tf_op jit(solution)/shard_map/front/pallas_call | solution.py:195
  29.6 1.3 %collective-permute-start.5 = (f32[2,16,128]{2,1,0:T(8,128)S(1)}, f32[2,16,128]{2,1,0:T(8,128)S(1)}, u32[]{:S(2)}, u32[]{:S(2)}) collective-permute-start(f32[2,16,128]{2,1,0:T(8,128)S(1)} %get-tuple-element.32), channel_id=1, source_target_pairs={{0,32},{1,33},{2,34},{3,35},{4,36},{5,37},{6,38},{7,39},{8,40},{9,... | collective-permute-start | bytes 49160 | tf_op jit(solution)/shard_map/ppermute | solution.py:484
  30.9 1.7 %collective-permute-start.6 = (f32[2,16,128]{2,1,0:T(8,128)S(1)}, f32[2,16,128]{2,1,0:T(8,128)S(1)}, u32[]{:S(2)}, u32[]{:S(2)}) collective-permute-start(f32[2,16,128]{2,1,0:T(8,128)S(1)} %get-tuple-element.33), channel_id=1, source_target_pairs={{0,64},{1,65},{2,66},{3,67},{4,68},{5,69},{6,70},{7,71},{8,72},{9,... | collective-permute-start | bytes 49160 | tf_op jit(solution)/shard_map/ppermute | solution.py:484
  33.5 1.4 %collective-permute-done.6.two = f32[2,16,128]{2,1,0:T(8,128)S(1)} collective-permute-done((f32[2,16,128]{2,1,0:T(8,128)S(1)}, f32[2,16,128]{2,1,0:T(8,128)S(1)}, u32[]{:S(2)}, u32[]{:S(2)}) %collective-permute-start.6) | collective-permute-done | bytes 16416 | tf_op jit(solution)/shard_map/ppermute | solution.py:484
  35.0 1.4 %collective-permute-done.7.three = f32[2,16,128]{2,1,0:T(8,128)S(1)} collective-permute-done((f32[2,16,128]{2,1,0:T(8,128)S(1)}, f32[2,16,128]{2,1,0:T(8,128)S(1)}, u32[]{:S(2)}, u32[]{:S(2)}) %collective-permute-start.7) | collective-permute-done | bytes 16416 | tf_op jit(solution)/shard_map/ppermute | solution.py:484
  36.5 5.4 %collective-permute-start.10 = (f32[3,16,128]{2,1,0:T(8,128)S(1)}, f32[3,16,128]{2,1,0:T(8,128)S(1)}, u32[]{:S(2)}, u32[]{:S(2)}) collective-permute-start(f32[3,16,128]{2,1,0:T(8,128)S(1)} %join.1.own), channel_id=1, source_target_pairs={{0,24},{1,25},{2,26},{3,27},{4,28},{5,29},{6,30},{7,31},{8,16},{9,... | collective-permute-start | bytes 73736 | tf_op jit(solution)/shard_map/ppermute | solution.py:484
  41.9 1.3 %collective-permute-start.9 = (f32[3,16,128]{2,1,0:T(8,128)S(1)}, f32[3,16,128]{2,1,0:T(8,128)S(1)}, u32[]{:S(2)}, u32[]{:S(2)}) collective-permute-start(f32[3,16,128]{2,1,0:T(8,128)S(1)} %join.1.own), channel_id=1, source_target_pairs={{0,16},{1,17},{2,18},{3,19},{4,20},{5,21},{6,22},{7,23},{8,24},{9,... | collective-permute-start | bytes 73736 | tf_op jit(solution)/shard_map/ppermute | solution.py:484
  43.5 7.3 %collective-permute-done.8.one = f32[3,16,128]{2,1,0:T(8,128)S(1)} collective-permute-done((f32[3,16,128]{2,1,0:T(8,128)S(1)}, f32[3,16,128]{2,1,0:T(8,128)S(1)}, u32[]{:S(2)}, u32[]{:S(2)}) %collective-permute-start.8) | collective-permute-done | bytes 24608 | tf_op jit(solution)/shard_map/ppermute | solution.py:484
  51.4 2.4 %collective-permute-done.11 = f32[5,16,128]{2,1,0:T(8,128)S(1)} collective-permute-done((f32[5,16,128]{2,1,0:T(8,128)S(1)}, f32[5,16,128]{2,1,0:T(8,128)S(1)}, u32[]{:S(2)}, u32[]{:S(2)}) %collective-permute-start.11) | collective-permute-done | bytes 40992 | tf_op jit(solution)/shard_map/ppermute | solution.py:484
  53.8 2.4 %collective-permute-start.12 = (f32[5,16,128]{2,1,0:T(8,128)S(1)}, f32[5,16,128]{2,1,0:T(8,128)S(1)}, u32[]{:S(2)}, u32[]{:S(2)}) collective-permute-start(f32[5,16,128]{2,1,0:T(8,128)S(1)} %add.9), channel_id=1, source_target_pairs={{0,4},{1,5},{2,6},{3,7},{4,0},{5,1},{6,2},{7,3},{8,12},{9,13},{10,... | collective-permute-start | bytes 122888 | tf_op jit(solution)/shard_map/ppermute | solution.py:484
  56.2 3.1 %collective-permute-start.3 = (f32[2,16,512]{2,1,0:T(8,128)S(1)}, f32[2,16,512]{2,1,0:T(8,128)S(1)}, u32[]{:S(2)}, u32[]{:S(2)}) collective-permute-start(f32[2,16,512]{2,1,0:T(8,128)S(1)} %get-tuple-element.29), channel_id=1, source_target_pairs={{0,16},{1,17},{2,18},{3,19},{4,20},{5,21},{6,22},{7,23},{8,24},{9,... | collective-permute-start | bytes 196616 | tf_op jit(solution)/shard_map/ppermute | solution.py:484
  59.3 2.2 %collective-permute-start.13 = (f32[5,16,128]{2,1,0:T(8,128)S(1)}, f32[5,16,128]{2,1,0:T(8,128)S(1)}, u32[]{:S(2)}, u32[]{:S(2)}) collective-permute-start(f32[5,16,128]{2,1,0:T(8,128)S(1)} %add.10), channel_id=1, source_target_pairs={{0,1},{1,0},{2,3},{3,2},{4,5},{5,4},{6,7},{7,6},{8,9},{9,8},{10,11... | collective-permute-start | bytes 122888 | tf_op jit(solution)/shard_map/ppermute | solution.py:484
  62.4 6.7 %interior.4 = (f32[2,8,16,16,512]{4,3,2,1,0:T(8,128)}, f32[2,2,2,16,512]{4,3,2,1,0:T(8,128)S(1)}, f32[2,2,16,16,128]{4,3,2,1,0:T(8,128)S(1)}) custom-call(f32[2,8,16,16,512]{4,3,2,1,0:T(8,128)} %volume.7, bf16[3,16,16,512]{3,2,1,0:T(8,128)(2,1)S(1)} %copy-done, f32[16,16,512]{2,1,0:T(8,128)S(1)} %collective-permute-done.1.before, ...), custom_call_target="tpu_custom_call" | custom-call | tf_op jit(solution)/shard_map/interior/pallas_call | solution.py:358
  69.1 6.7 %interior.5 = (f32[2,8,16,16,512]{4,3,2,1,0:T(8,128)}, f32[2,2,2,16,512]{4,3,2,1,0:T(8,128)S(1)}, f32[2,2,16,16,128]{4,3,2,1,0:T(8,128)S(1)}) custom-call(f32[2,8,16,16,512]{4,3,2,1,0:T(8,128)} %volume.7, bf16[3,16,16,512]{3,2,1,0:T(8,128)(2,1)S(1)} %copy-done, f32[16,16,512]{2,1,0:T(8,128)S(1)} %collective-permute-done.1.before, ...), custom_call_target="tpu_custom_call", output_to_operand_aliasing={{0}: (4, {})} | custom-call | tf_op jit(solution)/shard_map/interior/pallas_call | solution.py:358
  75.8 6.7 %interior.6 = (f32[2,8,16,16,512]{4,3,2,1,0:T(8,128)}, f32[2,2,2,16,512]{4,3,2,1,0:T(8,128)S(1)}, f32[2,2,16,16,128]{4,3,2,1,0:T(8,128)S(1)}) custom-call(f32[2,8,16,16,512]{4,3,2,1,0:T(8,128)} %volume.7, bf16[3,16,16,512]{3,2,1,0:T(8,128)(2,1)S(1)} %copy-done, f32[16,16,512]{2,1,0:T(8,128)S(1)} %collective-permute-done.1.before, ...), custom_call_target="tpu_custom_call", output_to_operand_aliasing={{0}: (4, {})} | custom-call | tf_op jit(solution)/shard_map/interior/pallas_call | solution.py:358
  82.6 6.7 %interior.7 = (f32[2,8,16,16,512]{4,3,2,1,0:T(8,128)}, f32[2,2,2,16,512]{4,3,2,1,0:T(8,128)S(1)}, f32[2,2,16,16,128]{4,3,2,1,0:T(8,128)S(1)}) custom-call(f32[2,8,16,16,512]{4,3,2,1,0:T(8,128)} %volume.7, bf16[3,16,16,512]{3,2,1,0:T(8,128)(2,1)S(1)} %copy-done, f32[16,16,512]{2,1,0:T(8,128)S(1)} %collective-permute-done.1.before, ...), custom_call_target="tpu_custom_call", output_to_operand_aliasing={{0}: (4, {})} | custom-call | tf_op jit(solution)/shard_map/interior/pallas_call | solution.py:358
  89.3 3.7 %final.1 = (f32[16,16,16,512]{3,2,1,0:T(8,128)}, f32[2,4,8]{2,1,0:T(4,128)}) custom-call(bf16[3,16,16,512]{3,2,1,0:T(8,128)(2,1)} %coefficients.9, f32[16,16,512]{2,1,0:T(8,128)S(1)} %collective-permute-done.same_plane, f32[2,16,512]{2,1,0:T(8,128)S(1)} %collective-permute-done.3.same_corner, ...), custom_call_target="tpu_custom_call", output_to_operand_aliasing={{0}: (14, {})} | custom-call | tf_op jit(solution)/shard_map/final/pallas_call | solution.py:451
  (29 shorter events, 3.7 us)
Async XLA Ops:
  0.6 25.0 %copy-start.1 = (bf16[2,4,64,4096]{3,2,1,0:T(8,128)(2,1)S(1)}, bf16[2,4,64,4096]{3,2,1,0:T(8,128)(2,1)}, u32[]{:S(2)}) copy-start(bf16[2,4,64,4096]{3,2,1,0:T(8,128)(2,1)} %matrix.1) | copy-start | bytes 12582916
  0.6 25.0 %copy-start.2 = (f32[2,8,4096]{2,1,0:T(8,128)S(1)}, f32[2,8,4096]{2,1,0:T(8,128)}, u32[]{:S(2)}) copy-start(f32[2,8,4096]{2,1,0:T(8,128)} %param.10) | copy-start | bytes 786436
  0.7 25.0 %copy-start.3 = (s32[1,1,256]{2,1,0:T(1,128)S(1)}, s32[1,1,256]{2,1,0:T(1,128)}, u32[]{:S(2)}) copy-start(s32[1,1,256]{2,1,0:T(1,128)} %param.13) | copy-start | bytes 3076
  0.7 25.0 %copy-start.4 = (s32[1,1,256]{2,1,0:T(1,128)S(1)}, s32[1,1,256]{2,1,0:T(1,128)}, u32[]{:S(2)}) copy-start(s32[1,1,256]{2,1,0:T(1,128)} %param.14) | copy-start | bytes 3076
  0.7 25.0 %copy-start.5 = (s32[8]{0:T(128)S(1)}, s32[8]{0:T(128)}, u32[]{:S(2)}) copy-start(s32[8]{0:T(128)} %upsample.1) | copy-start | bytes 100
  2.3 11.2 %collective-permute-start.1 = (f32[16,16,512]{2,1,0:T(8,128)S(1)}, f32[16,16,512]{2,1,0:T(8,128)S(1)}, u32[]{:S(2)}, u32[]{:S(2)}) collective-permute-start(f32[16,16,512]{2,1,0:T(8,128)S(1)} %get-tuple-element.27), channel_id=1, source_target_pairs={{0,1},{1,2},{2,3},{3,4},{4,5},{5,6},{6,7},{7,8},{8,9},{9,10},{10,1... | collective-permute-start | bytes 1572872 | tf_op jit(solution)/shard_map/ppermute | solution.py:484
  7.3 10.5 %collective-permute-start.2 = (f32[16,16,512]{2,1,0:T(8,128)S(1)}, f32[16,16,512]{2,1,0:T(8,128)S(1)}, u32[]{:S(2)}, u32[]{:S(2)}) collective-permute-start(f32[16,16,512]{2,1,0:T(8,128)S(1)} %get-tuple-element.28), channel_id=1, source_target_pairs={{1,0},{2,1},{3,2},{4,3},{5,4},{6,5},{7,6},{8,7},{9,8},{10,9},{11,1... | collective-permute-start | bytes 1572872 | tf_op jit(solution)/shard_map/ppermute | solution.py:484
  18.9 43.5 %copy-start = (bf16[3,16,16,512]{3,2,1,0:T(8,128)(2,1)S(1)}, bf16[3,16,16,512]{3,2,1,0:T(8,128)(2,1)}, u32[]{:S(2)}) copy-start(bf16[3,16,16,512]{3,2,1,0:T(8,128)(2,1)} %coefficients.9) | copy-start | bytes 2359300
  18.9 70.3 %collective-permute-start.4 = (f32[18,16,512]{2,1,0:T(8,128)S(1)}, f32[18,16,512]{2,1,0:T(8,128)S(1)}, u32[]{:S(2)}, u32[]{:S(2)}) collective-permute-start(f32[18,16,512]{2,1,0:T(8,128)S(1)} %get-tuple-element.30), channel_id=1, source_target_pairs={{16,32},{17,33},{18,34},{19,35},{20,36},{21,37},{22,38},{23,39},{2... | collective-permute-start | bytes 1769480 | tf_op jit(solution)/shard_map/ppermute | solution.py:484
  19.8 69.5 %collective-permute-start = (f32[16,16,512]{2,1,0:T(8,128)S(1)}, f32[16,16,512]{2,1,0:T(8,128)S(1)}, u32[]{:S(2)}, u32[]{:S(2)}) collective-permute-start(f32[16,16,512]{2,1,0:T(8,128)S(1)} %get-tuple-element.26), channel_id=1, source_target_pairs={{0,16},{1,17},{2,18},{3,19},{4,20},{5,21},{6,22},{7,23},{8,24},{9,... | collective-permute-start | bytes 1572872 | tf_op jit(solution)/shard_map/ppermute | solution.py:484
  29.6 3.9 %collective-permute-start.5 = (f32[2,16,128]{2,1,0:T(8,128)S(1)}, f32[2,16,128]{2,1,0:T(8,128)S(1)}, u32[]{:S(2)}, u32[]{:S(2)}) collective-permute-start(f32[2,16,128]{2,1,0:T(8,128)S(1)} %get-tuple-element.32), channel_id=1, source_target_pairs={{0,32},{1,33},{2,34},{3,35},{4,36},{5,37},{6,38},{7,39},{8,40},{9,... | collective-permute-start | bytes 49160 | tf_op jit(solution)/shard_map/ppermute | solution.py:484
  30.9 4.1 %collective-permute-start.6 = (f32[2,16,128]{2,1,0:T(8,128)S(1)}, f32[2,16,128]{2,1,0:T(8,128)S(1)}, u32[]{:S(2)}, u32[]{:S(2)}) collective-permute-start(f32[2,16,128]{2,1,0:T(8,128)S(1)} %get-tuple-element.33), channel_id=1, source_target_pairs={{0,64},{1,65},{2,66},{3,67},{4,68},{5,69},{6,70},{7,71},{8,72},{9,... | collective-permute-start | bytes 49160 | tf_op jit(solution)/shard_map/ppermute | solution.py:484
  32.6 3.8 %collective-permute-start.7 = (f32[2,16,128]{2,1,0:T(8,128)S(1)}, f32[2,16,128]{2,1,0:T(8,128)S(1)}, u32[]{:S(2)}, u32[]{:S(2)}) collective-permute-start(f32[2,16,128]{2,1,0:T(8,128)S(1)} %get-tuple-element.34), channel_id=1, source_target_pairs={{0,96},{1,97},{2,98},{3,99},{4,100},{5,101},{6,102},{7,103},{8,104... | collective-permute-start | bytes 49160 | tf_op jit(solution)/shard_map/ppermute | solution.py:484
  36.5 7.0 %collective-permute-start.10 = (f32[3,16,128]{2,1,0:T(8,128)S(1)}, f32[3,16,128]{2,1,0:T(8,128)S(1)}, u32[]{:S(2)}, u32[]{:S(2)}) collective-permute-start(f32[3,16,128]{2,1,0:T(8,128)S(1)} %join.1.own), channel_id=1, source_target_pairs={{0,24},{1,25},{2,26},{3,27},{4,28},{5,29},{6,30},{7,31},{8,16},{9,... | collective-permute-start | bytes 73736 | tf_op jit(solution)/shard_map/ppermute | solution.py:484
  41.9 8.9 %collective-permute-start.8 = (f32[3,16,128]{2,1,0:T(8,128)S(1)}, f32[3,16,128]{2,1,0:T(8,128)S(1)}, u32[]{:S(2)}, u32[]{:S(2)}) collective-permute-start(f32[3,16,128]{2,1,0:T(8,128)S(1)} %join.1.own), channel_id=1, source_target_pairs={{0,8},{1,9},{2,10},{3,11},{4,12},{5,13},{6,14},{7,15},{8,0},{9,1},... | collective-permute-start | bytes 73736 | tf_op jit(solution)/shard_map/ppermute | solution.py:484
  41.9 8.9 %collective-permute-start.9 = (f32[3,16,128]{2,1,0:T(8,128)S(1)}, f32[3,16,128]{2,1,0:T(8,128)S(1)}, u32[]{:S(2)}, u32[]{:S(2)}) collective-permute-start(f32[3,16,128]{2,1,0:T(8,128)S(1)} %join.1.own), channel_id=1, source_target_pairs={{0,16},{1,17},{2,18},{3,19},{4,20},{5,21},{6,22},{7,23},{8,24},{9,... | collective-permute-start | bytes 73736 | tf_op jit(solution)/shard_map/ppermute | solution.py:484
  50.9 2.9 %collective-permute-start.11 = (f32[5,16,128]{2,1,0:T(8,128)S(1)}, f32[5,16,128]{2,1,0:T(8,128)S(1)}, u32[]{:S(2)}, u32[]{:S(2)}) collective-permute-start(f32[5,16,128]{2,1,0:T(8,128)S(1)} %spread.1), channel_id=1, source_target_pairs={{0,2},{1,3},{2,0},{3,1},{4,6},{5,7},{6,4},{7,5},{8,10},{9,11},{10,... | collective-permute-start | bytes 122888 | tf_op jit(solution)/shard_map/ppermute | solution.py:484
  53.8 5.5 %collective-permute-start.12 = (f32[5,16,128]{2,1,0:T(8,128)S(1)}, f32[5,16,128]{2,1,0:T(8,128)S(1)}, u32[]{:S(2)}, u32[]{:S(2)}) collective-permute-start(f32[5,16,128]{2,1,0:T(8,128)S(1)} %add.9), channel_id=1, source_target_pairs={{0,4},{1,5},{2,6},{3,7},{4,0},{5,1},{6,2},{7,3},{8,12},{9,13},{10,... | collective-permute-start | bytes 122888 | tf_op jit(solution)/shard_map/ppermute | solution.py:484
  56.2 33.1 %collective-permute-start.3 = (f32[2,16,512]{2,1,0:T(8,128)S(1)}, f32[2,16,512]{2,1,0:T(8,128)S(1)}, u32[]{:S(2)}, u32[]{:S(2)}) collective-permute-start(f32[2,16,512]{2,1,0:T(8,128)S(1)} %get-tuple-element.29), channel_id=1, source_target_pairs={{0,16},{1,17},{2,18},{3,19},{4,20},{5,21},{6,22},{7,23},{8,24},{9,... | collective-permute-start | bytes 196616 | tf_op jit(solution)/shard_map/ppermute | solution.py:484
  59.3 3.1 %collective-permute-start.13 = (f32[5,16,128]{2,1,0:T(8,128)S(1)}, f32[5,16,128]{2,1,0:T(8,128)S(1)}, u32[]{:S(2)}, u32[]{:S(2)}) collective-permute-start(f32[5,16,128]{2,1,0:T(8,128)S(1)} %add.10), channel_id=1, source_target_pairs={{0,1},{1,0},{2,3},{3,2},{4,5},{5,4},{6,7},{7,6},{8,9},{9,8},{10,11... | collective-permute-start | bytes 122888 | tf_op jit(solution)/shard_map/ppermute | solution.py:484
where the time goes:
time: 93.3 us; the launch traced here: 93 us
  Pallas kernels  37.3 us (40%)
  starting transfers between devices  31.8 us (34%)
  waiting for transfers between devices  22.4 us (24%)
  between operations  1.45 us (2%)
    ppermute x14, starting transfers between devices, moved(): return lax.ppermute(value, AXES, pairs)  31.8 us
    pallas_call x4, Pallas kernels, interior(): pl.pallas_call(partial(interior_kernel, first=first), grid=(count,), in_s...  26.9 us
    ppermute x14, waiting for transfers between devices, moved(): return lax.ppermute(value, AXES, pairs)  22.4 us
    pallas_call x1, Pallas kernels, front(): pl.pallas_call(front_kernel, grid=(blocks // BLOCKS_A_STEP,), in_specs=[S...  3.9 us
    pallas_call x1, Pallas kernels, final(): pl.pallas_call(final_kernel, in_specs=[HBM] + [VMEM] * len(close) + [ANY]...  3.7 us
  transfers between devices with their start and end apart: 14, of which 8 were waited for; matrix products, arithmetic and copies ran while one was open for 0% of the time, Pallas kernels for 33%

commit v1 on v0

v1 whole, which is shorter than its diff:
```python
from functools import partial

import jax
import jax.numpy as jnp
from jax import lax
from jax.experimental import pallas as pl
from jax.experimental.pallas import tpu as pltpu
from jax.sharding import PartitionSpec as P


UMAX = 4
CALLS = 4
F32 = jnp.float32
BF16 = jnp.bfloat16
NT = (((1,), (1,)), ((), ()))
TN = (((0,), (0,)), ((), ()))


def split3(value):
    high = value.astype(BF16)
    rest = value - high.astype(F32)
    middle = rest.astype(BF16)
    low = (rest - middle.astype(F32)).astype(BF16)
    return high, middle, low


VMEM = pl.BlockSpec(memory_space=pltpu.VMEM)
ANY = pl.BlockSpec(memory_space=pl.ANY)
HBM = pl.BlockSpec(memory_space=pltpu.HBM)
LIMIT = pltpu.CompilerParams(vmem_limit_bytes=30 << 20)
SMEM = pl.BlockSpec(memory_space=pltpu.SMEM)


def near(value):
    return pltpu.with_memory_space_constraint(value, pltpu.VMEM)


def afar(value):
    return pltpu.with_memory_space_constraint(value, pltpu.HBM)


def sides_of(size_x):
    even = lax.axis_index("wide") % 2 == 0
    return jnp.where(even, size_x - 1, 0), jnp.where(even, 0, size_x - 1)


def run_all(copies):
    for copy in copies:
        copy.start()
    for copy in copies:
        copy.wait()


def faces_kernel(volume, upward, downward, same, cross, sems):
    channels, size_x, size_y, _ = volume.shape
    same_x, cross_x = sides_of(size_x)
    run_all(
        [
            pltpu.make_async_copy(volume.at[:, :, size_y - 1], upward, sems.at[0]),
            pltpu.make_async_copy(volume.at[:, :, 0], downward, sems.at[1]),
            pltpu.make_async_copy(volume.at[:, same_x], same, sems.at[2]),
            pltpu.make_async_copy(volume.at[:, cross_x], cross.at[pl.ds(0, channels)], sems.at[3]),
        ]
    )


def faces(volume):
    channels, size_x, size_y, size_z = volume.shape
    return pl.pallas_call(
        faces_kernel,
        in_specs=[HBM],
        out_specs=[VMEM] * 4,
        out_shape=[
            pltpu.VMEM((channels, size_x, size_z), F32),
            pltpu.VMEM((channels, size_x, size_z), F32),
            pltpu.VMEM((channels, size_y, size_z), F32),
            pltpu.VMEM((channels + 2, size_y, size_z), F32),
        ],
        scratch_shapes=[pltpu.SemaphoreType.DMA((4,))],
        compiler_params=LIMIT,
        name="faces",
    )(afar(volume))


def front_kernel(
    upsample, counts, volume, cells, rows, density_far, matrix_far,
    own, one, two, three, count_out, density, matrix, sems,
):
    wide = lax.axis_index("wide")
    density_copy = pltpu.make_async_copy(density_far, density, sems.at[UMAX])
    density_copy.start()
    level_copies = [
        pltpu.make_async_copy(matrix_far.at[:, level], matrix.at[level], sems.at[level])
        for level in range(UMAX)
    ]
    for copy in level_copies:
        copy.start()
    channels, _, _, size_z = volume.shape
    slots = cells.shape[1]
    cell_count, row_count = count_out.shape
    live = lax.broadcasted_iota(jnp.int32, (1, slots), 1) < counts[0, 0]
    cell_of = jnp.where(live, cells[...], -1)
    cell_hit = lax.broadcasted_iota(jnp.int32, (cell_count, slots), 0) == cell_of
    row_of = rows[...] ^ (wide * (row_count // 8))
    row_hit = lax.broadcasted_iota(jnp.int32, (row_count, slots), 0) == row_of
    cell_hit = jnp.where(cell_hit, 1.0, 0.0).astype(BF16)
    row_hit = jnp.where(row_hit, 1.0, 0.0).astype(BF16)
    counted = lax.dot_general(cell_hit, row_hit, NT, preferred_element_type=F32).astype(BF16)
    count_out[...] = counted

    at = lax.broadcasted_iota(jnp.int32, (cell_count, 128), 1)
    tops = jnp.zeros((cell_count, 128), F32)
    for channel in range(channels):
        value = volume[channel, :, :, pl.ds(size_z - 128, 128)].reshape(cell_count, 128)
        tops = jnp.where(at == channel, pltpu.roll(value, (channel + 1) % 128, 1), tops)
    traces = jnp.zeros((128, row_count), F32)
    for piece in reversed(split3(tops)):
        traces = traces + lax.dot_general(piece, counted, TN, preferred_element_type=F32)
    blocks = upsample.shape[0]
    width = density.shape[1] // blocks
    group = matrix.shape[2]
    lane = lax.broadcasted_iota(jnp.int32, (channels, width), 1)
    total = jnp.zeros((channels, 2 * group), F32)
    density_copy.wait()
    pairs = []
    for block in range(blocks):
        here = density[:, pl.ds(block * width, width)]
        factor = upsample[block]
        inverse = jnp.where(
            factor == 1, 1.0, jnp.where(factor == 2, 0.5, jnp.where(factor == 3, 1.0 / 3.0, 0.25))
        )
        pairs.append((here, factor, inverse))
    for level in range(UMAX):
        level_copies[level].wait()
        for block, (here, factor, inverse) in enumerate(pairs):
            following = jnp.where(lane == width - 1, here, pltpu.roll(here, width - 1, 1))
            share = jnp.where(level < factor, inverse, 0.0)
            blend = level * inverse
            fine = ((1.0 - blend) * share) * here + (blend * share) * following
            both = matrix[level, :, :, pl.ds(block * width, width)].reshape(2 * group, width)
            total = total + lax.dot_general(
                fine.astype(BF16), both, NT, preferred_element_type=F32
            )

    waves = channels // 2
    turned = pltpu.roll(total, group, 1)
    bem = jnp.concatenate(
        [total[:waves] - turned[waves:], total[waves:] + turned[:waves]], axis=0
    )
    for part, target in enumerate((own, one, two, three)):
        target[0] = bem
        target[1] = traces[:channels, part * 128 : (part + 1) * 128]


def front(upsample, counts, volume, density, matrix, cells, rows):
    channels = density.shape[0]
    message = pltpu.VMEM((2, channels, 128), F32)
    return pl.pallas_call(
        front_kernel,
        in_specs=[SMEM, SMEM] + [VMEM] * 3 + [HBM] * 2,
        out_specs=[VMEM] * 5,
        out_shape=[message] * 4 + [pltpu.VMEM((256, 512), BF16)],
        scratch_shapes=[
            pltpu.VMEM(density.shape, F32),
            pltpu.VMEM((UMAX, 2) + matrix.shape[2:], BF16),
            pltpu.SemaphoreType.DMA((UMAX + 1,)),
        ],
        compiler_params=LIMIT,
        name="front",
    )(upsample, counts, near(volume), near(cells), near(rows), afar(density), afar(matrix))


def join_kernel(own, one, two, three, before, after, cross_in, out, corner, cross, sems):
    group = 64
    channels, size_x, size_z = before.shape
    same_x, cross_x = sides_of(size_x)
    copies = [
        pltpu.make_async_copy(face.at[:, cross_x], cross.at[channels + k], sems.at[k])
        for k, face in enumerate((before, after))
    ]
    for copy in copies:
        copy.start()
    lane = lax.broadcasted_iota(jnp.int32, own.shape[1:], 1)
    sums = (
        jnp.where(lane < group, own[0], pltpu.roll(one[0], group, 1)),
        jnp.where(lane < group, two[0], pltpu.roll(three[0], group, 1)),
        (own[1] + one[1]) + (two[1] + three[1]),
    )
    for k in range(3):
        out[k] = sums[k]
        corner[k] = sums[k]
    for channel in range(channels):
        for k, face in enumerate((before, after)):
            row = face[channel, pl.ds(same_x, 1), :]
            for tile in range(size_z // 128):
                corner[3 + 4 * k + tile, pl.ds(channel, 1), :] = row[
                    :, 128 * tile : 128 * (tile + 1)
                ]
    for copy in copies:
        copy.wait()


def join(own, one, two, three, before, after, cross):
    channels = before.shape[0]
    operands = [near(v) for v in (own, one, two, three, before, after, cross)]
    return pl.pallas_call(
        join_kernel,
        in_specs=[VMEM] * 7,
        out_specs=[VMEM] * 3,
        out_shape=[
            pltpu.VMEM((3, channels, 128), F32),
            pltpu.VMEM((11, channels, 128), F32),
            pltpu.VMEM(cross.shape, F32),
        ],
        scratch_shapes=[pltpu.SemaphoreType.DMA((2,))],
        input_output_aliases={6: 2},
        compiler_params=LIMIT,
        name="join",
    )(*operands)


def spread_kernel(own, one, two, three, out):
    group = 64
    lane = lax.broadcasted_iota(jnp.int32, own.shape[1:], 1)
    for pair in range(2):
        close = own[pair] + one[pair]
        distant = two[pair] + three[pair]
        out[2 * pair] = jnp.where(lane < group, close, pltpu.roll(distant, group, 1))
        out[2 * pair + 1] = jnp.where(lane < group, pltpu.roll(close, group, 1), distant)
    out[4] = (own[2] + one[2]) + pltpu.roll(two[2] + three[2], group, 1)


def spread(own, one, two, three):
    return pl.pallas_call(
        spread_kernel,
        in_specs=[VMEM] * 4,
        out_specs=VMEM,
        out_shape=pltpu.VMEM((5,) + own.shape[1:], F32),
        compiler_params=LIMIT,
        name="spread",
    )(*[near(value) for value in (own, one, two, three)])


def y_sum(value, before, after):
    half = value.shape[0] // 2
    low, high = value[:half], value[half:]
    at = lax.broadcasted_iota(jnp.int32, low.shape, 0)
    low_down, high_down = pltpu.roll(low, 1, 0), pltpu.roll(high, 1, 0)
    low_up, high_up = pltpu.roll(low, half - 1, 0), pltpu.roll(high, half - 1, 0)
    first, final_row = at == 0, at == half - 1
    low_sum = jnp.where(first, before, low_down) + jnp.where(final_row, high_up, low_up)
    high_sum = jnp.where(first, low_down, high_down) + jnp.where(final_row, after, high_up)
    return jnp.concatenate([low_sum, high_sum], axis=0)


def z_sum(value):
    tiles = value.shape[1] // 128
    pieces = [value[:, 128 * k : 128 * (k + 1)] for k in range(tiles)]
    at = lax.broadcasted_iota(jnp.int32, pieces[0].shape, 1)
    first, final_lane = at == 0, at == 127
    down = [pltpu.roll(piece, 1, 1) for piece in pieces]
    up = [pltpu.roll(piece, 127, 1) for piece in pieces]
    sums = []
    for k in range(tiles):
        below = down[k - 1] if k > 0 else 0.0
        above = up[k + 1] if k < tiles - 1 else 0.0
        sums.append(jnp.where(first, below, down[k]) + jnp.where(final_lane, above, up[k]))
    return jnp.concatenate(sums, axis=1)


PLANES = 4


def interior_kernel(volume, given, before, after, *refs, first, prepares):
    if prepares:
        out, planes, tops, scales, buffers, sums, mixed, sems = refs
    else:
        _, out, planes, tops, buffers, sums, mixed, sems = refs
        scales = given
    parts, count, size_x, size_y, size_z = buffers.shape
    low = size_z - 128
    waves = volume.shape[1]

    if prepares:

        def prepare(x, carry):
            scale = given[0, x].astype(F32)
            scales[0, x] = scale * (8.0 / 3.0) - given[1, x].astype(F32)
            scales[1, x] = scale * (1.0 / 6.0)
            scales[2, x] = given[2, x].astype(F32)
            return carry

        lax.fori_loop(0, size_x, prepare, 0)
    nothing = jnp.zeros((size_y, size_z), F32)
    for part in range(parts):
        for x in (0, size_x + 1):
            sums[part, x] = nothing
            mixed[part, x] = nothing

    for step in range(count):
        wave = first + step

        def along(group, carry):
            for x in [group * PLANES + k for k in range(PLANES)]:
                for part in range(parts):
                    value = volume[part, wave, x]
                    channel = part * waves + wave
                    row = pl.ds(x, 1)
                    total = y_sum(value, before[channel, row, :], after[channel, row, :])
                    sums[part, x + 1] = total
                    mixed[part, x + 1] = 0.5 * total + value
            return carry

        def across(group, carry):
            for x in [group * PLANES + k for k in range(PLANES)]:
                own = []
                for part in range(parts):
                    level = (mixed[part, x] + mixed[part, x + 2]) + sums[part, x + 1]
                    own.append(z_sum(level) + (sums[part, x] + sums[part, x + 2]))
                real, imag = volume[0, wave, x], volume[1, wave, x]
                diagonal, sixth, absorb = scales[0, x], scales[1, x], scales[2, x]
                real_out = (diagonal * real - sixth * own[0]) + absorb * imag
                imag_out = (diagonal * imag - sixth * own[1]) - absorb * real
                for part, result in enumerate((real_out, imag_out)):
                    buffers[part, step, x] = result
                    tops[part, step, x] = result[:, low:]
            some = pl.ds(group * PLANES, PLANES)
            for part in range(parts):
                pltpu.make_async_copy(
                    buffers.at[part, step, some], out.at[part, wave, some], sems.at[part, step]
                ).start()
            return carry

        lax.fori_loop(0, size_x // PLANES, along, 0)
        lax.fori_loop(0, size_x // PLANES, across, 0)
        for part in range(parts):
            planes[0, part, step] = buffers[part, step, 0]
            planes[1, part, step] = buffers[part, step, size_x - 1]
    for step in range(count):
        for part in range(parts):
            pltpu.make_async_copy(
                buffers.at[part, step], out.at[part, first + step], sems.at[part, step]
            ).wait()


def interior(volume, given, before, after, first, count, previous=None):
    parts, _, size_x, size_y, size_z = volume.shape
    prepares = previous is None
    operands = [near(value) for value in (volume, given, before, after)]
    specs = [VMEM] * 4
    aliases = {}
    results = [
        jax.ShapeDtypeStruct(volume.shape, F32),
        pltpu.VMEM((2, parts, count, size_y, size_z), F32),
        pltpu.VMEM((parts, count, size_x, size_y, 128), F32),
    ]
    if prepares:
        results.append(pltpu.VMEM((3, size_x, size_y, size_z), F32))
    else:
        specs.append(ANY)
        operands.append(previous)
        aliases = {4: 0}
    work = pltpu.VMEM((parts, size_x + 2, size_y, size_z), F32)
    return pl.pallas_call(
        partial(interior_kernel, first=first, prepares=prepares),
        in_specs=specs,
        out_specs=[ANY] + [VMEM] * (len(results) - 1),
        out_shape=results,
        scratch_shapes=[
            pltpu.VMEM((parts, count, size_x, size_y, size_z), F32),
            work,
            work,
            pltpu.SemaphoreType.DMA((parts, count)),
        ],
        input_output_aliases=aliases,
        compiler_params=LIMIT,
        name="interior",
    )(*operands)


def final_kernel(scales, same_plane, same_corner, cross_plane, small, counted, *refs):
    edges = refs[: 2 * CALLS]
    out, boundary, planes, tops, sems = refs[2 * CALLS + 1 :]
    narrow = lax.axis_index("narrow")
    channels, size_x, size_y, size_z = out.shape
    places = sides_of(size_x)
    last = size_x - 1
    low = size_z - 128
    waves = channels // 2
    mine = pltpu.roll(small[0] - 0.25 * small[4], (128 - narrow * 4) % 128, 1)
    mine = mine.T
    boundary[0] = mine[:4, :waves]
    boundary[1] = mine[:4, waves:]
    rows = jnp.concatenate([small[k] for k in range(4)], axis=1)
    added = jnp.zeros((counted.shape[0], channels), F32)
    for piece in reversed(split3(rows)):
        added = added + lax.dot_general(counted[...], piece, NT, preferred_element_type=F32)
    added = jnp.concatenate([added, jnp.zeros((added.shape[0], 128 - channels), F32)], axis=1)
    at_top = lax.broadcasted_iota(jnp.int32, added.shape, 1) == 127
    copies = []
    count = waves // CALLS
    even = places[1] == 0
    for channel in range(channels):
        part, wave = divmod(channel, waves)
        source, source_top = edges[2 * (wave // count)], edges[2 * (wave // count) + 1]
        wave = wave % count
        lifted = jnp.where(at_top, pltpu.roll(added, 127 - channel, 1), 0.0)
        lifted = lifted.reshape(size_x, size_y, 128)
        for side in range(2):
            scale = 0.5 * scales[1, places[side]]
            if side == 0:
                value = same_plane[channel]
                ends = [
                    jnp.concatenate(
                        [
                            same_corner[3 + 4 * k + tile, pl.ds(channel, 1), :]
                            for tile in range(size_z // 128)
                        ],
                        axis=1,
                    )
                    for k in range(2)
                ]
                begun = source[jnp.where(even, 1, 0), part, wave]
                raised = jnp.where(even, lifted[last], lifted[0])
            else:
                value = cross_plane[channel]
                ends = [cross_plane[channels + k, pl.ds(channel, 1), :] for k in range(2)]
                begun = source[jnp.where(even, 0, 1), part, wave]
                raised = jnp.where(even, lifted[0], lifted[last])
            total = y_sum(value, *ends)
            total2 = total + total
            nearby = z_sum(total + (value + value)) + total2
            result = begun - scale * nearby
            planes[side, channel, :, pl.ds(0, low)] = result[:, :low]
            planes[side, channel, :, pl.ds(low, 128)] = result[:, low:] + raised
            copy = pltpu.make_async_copy(
                planes.at[side, channel], out.at[channel, places[side]], sems.at[side, channel]
            )
            copy.start()
            copies.append(copy)
        tops[channel] = source_top[part, wave, pl.ds(1, size_x - 2)] + lifted[1:last]
        copy = pltpu.make_async_copy(
            tops.at[channel],
            out.at[channel, pl.ds(1, size_x - 2), :, pl.ds(low, 128)],
            sems.at[2, channel],
        )
        copy.start()
        copies.append(copy)
    for copy in copies:
        copy.wait()


def final(scales, wide_faces, small, counted, edges, started):
    channels, size_x, size_y, size_z = started.shape
    close = [near(v) for v in (scales,) + wide_faces + (small, counted) + tuple(edges)]
    return pl.pallas_call(
        final_kernel,
        in_specs=[VMEM] * len(close) + [ANY],
        out_specs=[ANY, VMEM],
        out_shape=[
            jax.ShapeDtypeStruct(started.shape, F32),
            jax.ShapeDtypeStruct((2, 4, channels // 2), F32),
        ],
        scratch_shapes=[
            pltpu.VMEM((2, channels, size_y, size_z), F32),
            pltpu.VMEM((channels, size_x - 2, size_y, 128), F32),
            pltpu.SemaphoreType.DMA((3, channels)),
        ],
        input_output_aliases={len(close): 0},
        compiler_params=LIMIT,
        name="final",
    )(*close, started)


N_WIDE = 8
N_NARROW = 16
AXES = ("wide", "narrow")


def moved(value, rule):
    pairs = []
    for wide in range(N_WIDE):
        for narrow in range(N_NARROW):
            target = rule(wide, narrow)
            if target is not None and 0 <= target[0] < N_WIDE and 0 <= target[1] < N_NARROW:
                pairs.append((wide * N_NARROW + narrow, target[0] * N_NARROW + target[1]))
    return lax.ppermute(value, AXES, pairs)


def along_y(step):
    return lambda w, n: (w ^ (step >> 1), n ^ ((step & 1) * 8))


def on_device(
    volume_field,
    coefficients,
    density,
    boundary_matrix,
    upsample,
    trace_cell,
    trace_row,
    slot_counts,
):
    parts, waves, size_x, size_y, size_z = volume_field.shape
    channels = parts * waves
    volume = volume_field.reshape(channels, size_x, size_y, size_z)

    upward, downward, same_out, cross_out = faces(volume)
    before = moved(upward, lambda w, n: (w, n + 1))
    after = moved(downward, lambda w, n: (w, n - 1))
    same_plane = moved(same_out, lambda w, n: (w ^ 1, n))

    own, one, two, three, counted = front(
        upsample,
        slot_counts,
        volume,
        density.reshape(channels, density.shape[2]),
        boundary_matrix,
        trace_cell.reshape(1, -1),
        trace_row.reshape(1, -1),
    )
    got = [
        moved(message, lambda w, n, s=step: (w ^ (2 * s), n))
        for step, message in ((1, one), (2, two), (3, three))
    ]
    small, small_corner, cross_out = join(own, *got, before, after, cross_out)

    count = waves // CALLS
    edges = []
    started, *more, scales = interior(volume_field, coefficients, before, after, 0, count)
    edges += more

    def some_waves(call, started):
        return interior(volume_field, scales, before, after, call * count, count, started)

    got = [
        moved(message, along_y(step))
        for step, message in ((1, small), (2, small_corner), (3, small))
    ]
    same_corner = got[1]
    cross_plane = moved(cross_out, lambda w, n: (w + (1 if w % 2 else -1), n))
    small = spread(small, *got)
    for call, step in enumerate((2, 4, 1)):
        started, *more = some_waves(call + 1, started)
        edges += more
        small = small + moved(small, lambda w, n, s=step: (w, n ^ s))

    volume_out, boundary = final(
        scales,
        (same_plane, same_corner, cross_plane),
        small,
        counted,
        edges,
        started.reshape(volume.shape),
    )
    return volume_out.reshape(volume_field.shape), boundary.transpose(0, 2, 1)


def solution(mesh):
    return jax.shard_map(
        on_device,
        mesh=mesh,
        in_specs=(
            P(None, None, "wide", "narrow", None),
            P(None, "wide", "narrow", None),
            P(None, None, "narrow"),
            P(None, None, "wide", "narrow"),
            P("narrow"),
            P("wide", "narrow", None),
            P("wide", "narrow", None),
            P("wide", "narrow"),
        ),
        out_specs=(P(None, None, "wide", "narrow", None), P(None, None, ("wide", "narrow"))),
        check_vma=False,
    )
```

time: 93.3 us -> 81.5 us (0.87)
  Pallas kernels: 37.3 us -> 22.2 us
  waiting for transfers between devices: 22.4 us -> 30.1 us
  starting transfers between devices: 31.8 us -> 27.6 us
    pallas_call x9 -> x8, Pallas kernels: 37.2 us -> 22.1 us  [the longest x4 12.2 us: interior(): pl.pallas_call(partial(interior_kernel, first=first, prepares=prepares),...]
    ppermute x14 -> x13, waiting for transfers between devices: 22.4 us -> 30.1 us  [moved(): return lax.ppermute(value, AXES, pairs)]
    ppermute x14 -> x13, starting transfers between devices: 31.8 us -> 27.6 us  [moved(): return lax.ppermute(value, AXES, pairs)]
  transfers between devices with their start and end apart: 14 -> 13, of which waited for: 8 -> 5; matrix products, arithmetic and copies ran while one was open for 0% -> 0% of each run, Pallas kernels for 33% -> 21%
where the time goes in v1:
time: 81.5 us; the launch traced here: 81.3 us
  waiting for transfers between devices  30.1 us (37%)
  starting transfers between devices  27.6 us (34%)
  Pallas kernels  22.2 us (27%)
  between operations  1.48 us (2%)
    ppermute x13, waiting for transfers between devices, moved(): return lax.ppermute(value, AXES, pairs)  30.1 us
    ppermute x13, starting transfers between devices, moved(): return lax.ppermute(value, AXES, pairs)  27.6 us
    pallas_call x4, Pallas kernels, interior(): pl.pallas_call(partial(interior_kernel, first=first, prepares=prepares),...  12.2 us
    pallas_call x1, Pallas kernels, front(): pl.pallas_call(front_kernel, in_specs=[SMEM, SMEM] + [VMEM] * 3 + [HBM] *...  4.84 us
    pallas_call x1, Pallas kernels, final(): pl.pallas_call(final_kernel, in_specs=[VMEM] * len(close) + [ANY], out_sp...  3.17 us
    pallas_call x1, Pallas kernels, faces(): pl.pallas_call(faces_kernel, in_specs=[HBM], out_specs=[VMEM] * 4, out_sh...  1.74 us
  transfers between devices with their start and end apart: 13, of which 5 were waited for; matrix products, arithmetic and copies ran while one was open for 0% of the time, Pallas kernels for 21%

profile of v1, /device:TPU:1, one launch (start us, length us, event | category | flops | bytes accessed | tf_op | source)
XLA Modules:
  0.0 81.3 jit_solution(590706120380010633)
XLA Ops:
  0.7 1.7 %faces.1 = (f32[16,16,512]{2,1,0:T(8,128)S(1)}, f32[16,16,512]{2,1,0:T(8,128)S(1)}, f32[16,16,512]{2,1,0:T(8,128)S(1)}, f32[18,16,512]{2,1,0:T(8,128)S(1)}) custom-call(f32[16,16,16,512]{3,2,1,0:T(8,128)} %bitcast.7), custom_call_target="tpu_custom_call" | custom-call | tf_op jit(solution)/shard_map/faces/pallas_call | solution.py:69
  2.4 5.2 %collective-permute-start = (f32[16,16,512]{2,1,0:T(8,128)S(1)}, f32[16,16,512]{2,1,0:T(8,128)S(1)}, u32[]{:S(2)}, u32[]{:S(2)}) collective-permute-start(f32[16,16,512]{2,1,0:T(8,128)S(1)} %get-tuple-element.29), channel_id=1, source_target_pairs={{0,1},{1,2},{2,3},{3,4},{4,5},{5,6},{6,7},{7,8},{8,9},{9,10},{10,1... | collective-permute-start | bytes 1572872 | tf_op jit(solution)/shard_map/ppermute | solution.py:487
  7.6 1.9 %collective-permute-start.1 = (f32[16,16,512]{2,1,0:T(8,128)S(1)}, f32[16,16,512]{2,1,0:T(8,128)S(1)}, u32[]{:S(2)}, u32[]{:S(2)}) collective-permute-start(f32[16,16,512]{2,1,0:T(8,128)S(1)} %get-tuple-element.30), channel_id=1, source_target_pairs={{1,0},{2,1},{3,2},{4,3},{5,4},{6,5},{7,6},{8,7},{9,8},{10,9},{11,1... | collective-permute-start | bytes 1572872 | tf_op jit(solution)/shard_map/ppermute | solution.py:487
  10.2 4.8 %front.1 = (f32[2,16,128]{2,1,0:T(8,128)S(1)}, f32[2,16,128]{2,1,0:T(8,128)S(1)}, f32[2,16,128]{2,1,0:T(8,128)S(1)}, f32[2,16,128]{2,1,0:T(8,128)S(1)}, bf16[256,512]{1,0:T(8,128)(2,1)S(1)}) custom-call(s32[8]{0:T(128)S(1)} %copy-done.4, s32[1,1]{1,0:T(1,128)S(6)} %copy.20.counts, f32[16,16,16,512]{3,2,1,0:T(8,128)S(1)} %bitcast.8, s32[1,256]{1,0:T(1,128)S(1)} %bitcast.9, ...), custom_call_target="tpu_custom_call" | custom-call | tf_op jit(solution)/shard_map/front/pallas_call | solution.py:158
  15.1 1.3 %collective-permute-start.3 = (f32[2,16,128]{2,1,0:T(8,128)S(1)}, f32[2,16,128]{2,1,0:T(8,128)S(1)}, u32[]{:S(2)}, u32[]{:S(2)}) collective-permute-start(f32[2,16,128]{2,1,0:T(8,128)S(1)} %get-tuple-element.34), channel_id=1, source_target_pairs={{0,32},{1,33},{2,34},{3,35},{4,36},{5,37},{6,38},{7,39},{8,40},{9,... | collective-permute-start | bytes 49160 | tf_op jit(solution)/shard_map/ppermute | solution.py:487
  16.4 2.5 %collective-permute-start.4 = (f32[2,16,128]{2,1,0:T(8,128)S(1)}, f32[2,16,128]{2,1,0:T(8,128)S(1)}, u32[]{:S(2)}, u32[]{:S(2)}) collective-permute-start(f32[2,16,128]{2,1,0:T(8,128)S(1)} %get-tuple-element.35), channel_id=1, source_target_pairs={{0,64},{1,65},{2,66},{3,67},{4,68},{5,69},{6,70},{7,71},{8,72},{9,... | collective-permute-start | bytes 49160 | tf_op jit(solution)/shard_map/ppermute | solution.py:487
  18.8 0.2 collective-permute-start.5
  19.0 1.4 %collective-permute-done.4.two = f32[2,16,128]{2,1,0:T(8,128)S(1)} collective-permute-done((f32[2,16,128]{2,1,0:T(8,128)S(1)}, f32[2,16,128]{2,1,0:T(8,128)S(1)}, u32[]{:S(2)}, u32[]{:S(2)}) %collective-permute-start.4) | collective-permute-done | bytes 16416 | tf_op jit(solution)/shard_map/ppermute | solution.py:487
  20.5 2.2 %collective-permute-done.5.three = f32[2,16,128]{2,1,0:T(8,128)S(1)} collective-permute-done((f32[2,16,128]{2,1,0:T(8,128)S(1)}, f32[2,16,128]{2,1,0:T(8,128)S(1)}, u32[]{:S(2)}, u32[]{:S(2)}) %collective-permute-start.5) | collective-permute-done | bytes 16416 | tf_op jit(solution)/shard_map/ppermute | solution.py:487
  22.8 0.7 collective-permute-start.7
  23.5 4.2 %collective-permute-start.2 = (f32[16,16,512]{2,1,0:T(8,128)S(1)}, f32[16,16,512]{2,1,0:T(8,128)S(1)}, u32[]{:S(2)}, u32[]{:S(2)}) collective-permute-start(f32[16,16,512]{2,1,0:T(8,128)S(1)} %get-tuple-element.32), channel_id=1, source_target_pairs={{0,16},{1,17},{2,18},{3,19},{4,20},{5,21},{6,22},{7,23},{8,24},{9,... | collective-permute-start | bytes 1572872 | tf_op jit(solution)/shard_map/ppermute | solution.py:487
  27.8 0.4 collective-permute-start.8
  28.2 2.8 %collective-permute-start.9 = (f32[3,16,128]{2,1,0:T(8,128)S(1)}, f32[3,16,128]{2,1,0:T(8,128)S(1)}, u32[]{:S(2)}, u32[]{:S(2)}) collective-permute-start(f32[3,16,128]{2,1,0:T(8,128)S(1)} %get-tuple-element.40.own), channel_id=1, source_target_pairs={{0,24},{1,25},{2,26},{3,27},{4,28},{5,29},{6,30},{7,31},{8,16},{9,... | collective-permute-start | bytes 73736 | tf_op jit(solution)/shard_map/ppermute | solution.py:487
  31.0 23.6 %collective-permute-done.8.one = f32[3,16,128]{2,1,0:T(8,128)S(1)} collective-permute-done((f32[3,16,128]{2,1,0:T(8,128)S(1)}, f32[3,16,128]{2,1,0:T(8,128)S(1)}, u32[]{:S(2)}, u32[]{:S(2)}) %collective-permute-start.8) | collective-permute-done | bytes 24608 | tf_op jit(solution)/shard_map/ppermute | solution.py:487
  54.7 1.7 %collective-permute-start.10 = (f32[5,16,128]{2,1,0:T(8,128)S(1)}, f32[5,16,128]{2,1,0:T(8,128)S(1)}, u32[]{:S(2)}, u32[]{:S(2)}) collective-permute-start(f32[5,16,128]{2,1,0:T(8,128)S(1)} %spread.1), channel_id=1, source_target_pairs={{0,2},{1,3},{2,0},{3,1},{4,6},{5,7},{6,4},{7,5},{8,10},{9,11},{10,... | collective-permute-start | bytes 122888 | tf_op jit(solution)/shard_map/ppermute | solution.py:487
  56.4 1.4 %collective-permute-done.10 = f32[5,16,128]{2,1,0:T(8,128)S(1)} collective-permute-done((f32[5,16,128]{2,1,0:T(8,128)S(1)}, f32[5,16,128]{2,1,0:T(8,128)S(1)}, u32[]{:S(2)}, u32[]{:S(2)}) %collective-permute-start.10) | collective-permute-done | bytes 40992 | tf_op jit(solution)/shard_map/ppermute | solution.py:487
  57.8 3.1 %collective-permute-start.11 = (f32[5,16,128]{2,1,0:T(8,128)S(1)}, f32[5,16,128]{2,1,0:T(8,128)S(1)}, u32[]{:S(2)}, u32[]{:S(2)}) collective-permute-start(f32[5,16,128]{2,1,0:T(8,128)S(1)} %add.9), channel_id=1, source_target_pairs={{0,4},{1,5},{2,6},{3,7},{4,0},{5,1},{6,2},{7,3},{8,12},{9,13},{10,... | collective-permute-start | bytes 122888 | tf_op jit(solution)/shard_map/ppermute | solution.py:487
  60.9 1.4 %collective-permute-done.11 = f32[5,16,128]{2,1,0:T(8,128)S(1)} collective-permute-done((f32[5,16,128]{2,1,0:T(8,128)S(1)}, f32[5,16,128]{2,1,0:T(8,128)S(1)}, u32[]{:S(2)}, u32[]{:S(2)}) %collective-permute-start.11) | collective-permute-done | bytes 40992 | tf_op jit(solution)/shard_map/ppermute | solution.py:487
  62.3 3.5 %collective-permute-start.12 = (f32[5,16,128]{2,1,0:T(8,128)S(1)}, f32[5,16,128]{2,1,0:T(8,128)S(1)}, u32[]{:S(2)}, u32[]{:S(2)}) collective-permute-start(f32[5,16,128]{2,1,0:T(8,128)S(1)} %add.10), channel_id=1, source_target_pairs={{0,1},{1,0},{2,3},{3,2},{4,5},{5,4},{6,7},{7,6},{8,9},{9,8},{10,11... | collective-permute-start | bytes 122888 | tf_op jit(solution)/shard_map/ppermute | solution.py:487
  65.9 3.2 %interior.4 = (f32[2,8,16,16,512]{4,3,2,1,0:T(8,128)}, f32[2,2,2,16,512]{4,3,2,1,0:T(8,128)S(1)}, f32[2,2,16,16,128]{4,3,2,1,0:T(8,128)S(1)}, f32[3,16,16,512]{3,2,1,0:T(8,128)S(1)}) custom-call(f32[2,8,16,16,512]{4,3,2,1,0:T(8,128)S(1)} %copy-done, bf16[3,16,16,512]{3,2,1,0:T(8,128)(2,1)S(1)} %copy-done.1, f32[16,16,512]{2,1,0:T(8,128)S(1)} %collective-permute-done.before, ...), custom_call_target="tpu_custom_call" | custom-call | tf_op jit(solution)/shard_map/interior/pallas_call | solution.py:364
  69.1 3.0 %interior.5 = (f32[2,8,16,16,512]{4,3,2,1,0:T(8,128)}, f32[2,2,2,16,512]{4,3,2,1,0:T(8,128)S(1)}, f32[2,2,16,16,128]{4,3,2,1,0:T(8,128)S(1)}) custom-call(f32[2,8,16,16,512]{4,3,2,1,0:T(8,128)S(1)} %copy-done, f32[3,16,16,512]{3,2,1,0:T(8,128)S(1)} %get-tuple-element.31.given.scales, ...), custom_call_target="tpu_custom_call", output_to_operand_aliasing={{0}: (4, {})} | custom-call | tf_op jit(solution)/shard_map/interior/pallas_call | solution.py:364
  72.1 3.0 %interior.6 = (f32[2,8,16,16,512]{4,3,2,1,0:T(8,128)}, f32[2,2,2,16,512]{4,3,2,1,0:T(8,128)S(1)}, f32[2,2,16,16,128]{4,3,2,1,0:T(8,128)S(1)}) custom-call(f32[2,8,16,16,512]{4,3,2,1,0:T(8,128)S(1)} %copy-done, f32[3,16,16,512]{3,2,1,0:T(8,128)S(1)} %get-tuple-element.31.given.scales, ...), custom_call_target="tpu_custom_call", output_to_operand_aliasing={{0}: (4, {})} | custom-call | tf_op jit(solution)/shard_map/interior/pallas_call | solution.py:364
  75.1 3.0 %interior.7 = (f32[2,8,16,16,512]{4,3,2,1,0:T(8,128)}, f32[2,2,2,16,512]{4,3,2,1,0:T(8,128)S(1)}, f32[2,2,16,16,128]{4,3,2,1,0:T(8,128)S(1)}) custom-call(f32[2,8,16,16,512]{4,3,2,1,0:T(8,128)S(1)} %copy-done, f32[3,16,16,512]{3,2,1,0:T(8,128)S(1)} %get-tuple-element.31.given.scales, ...), custom_call_target="tpu_custom_call", output_to_operand_aliasing={{0}: (4, {})} | custom-call | tf_op jit(solution)/shard_map/interior/pallas_call | solution.py:364
  78.1 3.2 %final.1 = (f32[16,16,16,512]{3,2,1,0:T(8,128)}, f32[2,4,8]{2,1,0:T(4,128)}) custom-call(f32[3,16,16,512]{3,2,1,0:T(8,128)S(1)} %get-tuple-element.31.given.scales, f32[16,16,512]{2,1,0:T(8,128)S(1)} %collective-permute-done.2.same_plane, f32[11,16,128]{2,1,0:T(8,128)S(1)} %collective-permute-done.6.two.same_corner, ...), custom_call_target="tpu_custom_call", output_to_operand_aliasing={{0}: (14, {})} | custom-call | tf_op jit(solution)/shard_map/final/pallas_call | solution.py:456
  (24 shorter events, 0.4 us)
Async XLA Ops:
  0.6 9.6 %copy-start = (f32[2,8,16,16,512]{4,3,2,1,0:T(8,128)S(1)}, f32[2,8,16,16,512]{4,3,2,1,0:T(8,128)}, u32[]{:S(2)}) copy-start(f32[2,8,16,16,512]{4,3,2,1,0:T(8,128)} %volume.7) | copy-start | bytes 25165828
  0.6 9.6 %copy-start.2 = (s32[1,1,256]{2,1,0:T(1,128)S(1)}, s32[1,1,256]{2,1,0:T(1,128)}, u32[]{:S(2)}) copy-start(s32[1,1,256]{2,1,0:T(1,128)} %param.13) | copy-start | bytes 3076
  0.7 9.6 %copy-start.3 = (s32[1,1,256]{2,1,0:T(1,128)S(1)}, s32[1,1,256]{2,1,0:T(1,128)}, u32[]{:S(2)}) copy-start(s32[1,1,256]{2,1,0:T(1,128)} %param.14) | copy-start | bytes 3076
  0.7 9.6 %copy-start.4 = (s32[8]{0:T(128)S(1)}, s32[8]{0:T(128)}, u32[]{:S(2)}) copy-start(s32[8]{0:T(128)} %upsample.1) | copy-start | bytes 100
  2.4 63.5 %copy-start.1 = (bf16[3,16,16,512]{3,2,1,0:T(8,128)(2,1)S(1)}, bf16[3,16,16,512]{3,2,1,0:T(8,128)(2,1)}, u32[]{:S(2)}) copy-start(bf16[3,16,16,512]{3,2,1,0:T(8,128)(2,1)} %given.1) | copy-start | bytes 2359300
  2.4 20.2 %collective-permute-start = (f32[16,16,512]{2,1,0:T(8,128)S(1)}, f32[16,16,512]{2,1,0:T(8,128)S(1)}, u32[]{:S(2)}, u32[]{:S(2)}) collective-permute-start(f32[16,16,512]{2,1,0:T(8,128)S(1)} %get-tuple-element.29), channel_id=1, source_target_pairs={{0,1},{1,2},{2,3},{3,4},{4,5},{5,6},{6,7},{7,8},{8,9},{9,10},{10,1... | collective-permute-start | bytes 1572872 | tf_op jit(solution)/shard_map/ppermute | solution.py:487
  7.6 15.0 %collective-permute-start.1 = (f32[16,16,512]{2,1,0:T(8,128)S(1)}, f32[16,16,512]{2,1,0:T(8,128)S(1)}, u32[]{:S(2)}, u32[]{:S(2)}) collective-permute-start(f32[16,16,512]{2,1,0:T(8,128)S(1)} %get-tuple-element.30), channel_id=1, source_target_pairs={{1,0},{2,1},{3,2},{4,3},{5,4},{6,5},{7,6},{8,7},{9,8},{10,9},{11,1... | collective-permute-start | bytes 1572872 | tf_op jit(solution)/shard_map/ppermute | solution.py:487
  15.1 3.9 %collective-permute-start.3 = (f32[2,16,128]{2,1,0:T(8,128)S(1)}, f32[2,16,128]{2,1,0:T(8,128)S(1)}, u32[]{:S(2)}, u32[]{:S(2)}) collective-permute-start(f32[2,16,128]{2,1,0:T(8,128)S(1)} %get-tuple-element.34), channel_id=1, source_target_pairs={{0,32},{1,33},{2,34},{3,35},{4,36},{5,37},{6,38},{7,39},{8,40},{9,... | collective-permute-start | bytes 49160 | tf_op jit(solution)/shard_map/ppermute | solution.py:487
  16.4 4.1 %collective-permute-start.4 = (f32[2,16,128]{2,1,0:T(8,128)S(1)}, f32[2,16,128]{2,1,0:T(8,128)S(1)}, u32[]{:S(2)}, u32[]{:S(2)}) collective-permute-start(f32[2,16,128]{2,1,0:T(8,128)S(1)} %get-tuple-element.35), channel_id=1, source_target_pairs={{0,64},{1,65},{2,66},{3,67},{4,68},{5,69},{6,70},{7,71},{8,72},{9,... | collective-permute-start | bytes 49160 | tf_op jit(solution)/shard_map/ppermute | solution.py:487
  18.8 3.8 %collective-permute-start.5 = (f32[2,16,128]{2,1,0:T(8,128)S(1)}, f32[2,16,128]{2,1,0:T(8,128)S(1)}, u32[]{:S(2)}, u32[]{:S(2)}) collective-permute-start(f32[2,16,128]{2,1,0:T(8,128)S(1)} %get-tuple-element.36), channel_id=1, source_target_pairs={{0,96},{1,97},{2,98},{3,99},{4,100},{5,101},{6,102},{7,103},{8,104... | collective-permute-start | bytes 49160 | tf_op jit(solution)/shard_map/ppermute | solution.py:487
  22.8 55.3 %collective-permute-start.7 = (f32[18,16,512]{2,1,0:T(8,128)S(1)}, f32[18,16,512]{2,1,0:T(8,128)S(1)}, u32[]{:S(2)}, u32[]{:S(2)}) collective-permute-start(f32[18,16,512]{2,1,0:T(8,128)S(1)} %get-tuple-element.39), channel_id=1, source_target_pairs={{16,32},{17,33},{18,34},{19,35},{20,36},{21,37},{22,38},{23,39},{2... | collective-permute-start | bytes 1769480 | tf_op jit(solution)/shard_map/ppermute | solution.py:487
  23.5 54.6 %collective-permute-start.2 = (f32[16,16,512]{2,1,0:T(8,128)S(1)}, f32[16,16,512]{2,1,0:T(8,128)S(1)}, u32[]{:S(2)}, u32[]{:S(2)}) collective-permute-start(f32[16,16,512]{2,1,0:T(8,128)S(1)} %get-tuple-element.32), channel_id=1, source_target_pairs={{0,16},{1,17},{2,18},{3,19},{4,20},{5,21},{6,22},{7,23},{8,24},{9,... | collective-permute-start | bytes 1572872 | tf_op jit(solution)/shard_map/ppermute | solution.py:487
  27.7 26.9 %collective-permute-start.6 = (f32[11,16,128]{2,1,0:T(8,128)S(1)}, f32[11,16,128]{2,1,0:T(8,128)S(1)}, u32[]{:S(2)}, u32[]{:S(2)}) collective-permute-start(f32[11,16,128]{2,1,0:T(8,128)S(1)} %get-tuple-element.38), channel_id=1, source_target_pairs={{0,16},{1,17},{2,18},{3,19},{4,20},{5,21},{6,22},{7,23},{8,24},{9,... | collective-permute-start | bytes 270344 | tf_op jit(solution)/shard_map/ppermute | solution.py:487
  27.8 26.8 %collective-permute-start.8 = (f32[3,16,128]{2,1,0:T(8,128)S(1)}, f32[3,16,128]{2,1,0:T(8,128)S(1)}, u32[]{:S(2)}, u32[]{:S(2)}) collective-permute-start(f32[3,16,128]{2,1,0:T(8,128)S(1)} %get-tuple-element.40.own), channel_id=1, source_target_pairs={{0,8},{1,9},{2,10},{3,11},{4,12},{5,13},{6,14},{7,15},{8,0},{9,1},... | collective-permute-start | bytes 73736 | tf_op jit(solution)/shard_map/ppermute | solution.py:487
  28.2 26.4 %collective-permute-start.9 = (f32[3,16,128]{2,1,0:T(8,128)S(1)}, f32[3,16,128]{2,1,0:T(8,128)S(1)}, u32[]{:S(2)}, u32[]{:S(2)}) collective-permute-start(f32[3,16,128]{2,1,0:T(8,128)S(1)} %get-tuple-element.40.own), channel_id=1, source_target_pairs={{0,24},{1,25},{2,26},{3,27},{4,28},{5,29},{6,30},{7,31},{8,16},{9,... | collective-permute-start | bytes 73736 | tf_op jit(solution)/shard_map/ppermute | solution.py:487
  54.7 3.1 %collective-permute-start.10 = (f32[5,16,128]{2,1,0:T(8,128)S(1)}, f32[5,16,128]{2,1,0:T(8,128)S(1)}, u32[]{:S(2)}, u32[]{:S(2)}) collective-permute-start(f32[5,16,128]{2,1,0:T(8,128)S(1)} %spread.1), channel_id=1, source_target_pairs={{0,2},{1,3},{2,0},{3,1},{4,6},{5,7},{6,4},{7,5},{8,10},{9,11},{10,... | collective-permute-start | bytes 122888 | tf_op jit(solution)/shard_map/ppermute | solution.py:487
  57.8 4.6 %collective-permute-start.11 = (f32[5,16,128]{2,1,0:T(8,128)S(1)}, f32[5,16,128]{2,1,0:T(8,128)S(1)}, u32[]{:S(2)}, u32[]{:S(2)}) collective-permute-start(f32[5,16,128]{2,1,0:T(8,128)S(1)} %add.9), channel_id=1, source_target_pairs={{0,4},{1,5},{2,6},{3,7},{4,0},{5,1},{6,2},{7,3},{8,12},{9,13},{10,... | collective-permute-start | bytes 122888 | tf_op jit(solution)/shard_map/ppermute | solution.py:487
  62.3 15.8 %collective-permute-start.12 = (f32[5,16,128]{2,1,0:T(8,128)S(1)}, f32[5,16,128]{2,1,0:T(8,128)S(1)}, u32[]{:S(2)}, u32[]{:S(2)}) collective-permute-start(f32[5,16,128]{2,1,0:T(8,128)S(1)} %add.10), channel_id=1, source_target_pairs={{0,1},{1,0},{2,3},{3,2},{4,5},{5,4},{6,7},{7,6},{8,9},{9,8},{10,11... | collective-permute-start | bytes 122888 | tf_op jit(solution)/shard_map/ppermute | solution.py:487

commit v2 on v1

--- a/solution.py
+++ b/solution.py
@@ -13,7 +13,7 @@
 F32 = jnp.float32
 BF16 = jnp.bfloat16
 NT = (((1,), (1,)), ((), ()))
-TN = (((0,), (0,)), ((), ()))
+NN = (((1,), (0,)), ((), ()))
 
 
 def split3(value):
@@ -22,6 +22,15 @@
     middle = rest.astype(BF16)
     low = (rest - middle.astype(F32)).astype(BF16)
     return high, middle, low
+
+
+def three_rows(value):
+    return jnp.concatenate(split3(value), axis=0)
+
+
+def sum_of_three(value):
+    size = value.shape[0] // 3
+    return (value[2 * size :] + value[size : 2 * size]) + value[:size]
 
 
 VMEM = pl.BlockSpec(memory_space=pltpu.VMEM)
@@ -101,11 +110,12 @@
     live = lax.broadcasted_iota(jnp.int32, (1, slots), 1) < counts[0, 0]
     cell_of = jnp.where(live, cells[...], -1)
     cell_hit = lax.broadcasted_iota(jnp.int32, (cell_count, slots), 0) == cell_of
-    row_of = rows[...] ^ (wide * (row_count // 8))
-    row_hit = lax.broadcasted_iota(jnp.int32, (row_count, slots), 0) == row_of
+    row_of = (rows[...] ^ (wide * (row_count // 8))).astype(F32)
+    row_of = jnp.broadcast_to(row_of, (8, slots)).T[:, :1]
+    row_hit = lax.broadcasted_iota(jnp.int32, (slots, row_count), 1).astype(F32) == row_of
     cell_hit = jnp.where(cell_hit, 1.0, 0.0).astype(BF16)
     row_hit = jnp.where(row_hit, 1.0, 0.0).astype(BF16)
-    counted = lax.dot_general(cell_hit, row_hit, NT, preferred_element_type=F32).astype(BF16)
+    counted = lax.dot_general(cell_hit, row_hit, NN, preferred_element_type=F32).astype(BF16)
     count_out[...] = counted
 
     at = lax.broadcasted_iota(jnp.int32, (cell_count, 128), 1)
@@ -113,9 +123,12 @@
     for channel in range(channels):
         value = volume[channel, :, :, pl.ds(size_z - 128, 128)].reshape(cell_count, 128)
         tops = jnp.where(at == channel, pltpu.roll(value, (channel + 1) % 128, 1), tops)
-    traces = jnp.zeros((128, row_count), F32)
-    for piece in reversed(split3(tops)):
-        traces = traces + lax.dot_general(piece, counted, TN, preferred_element_type=F32)
+    traces = sum_of_three(
+        lax.dot_general(
+            three_rows(tops.T[:channels]), counted, NN, preferred_element_type=F32
+        )
+    )
+
     blocks = upsample.shape[0]
     width = density.shape[1] // blocks
     group = matrix.shape[2]
@@ -125,22 +138,24 @@
     pairs = []
     for block in range(blocks):
         here = density[:, pl.ds(block * width, width)]
+        following = jnp.where(lane == width - 1, here, pltpu.roll(here, width - 1, 1))
         factor = upsample[block]
         inverse = jnp.where(
             factor == 1, 1.0, jnp.where(factor == 2, 0.5, jnp.where(factor == 3, 1.0 / 3.0, 0.25))
         )
-        pairs.append((here, factor, inverse))
+        pairs.append((here, following, factor, inverse))
     for level in range(UMAX):
-        level_copies[level].wait()
-        for block, (here, factor, inverse) in enumerate(pairs):
-            following = jnp.where(lane == width - 1, here, pltpu.roll(here, width - 1, 1))
+        pieces = []
+        for here, following, factor, inverse in pairs:
             share = jnp.where(level < factor, inverse, 0.0)
             blend = level * inverse
             fine = ((1.0 - blend) * share) * here + (blend * share) * following
-            both = matrix[level, :, :, pl.ds(block * width, width)].reshape(2 * group, width)
-            total = total + lax.dot_general(
-                fine.astype(BF16), both, NT, preferred_element_type=F32
-            )
+            pieces.append(fine.astype(BF16))
+        level_copies[level].wait()
+        both = matrix[level].reshape(2 * group, matrix.shape[3])
+        total = total + lax.dot_general(
+            jnp.concatenate(pieces, axis=1), both, NT, preferred_element_type=F32
+        )
 
     waves = channels // 2
     turned = pltpu.roll(total, group, 1)
@@ -170,74 +185,48 @@
     )(upsample, counts, near(volume), near(cells), near(rows), afar(density), afar(matrix))
 
 
-def join_kernel(own, one, two, three, before, after, cross_in, out, corner, cross, sems):
-    group = 64
-    channels, size_x, size_z = before.shape
+def edges_kernel(before, after, cross_in, corner, cross, sems):
+    channels, size_x, _ = before.shape
     same_x, cross_x = sides_of(size_x)
-    copies = [
-        pltpu.make_async_copy(face.at[:, cross_x], cross.at[channels + k], sems.at[k])
-        for k, face in enumerate((before, after))
-    ]
-    for copy in copies:
-        copy.start()
-    lane = lax.broadcasted_iota(jnp.int32, own.shape[1:], 1)
-    sums = (
-        jnp.where(lane < group, own[0], pltpu.roll(one[0], group, 1)),
-        jnp.where(lane < group, two[0], pltpu.roll(three[0], group, 1)),
-        (own[1] + one[1]) + (two[1] + three[1]),
-    )
-    for k in range(3):
-        out[k] = sums[k]
-        corner[k] = sums[k]
-    for channel in range(channels):
-        for k, face in enumerate((before, after)):
-            row = face[channel, pl.ds(same_x, 1), :]
-            for tile in range(size_z // 128):
-                corner[3 + 4 * k + tile, pl.ds(channel, 1), :] = row[
-                    :, 128 * tile : 128 * (tile + 1)
-                ]
-    for copy in copies:
-        copy.wait()
-
-
-def join(own, one, two, three, before, after, cross):
-    channels = before.shape[0]
-    operands = [near(v) for v in (own, one, two, three, before, after, cross)]
-    return pl.pallas_call(
-        join_kernel,
-        in_specs=[VMEM] * 7,
-        out_specs=[VMEM] * 3,
-        out_shape=[
-            pltpu.VMEM((3, channels, 128), F32),
-            pltpu.VMEM((11, channels, 128), F32),
-            pltpu.VMEM(cross.shape, F32),
-        ],
-        scratch_shapes=[pltpu.SemaphoreType.DMA((2,))],
-        input_output_aliases={6: 2},
-        compiler_params=LIMIT,
-        name="join",
-    )(*operands)
-
-
-def spread_kernel(own, one, two, three, out):
+    copies = []
+    for k, face in enumerate((before, after)):
+        copies.append(
+            pltpu.make_async_copy(face.at[:, cross_x], cross.at[channels + k], sems.at[0, k])
+        )
+        copies.append(pltpu.make_async_copy(face.at[:, same_x], corner.at[k], sems.at[1, k]))
+    run_all(copies)
+
+
+def edges_of(before, after, cross):
+    channels, _, size_z = before.shape
+    return pl.pallas_call(
+        edges_kernel,
+        in_specs=[VMEM] * 3,
+        out_specs=[VMEM] * 2,
+        out_shape=[pltpu.VMEM((2, channels, size_z), F32), pltpu.VMEM(cross.shape, F32)],
+        scratch_shapes=[pltpu.SemaphoreType.DMA((2, 2))],
+        input_output_aliases={2: 1},
+        compiler_params=LIMIT,
+        name="edges",
+    )(near(before), near(after), near(cross))
+
+
+def join_kernel(own, one, two, three, out):
     group = 64
     lane = lax.broadcasted_iota(jnp.int32, own.shape[1:], 1)
-    for pair in range(2):
-        close = own[pair] + one[pair]
-        distant = two[pair] + three[pair]
-        out[2 * pair] = jnp.where(lane < group, close, pltpu.roll(distant, group, 1))
-        out[2 * pair + 1] = jnp.where(lane < group, pltpu.roll(close, group, 1), distant)
-    out[4] = (own[2] + one[2]) + pltpu.roll(two[2] + three[2], group, 1)
-
-
-def spread(own, one, two, three):
-    return pl.pallas_call(
-        spread_kernel,
+    out[0] = jnp.where(lane < group, own[0], pltpu.roll(one[0], group, 1))
+    out[1] = jnp.where(lane < group, two[0], pltpu.roll(three[0], group, 1))
+    out[2] = (own[1] + one[1]) + (two[1] + three[1])
+
+
+def join(own, one, two, three):
+    return pl.pallas_call(
+        join_kernel,
         in_specs=[VMEM] * 4,
         out_specs=VMEM,
-        out_shape=pltpu.VMEM((5,) + own.shape[1:], F32),
-        compiler_params=LIMIT,
-        name="spread",
+        out_shape=pltpu.VMEM((3,) + own.shape[1:], F32),
+        compiler_params=LIMIT,
+        name="join",
     )(*[near(value) for value in (own, one, two, three)])
 
 
@@ -378,81 +367,107 @@
     )(*operands)
 
 
-def final_kernel(scales, same_plane, same_corner, cross_plane, small, counted, *refs):
-    edges = refs[: 2 * CALLS]
-    out, boundary, planes, tops, sems = refs[2 * CALLS + 1 :]
+def side_kernel(scales, plane, ends, *refs, side):
+    begun, out = refs[:CALLS], refs[CALLS]
+    channels = out.shape[0]
+    waves = channels // 2
+    count = waves // CALLS
+    size_x = scales.shape[1]
+    place = sides_of(size_x)[side]
+    end = jnp.where(place == 0, 0, 1)
+    base = ends.shape[0] - 2
+    scale = 0.5 * scales[1, place]
+    for channel in range(channels):
+        part, wave = divmod(channel, waves)
+        value = plane[channel]
+        low, high = [ends[base + k, pl.ds(channel, 1), :] for k in range(2)]
+        total = y_sum(value, low, high)
+        nearby = z_sum(total + (value + value)) + (total + total)
+        out[channel] = begun[wave // count][end, part, wave % count] - scale * nearby
+
+
+def one_side(scales, plane, ends, begun, side):
+    size_y, size_z = scales.shape[2], scales.shape[3]
+    return pl.pallas_call(
+        partial(side_kernel, side=side),
+        in_specs=[VMEM] * (3 + CALLS),
+        out_specs=VMEM,
+        out_shape=pltpu.VMEM((begun[0].shape[1] * begun[0].shape[2] * CALLS, size_y, size_z), F32),
+        compiler_params=LIMIT,
+        name="side",
+    )(*[near(value) for value in (scales, plane, ends, *begun)])
+
+
+def final_kernel(same, cross, zero, one, two, three, counted, *refs):
+    begun = refs[:CALLS]
+    out, boundary, planes, tops, sems = refs[CALLS + 1 :]
     narrow = lax.axis_index("narrow")
     channels, size_x, size_y, size_z = out.shape
     places = sides_of(size_x)
     last = size_x - 1
     low = size_z - 128
     waves = channels // 2
-    mine = pltpu.roll(small[0] - 0.25 * small[4], (128 - narrow * 4) % 128, 1)
-    mine = mine.T
-    boundary[0] = mine[:4, :waves]
-    boundary[1] = mine[:4, waves:]
-    rows = jnp.concatenate([small[k] for k in range(4)], axis=1)
-    added = jnp.zeros((counted.shape[0], channels), F32)
-    for piece in reversed(split3(rows)):
-        added = added + lax.dot_general(counted[...], piece, NT, preferred_element_type=F32)
-    added = jnp.concatenate([added, jnp.zeros((added.shape[0], 128 - channels), F32)], axis=1)
+    count = waves // CALLS
+
+    group = 64
+    lane = lax.broadcasted_iota(jnp.int32, (channels, 128), 1)
+    blocks = []
+    for pair in range(2):
+        close = zero[pair] + one[pair]
+        distant = two[pair] + three[pair]
+        blocks.append(jnp.where(lane < group, close, pltpu.roll(distant, group, 1)))
+        blocks.append(jnp.where(lane < group, pltpu.roll(close, group, 1), distant))
+    rows = three_rows(jnp.concatenate(blocks, axis=1))
+    added = sum_of_three(
+        lax.dot_general(rows, counted[...], NT, preferred_element_type=F32)
+    )
+    added = jnp.concatenate([added, jnp.zeros((128 - channels, added.shape[1]), F32)], axis=0).T
     at_top = lax.broadcasted_iota(jnp.int32, added.shape, 1) == 127
+
     copies = []
-    count = waves // CALLS
     even = places[1] == 0
     for channel in range(channels):
         part, wave = divmod(channel, waves)
-        source, source_top = edges[2 * (wave // count)], edges[2 * (wave // count) + 1]
-        wave = wave % count
         lifted = jnp.where(at_top, pltpu.roll(added, 127 - channel, 1), 0.0)
         lifted = lifted.reshape(size_x, size_y, 128)
-        for side in range(2):
-            scale = 0.5 * scales[1, places[side]]
-            if side == 0:
-                value = same_plane[channel]
-                ends = [
-                    jnp.concatenate(
-                        [
-                            same_corner[3 + 4 * k + tile, pl.ds(channel, 1), :]
-                            for tile in range(size_z // 128)
-                        ],
-                        axis=1,
-                    )
-                    for k in range(2)
-                ]
-                begun = source[jnp.where(even, 1, 0), part, wave]
-                raised = jnp.where(even, lifted[last], lifted[0])
-            else:
-                value = cross_plane[channel]
-                ends = [cross_plane[channels + k, pl.ds(channel, 1), :] for k in range(2)]
-                begun = source[jnp.where(even, 0, 1), part, wave]
-                raised = jnp.where(even, lifted[0], lifted[last])
-            total = y_sum(value, *ends)
-            total2 = total + total
-            nearby = z_sum(total + (value + value)) + total2
-            result = begun - scale * nearby
-            planes[side, channel, :, pl.ds(0, low)] = result[:, :low]
-            planes[side, channel, :, pl.ds(low, 128)] = result[:, low:] + raised
-            copy = pltpu.make_async_copy(
-                planes.at[side, channel], out.at[channel, places[side]], sems.at[side, channel]
+        raised = (
+            jnp.where(even, lifted[last], lifted[0]),
+            jnp.where(even, lifted[0], lifted[last]),
+        )
+        for side, source in enumerate((same, cross)):
+            planes[side, channel, :, pl.ds(0, low)] = source[channel, :, pl.ds(0, low)]
+            planes[side, channel, :, pl.ds(low, 128)] = (
+                source[channel, :, pl.ds(low, 128)] + raised[side]
             )
-            copy.start()
-            copies.append(copy)
-        tops[channel] = source_top[part, wave, pl.ds(1, size_x - 2)] + lifted[1:last]
-        copy = pltpu.make_async_copy(
-            tops.at[channel],
-            out.at[channel, pl.ds(1, size_x - 2), :, pl.ds(low, 128)],
-            sems.at[2, channel],
-        )
-        copy.start()
-        copies.append(copy)
+            copies.append(
+                pltpu.make_async_copy(
+                    planes.at[side, channel], out.at[channel, places[side]], sems.at[side, channel]
+                )
+            )
+            copies[-1].start()
+        tops[channel] = (
+            begun[wave // count][part, wave % count, pl.ds(1, size_x - 2)] + lifted[1:last]
+        )
+        copies.append(
+            pltpu.make_async_copy(
+                tops.at[channel],
+                out.at[channel, pl.ds(1, size_x - 2), :, pl.ds(low, 128)],
+                sems.at[2, channel],
+            )
+        )
+        copies[-1].start()
+
+    trace = (zero[2] + one[2]) + pltpu.roll(two[2] + three[2], group, 1)
+    mine = pltpu.roll(blocks[0] - 0.25 * trace, (128 - narrow * 4) % 128, 1).T
+    boundary[0] = mine[:4, :waves]
+    boundary[1] = mine[:4, waves:]
     for copy in copies:
         copy.wait()
 
 
-def final(scales, wide_faces, small, counted, edges, started):
+def final(same, cross, messages, counted, begun, started):
     channels, size_x, size_y, size_z = started.shape
-    close = [near(v) for v in (scales,) + wide_faces + (small, counted) + tuple(edges)]
+    close = [near(v) for v in (same, cross, *messages, counted, *begun)]
     return pl.pallas_call(
         final_kernel,
         in_specs=[VMEM] * len(close) + [ANY],
@@ -523,35 +538,27 @@
         moved(message, lambda w, n, s=step: (w ^ (2 * s), n))
         for step, message in ((1, one), (2, two), (3, three))
     ]
-    small, small_corner, cross_out = join(own, *got, before, after, cross_out)
+    corner_out, cross_out = edges_of(before, after, cross_out)
+    corner = moved(corner_out, lambda w, n: (w ^ 1, n))
+    cross_plane = moved(cross_out, lambda w, n: (w + (1 if w % 2 else -1), n))
 
     count = waves // CALLS
-    edges = []
-    started, *more, scales = interior(volume_field, coefficients, before, after, 0, count)
-    edges += more
-
-    def some_waves(call, started):
-        return interior(volume_field, scales, before, after, call * count, count, started)
-
-    got = [
-        moved(message, along_y(step))
-        for step, message in ((1, small), (2, small_corner), (3, small))
-    ]
-    same_corner = got[1]
-    cross_plane = moved(cross_out, lambda w, n: (w + (1 if w % 2 else -1), n))
-    small = spread(small, *got)
+    started, planes, top, scales = interior(volume_field, coefficients, before, after, 0, count)
+    planes, tops = [planes], [top]
+    small = join(own, *got)
     for call, step in enumerate((2, 4, 1)):
-        started, *more = some_waves(call + 1, started)
-        edges += more
+        started, plane, top = interior(
+            volume_field, scales, before, after, (call + 1) * count, count, started
+        )
+        planes.append(plane)
+        tops.append(top)
         small = small + moved(small, lambda w, n, s=step: (w, n ^ s))
+    messages = [small] + [moved(small, along_y(step)) for step in range(1, 4)]
+    same = one_side(scales, same_plane, corner, planes, 0)
+    cross = one_side(scales, cross_plane, cross_plane, planes, 1)
 
     volume_out, boundary = final(
-        scales,
-        (same_plane, same_corner, cross_plane),
-        small,
-        counted,
-        edges,
-        started.reshape(volume.shape),
+        same, cross, messages, counted, tops, started.reshape(volume.shape)
     )
     return volume_out.reshape(volume_field.shape), boundary.transpose(0, 2, 1)
 

time: 81.5 us -> 70.2 us (0.86)
  waiting for transfers between devices: 30.1 us -> 13.5 us
  starting transfers between devices: 27.6 us -> 31.5 us
  Pallas kernels: 22.2 us -> 23.4 us
    ppermute x13 -> x14, waiting for transfers between devices: 30.1 us -> 13.5 us  [moved(): return lax.ppermute(value, AXES, pairs)]
    ppermute x13 -> x14, starting transfers between devices: 27.6 us -> 31.5 us  [moved(): return lax.ppermute(value, AXES, pairs)]
  transfers between devices with their start and end apart: 13 -> 14, of which waited for: 5 -> 6; matrix products, arithmetic and copies ran while one was open for 0% -> 0% of each run, Pallas kernels for 21% -> 26%
where the time goes in v2:
time: 70.2 us; the launch traced here: 70 us
  starting transfers between devices  31.5 us (45%)
  Pallas kernels  23.4 us (33%)
  waiting for transfers between devices  13.5 us (19%)
  between operations  1.51 us (2%)
    ppermute x14, starting transfers between devices, moved(): return lax.ppermute(value, AXES, pairs)  31.5 us
    ppermute x14, waiting for transfers between devices, moved(): return lax.ppermute(value, AXES, pairs)  13.5 us
    pallas_call x4, Pallas kernels, interior(): pl.pallas_call(partial(interior_kernel, first=first, prepares=prepares),...  12.2 us
    pallas_call x1, Pallas kernels, front(): pl.pallas_call(front_kernel, in_specs=[SMEM, SMEM] + [VMEM] * 3 + [HBM] *...  5.41 us
    pallas_call x1, Pallas kernels, final(): pl.pallas_call(final_kernel, in_specs=[VMEM] * len(close) + [ANY], out_sp...  3.13 us
    pallas_call x1, Pallas kernels, faces(): pl.pallas_call(faces_kernel, in_specs=[HBM], out_specs=[VMEM] * 4, out_sh...  1.74 us
  transfers between devices with their start and end apart: 14, of which 6 were waited for; matrix products, arithmetic and copies ran while one was open for 0% of the time, Pallas kernels for 26%

profile of v2, /device:TPU:1, one launch (start us, length us, event | category | flops | bytes accessed | tf_op | source)
XLA Modules:
  0.0 70.0 jit_solution(2776885341957359684)
XLA Ops:
  0.7 1.7 %faces.1 = (f32[16,16,512]{2,1,0:T(8,128)S(1)}, f32[16,16,512]{2,1,0:T(8,128)S(1)}, f32[16,16,512]{2,1,0:T(8,128)S(1)}, f32[18,16,512]{2,1,0:T(8,128)S(1)}) custom-call(f32[16,16,16,512]{3,2,1,0:T(8,128)} %bitcast.7), custom_call_target="tpu_custom_call" | custom-call | tf_op jit(solution)/shard_map/faces/pallas_call | solution.py:78
  2.4 5.2 %collective-permute-start = (f32[16,16,512]{2,1,0:T(8,128)S(1)}, f32[16,16,512]{2,1,0:T(8,128)S(1)}, u32[]{:S(2)}, u32[]{:S(2)}) collective-permute-start(f32[16,16,512]{2,1,0:T(8,128)S(1)} %get-tuple-element.28), channel_id=1, source_target_pairs={{0,1},{1,2},{2,3},{3,4},{4,5},{5,6},{6,7},{7,8},{8,9},{9,10},{10,1... | collective-permute-start | bytes 1572872 | tf_op jit(solution)/shard_map/ppermute | solution.py:502
  7.6 1.9 %collective-permute-start.1 = (f32[16,16,512]{2,1,0:T(8,128)S(1)}, f32[16,16,512]{2,1,0:T(8,128)S(1)}, u32[]{:S(2)}, u32[]{:S(2)}) collective-permute-start(f32[16,16,512]{2,1,0:T(8,128)S(1)} %get-tuple-element.29), channel_id=1, source_target_pairs={{1,0},{2,1},{3,2},{4,3},{5,4},{6,5},{7,6},{8,7},{9,8},{10,9},{11,1... | collective-permute-start | bytes 1572872 | tf_op jit(solution)/shard_map/ppermute | solution.py:502
  9.6 4.2 %collective-permute-done.before = f32[16,16,512]{2,1,0:T(8,128)S(1)} collective-permute-done((f32[16,16,512]{2,1,0:T(8,128)S(1)}, f32[16,16,512]{2,1,0:T(8,128)S(1)}, u32[]{:S(2)}, u32[]{:S(2)}) %collective-permute-start) | collective-permute-done | bytes 524320 | tf_op jit(solution)/shard_map/ppermute | solution.py:502
  13.7 4.4 %collective-permute-done.1.after = f32[16,16,512]{2,1,0:T(8,128)S(1)} collective-permute-done((f32[16,16,512]{2,1,0:T(8,128)S(1)}, f32[16,16,512]{2,1,0:T(8,128)S(1)}, u32[]{:S(2)}, u32[]{:S(2)}) %collective-permute-start.1) | collective-permute-done | bytes 524320 | tf_op jit(solution)/shard_map/ppermute | solution.py:502
  19.0 5.2 %collective-permute-start.2 = (f32[16,16,512]{2,1,0:T(8,128)S(1)}, f32[16,16,512]{2,1,0:T(8,128)S(1)}, u32[]{:S(2)}, u32[]{:S(2)}) collective-permute-start(f32[16,16,512]{2,1,0:T(8,128)S(1)} %get-tuple-element.31), channel_id=1, source_target_pairs={{0,16},{1,17},{2,18},{3,19},{4,20},{5,21},{6,22},{7,23},{8,24},{9,... | collective-permute-start | bytes 1572872 | tf_op jit(solution)/shard_map/ppermute | solution.py:502
  24.9 5.4 %front.1 = (f32[2,16,128]{2,1,0:T(8,128)S(1)}, f32[2,16,128]{2,1,0:T(8,128)S(1)}, f32[2,16,128]{2,1,0:T(8,128)S(1)}, f32[2,16,128]{2,1,0:T(8,128)S(1)}, bf16[256,512]{1,0:T(8,128)(2,1)S(1)}) custom-call(s32[8]{0:T(128)S(1)} %copy-done.4, s32[1,1]{1,0:T(1,128)S(6)} %copy.20.counts, f32[16,16,16,512]{3,2,1,0:T(8,128)S(1)} %bitcast.8, s32[1,256]{1,0:T(1,128)S(1)} %bitcast.9, ...), custom_call_target="tpu_custom_call" | custom-call | tf_op jit(solution)/shard_map/front/pallas_call | solution.py:173
  30.3 1.3 %collective-permute-start.5 = (f32[2,16,128]{2,1,0:T(8,128)S(1)}, f32[2,16,128]{2,1,0:T(8,128)S(1)}, u32[]{:S(2)}, u32[]{:S(2)}) collective-permute-start(f32[2,16,128]{2,1,0:T(8,128)S(1)} %get-tuple-element.43), channel_id=1, source_target_pairs={{0,32},{1,33},{2,34},{3,35},{4,36},{5,37},{6,38},{7,39},{8,40},{9,... | collective-permute-start | bytes 49160 | tf_op jit(solution)/shard_map/ppermute | solution.py:502
  31.6 1.7 %collective-permute-start.6 = (f32[2,16,128]{2,1,0:T(8,128)S(1)}, f32[2,16,128]{2,1,0:T(8,128)S(1)}, u32[]{:S(2)}, u32[]{:S(2)}) collective-permute-start(f32[2,16,128]{2,1,0:T(8,128)S(1)} %get-tuple-element.44), channel_id=1, source_target_pairs={{0,64},{1,65},{2,66},{3,67},{4,68},{5,69},{6,70},{7,71},{8,72},{9,... | collective-permute-start | bytes 49160 | tf_op jit(solution)/shard_map/ppermute | solution.py:502
  33.3 0.9 %collective-permute-start.7 = (f32[2,16,128]{2,1,0:T(8,128)S(1)}, f32[2,16,128]{2,1,0:T(8,128)S(1)}, u32[]{:S(2)}, u32[]{:S(2)}) collective-permute-start(f32[2,16,128]{2,1,0:T(8,128)S(1)} %get-tuple-element.45), channel_id=1, source_target_pairs={{0,96},{1,97},{2,98},{3,99},{4,100},{5,101},{6,102},{7,103},{8,104... | collective-permute-start | bytes 49160 | tf_op jit(solution)/shard_map/ppermute | solution.py:502
  34.2 1.4 %collective-permute-done.6.two = f32[2,16,128]{2,1,0:T(8,128)S(1)} collective-permute-done((f32[2,16,128]{2,1,0:T(8,128)S(1)}, f32[2,16,128]{2,1,0:T(8,128)S(1)}, u32[]{:S(2)}, u32[]{:S(2)}) %collective-permute-start.6) | collective-permute-done | bytes 16416 | tf_op jit(solution)/shard_map/ppermute | solution.py:502
  35.7 1.4 %collective-permute-done.7.three = f32[2,16,128]{2,1,0:T(8,128)S(1)} collective-permute-done((f32[2,16,128]{2,1,0:T(8,128)S(1)}, f32[2,16,128]{2,1,0:T(8,128)S(1)}, u32[]{:S(2)}, u32[]{:S(2)}) %collective-permute-start.7) | collective-permute-done | bytes 16416 | tf_op jit(solution)/shard_map/ppermute | solution.py:502
  37.2 1.8 %collective-permute-start.8 = (f32[3,16,128]{2,1,0:T(8,128)S(1)}, f32[3,16,128]{2,1,0:T(8,128)S(1)}, u32[]{:S(2)}, u32[]{:S(2)}) collective-permute-start(f32[3,16,128]{2,1,0:T(8,128)S(1)} %join.1), channel_id=1, source_target_pairs={{0,2},{1,3},{2,0},{3,1},{4,6},{5,7},{6,4},{7,5},{8,10},{9,11},{10,... | collective-permute-start | bytes 73736 | tf_op jit(solution)/shard_map/ppermute | solution.py:502
  38.9 1.2 %collective-permute-done.8 = f32[3,16,128]{2,1,0:T(8,128)S(1)} collective-permute-done((f32[3,16,128]{2,1,0:T(8,128)S(1)}, f32[3,16,128]{2,1,0:T(8,128)S(1)}, u32[]{:S(2)}, u32[]{:S(2)}) %collective-permute-start.8) | collective-permute-done | bytes 24608 | tf_op jit(solution)/shard_map/ppermute | solution.py:502
  40.2 3.4 %collective-permute-start.9 = (f32[3,16,128]{2,1,0:T(8,128)S(1)}, f32[3,16,128]{2,1,0:T(8,128)S(1)}, u32[]{:S(2)}, u32[]{:S(2)}) collective-permute-start(f32[3,16,128]{2,1,0:T(8,128)S(1)} %add.9), channel_id=1, source_target_pairs={{0,4},{1,5},{2,6},{3,7},{4,0},{5,1},{6,2},{7,3},{8,12},{9,13},{10,... | collective-permute-start | bytes 73736 | tf_op jit(solution)/shard_map/ppermute | solution.py:502
  43.6 3.3 %collective-permute-start.3 = (f32[2,16,512]{2,1,0:T(8,128)S(1)}, f32[2,16,512]{2,1,0:T(8,128)S(1)}, u32[]{:S(2)}, u32[]{:S(2)}) collective-permute-start(f32[2,16,512]{2,1,0:T(8,128)S(1)} %get-tuple-element.33), channel_id=1, source_target_pairs={{0,16},{1,17},{2,18},{3,19},{4,20},{5,21},{6,22},{7,23},{8,24},{9,... | collective-permute-start | bytes 196616 | tf_op jit(solution)/shard_map/ppermute | solution.py:502
  46.9 2.0 %collective-permute-start.10 = (f32[3,16,128]{2,1,0:T(8,128)S(1)}, f32[3,16,128]{2,1,0:T(8,128)S(1)}, u32[]{:S(2)}, u32[]{:S(2)}) collective-permute-start(f32[3,16,128]{2,1,0:T(8,128)S(1)} %add.10), channel_id=1, source_target_pairs={{0,1},{1,0},{2,3},{3,2},{4,5},{5,4},{6,7},{7,6},{8,9},{9,8},{10,11... | collective-permute-start | bytes 73736 | tf_op jit(solution)/shard_map/ppermute | solution.py:502
  48.8 0.8 %collective-permute-done.10 = f32[3,16,128]{2,1,0:T(8,128)S(1)} collective-permute-done((f32[3,16,128]{2,1,0:T(8,128)S(1)}, f32[3,16,128]{2,1,0:T(8,128)S(1)}, u32[]{:S(2)}, u32[]{:S(2)}) %collective-permute-start.10) | collective-permute-done | bytes 24608 | tf_op jit(solution)/shard_map/ppermute | solution.py:502
  50.5 3.4 %collective-permute-start.12 = (f32[3,16,128]{2,1,0:T(8,128)S(1)}, f32[3,16,128]{2,1,0:T(8,128)S(1)}, u32[]{:S(2)}, u32[]{:S(2)}) collective-permute-start(f32[3,16,128]{2,1,0:T(8,128)S(1)} %add.11.zero), channel_id=1, source_target_pairs={{0,16},{1,17},{2,18},{3,19},{4,20},{5,21},{6,22},{7,23},{8,24},{9,... | collective-permute-start | bytes 73736 | tf_op jit(solution)/shard_map/ppermute | solution.py:502
  53.9 3.2 %interior.4 = (f32[2,8,16,16,512]{4,3,2,1,0:T(8,128)}, f32[2,2,2,16,512]{4,3,2,1,0:T(8,128)S(1)}, f32[2,2,16,16,128]{4,3,2,1,0:T(8,128)S(1)}, f32[3,16,16,512]{3,2,1,0:T(8,128)S(1)}) custom-call(f32[2,8,16,16,512]{4,3,2,1,0:T(8,128)S(1)} %copy-done, bf16[3,16,16,512]{3,2,1,0:T(8,128)(2,1)S(1)} %copy-done.1, f32[16,16,512]{2,1,0:T(8,128)S(1)} %collective-permute-done.before, ...), custom_call_target="tpu_custom_call" | custom-call | tf_op jit(solution)/shard_map/interior/pallas_call | solution.py:353
  57.1 3.0 %interior.5 = (f32[2,8,16,16,512]{4,3,2,1,0:T(8,128)}, f32[2,2,2,16,512]{4,3,2,1,0:T(8,128)S(1)}, f32[2,2,16,16,128]{4,3,2,1,0:T(8,128)S(1)}) custom-call(f32[2,8,16,16,512]{4,3,2,1,0:T(8,128)S(1)} %copy-done, f32[3,16,16,512]{3,2,1,0:T(8,128)S(1)} %get-tuple-element.30.given.scales, ...), custom_call_target="tpu_custom_call", output_to_operand_aliasing={{0}: (4, {})} | custom-call | tf_op jit(solution)/shard_map/interior/pallas_call | solution.py:353
  60.1 3.0 %interior.6 = (f32[2,8,16,16,512]{4,3,2,1,0:T(8,128)}, f32[2,2,2,16,512]{4,3,2,1,0:T(8,128)S(1)}, f32[2,2,16,16,128]{4,3,2,1,0:T(8,128)S(1)}) custom-call(f32[2,8,16,16,512]{4,3,2,1,0:T(8,128)S(1)} %copy-done, f32[3,16,16,512]{3,2,1,0:T(8,128)S(1)} %get-tuple-element.30.given.scales, ...), custom_call_target="tpu_custom_call", output_to_operand_aliasing={{0}: (4, {})} | custom-call | tf_op jit(solution)/shard_map/interior/pallas_call | solution.py:353
  63.1 3.0 %interior.7 = (f32[2,8,16,16,512]{4,3,2,1,0:T(8,128)}, f32[2,2,2,16,512]{4,3,2,1,0:T(8,128)S(1)}, f32[2,2,16,16,128]{4,3,2,1,0:T(8,128)S(1)}) custom-call(f32[2,8,16,16,512]{4,3,2,1,0:T(8,128)S(1)} %copy-done, f32[3,16,16,512]{3,2,1,0:T(8,128)S(1)} %get-tuple-element.30.given.scales, ...), custom_call_target="tpu_custom_call", output_to_operand_aliasing={{0}: (4, {})} | custom-call | tf_op jit(solution)/shard_map/interior/pallas_call | solution.py:353
  66.9 3.1 %final.1 = (f32[16,16,16,512]{3,2,1,0:T(8,128)}, f32[2,4,8]{2,1,0:T(4,128)}) custom-call(f32[16,16,512]{2,1,0:T(8,128)S(1)} %side.2.same, f32[16,16,512]{2,1,0:T(8,128)S(1)} %side.3.cross, f32[3,16,128]{2,1,0:T(8,128)S(1)} %add.11.zero, f32[3,16,128]{2,1,0:T(8,128)S(1)} %collective-permute-done.11.one, ...), custom_call_target="tpu_custom_call", output_to_operand_aliasing={{0}: (11, {})} | custom-call | tf_op jit(solution)/shard_map/final/pallas_call | solution.py:471
  (28 shorter events, 2.5 us)
Async XLA Ops:
  0.6 24.2 %copy-start = (f32[2,8,16,16,512]{4,3,2,1,0:T(8,128)S(1)}, f32[2,8,16,16,512]{4,3,2,1,0:T(8,128)}, u32[]{:S(2)}) copy-start(f32[2,8,16,16,512]{4,3,2,1,0:T(8,128)} %volume.7) | copy-start | bytes 25165828
  0.6 24.2 %copy-start.2 = (s32[1,1,256]{2,1,0:T(1,128)S(1)}, s32[1,1,256]{2,1,0:T(1,128)}, u32[]{:S(2)}) copy-start(s32[1,1,256]{2,1,0:T(1,128)} %param.13) | copy-start | bytes 3076
  0.7 24.2 %copy-start.3 = (s32[1,1,256]{2,1,0:T(1,128)S(1)}, s32[1,1,256]{2,1,0:T(1,128)}, u32[]{:S(2)}) copy-start(s32[1,1,256]{2,1,0:T(1,128)} %param.14) | copy-start | bytes 3076
  0.7 24.2 %copy-start.4 = (s32[8]{0:T(128)S(1)}, s32[8]{0:T(128)}, u32[]{:S(2)}) copy-start(s32[8]{0:T(128)} %upsample.1) | copy-start | bytes 100
  2.4 51.5 %copy-start.1 = (bf16[3,16,16,512]{3,2,1,0:T(8,128)(2,1)S(1)}, bf16[3,16,16,512]{3,2,1,0:T(8,128)(2,1)}, u32[]{:S(2)}) copy-start(bf16[3,16,16,512]{3,2,1,0:T(8,128)(2,1)} %given.1) | copy-start | bytes 2359300
  2.4 11.3 %collective-permute-start = (f32[16,16,512]{2,1,0:T(8,128)S(1)}, f32[16,16,512]{2,1,0:T(8,128)S(1)}, u32[]{:S(2)}, u32[]{:S(2)}) collective-permute-start(f32[16,16,512]{2,1,0:T(8,128)S(1)} %get-tuple-element.28), channel_id=1, source_target_pairs={{0,1},{1,2},{2,3},{3,4},{4,5},{5,6},{6,7},{7,8},{8,9},{9,10},{10,1... | collective-permute-start | bytes 1572872 | tf_op jit(solution)/shard_map/ppermute | solution.py:502
  7.6 10.5 %collective-permute-start.1 = (f32[16,16,512]{2,1,0:T(8,128)S(1)}, f32[16,16,512]{2,1,0:T(8,128)S(1)}, u32[]{:S(2)}, u32[]{:S(2)}) collective-permute-start(f32[16,16,512]{2,1,0:T(8,128)S(1)} %get-tuple-element.29), channel_id=1, source_target_pairs={{1,0},{2,1},{3,2},{4,3},{5,4},{6,5},{7,6},{8,7},{9,8},{10,9},{11,1... | collective-permute-start | bytes 1572872 | tf_op jit(solution)/shard_map/ppermute | solution.py:502
  18.3 48.2 %collective-permute-start.4 = (f32[18,16,512]{2,1,0:T(8,128)S(1)}, f32[18,16,512]{2,1,0:T(8,128)S(1)}, u32[]{:S(2)}, u32[]{:S(2)}) collective-permute-start(f32[18,16,512]{2,1,0:T(8,128)S(1)} %get-tuple-element.41), channel_id=1, source_target_pairs={{16,32},{17,33},{18,34},{19,35},{20,36},{21,37},{22,38},{23,39},{2... | collective-permute-start | bytes 1769480 | tf_op jit(solution)/shard_map/ppermute | solution.py:502
  19.0 34.9 %collective-permute-start.2 = (f32[16,16,512]{2,1,0:T(8,128)S(1)}, f32[16,16,512]{2,1,0:T(8,128)S(1)}, u32[]{:S(2)}, u32[]{:S(2)}) collective-permute-start(f32[16,16,512]{2,1,0:T(8,128)S(1)} %get-tuple-element.31), channel_id=1, source_target_pairs={{0,16},{1,17},{2,18},{3,19},{4,20},{5,21},{6,22},{7,23},{8,24},{9,... | collective-permute-start | bytes 1572872 | tf_op jit(solution)/shard_map/ppermute | solution.py:502
  30.3 3.9 %collective-permute-start.5 = (f32[2,16,128]{2,1,0:T(8,128)S(1)}, f32[2,16,128]{2,1,0:T(8,128)S(1)}, u32[]{:S(2)}, u32[]{:S(2)}) collective-permute-start(f32[2,16,128]{2,1,0:T(8,128)S(1)} %get-tuple-element.43), channel_id=1, source_target_pairs={{0,32},{1,33},{2,34},{3,35},{4,36},{5,37},{6,38},{7,39},{8,40},{9,... | collective-permute-start | bytes 49160 | tf_op jit(solution)/shard_map/ppermute | solution.py:502
  31.6 4.1 %collective-permute-start.6 = (f32[2,16,128]{2,1,0:T(8,128)S(1)}, f32[2,16,128]{2,1,0:T(8,128)S(1)}, u32[]{:S(2)}, u32[]{:S(2)}) collective-permute-start(f32[2,16,128]{2,1,0:T(8,128)S(1)} %get-tuple-element.44), channel_id=1, source_target_pairs={{0,64},{1,65},{2,66},{3,67},{4,68},{5,69},{6,70},{7,71},{8,72},{9,... | collective-permute-start | bytes 49160 | tf_op jit(solution)/shard_map/ppermute | solution.py:502
  33.3 3.8 %collective-permute-start.7 = (f32[2,16,128]{2,1,0:T(8,128)S(1)}, f32[2,16,128]{2,1,0:T(8,128)S(1)}, u32[]{:S(2)}, u32[]{:S(2)}) collective-permute-start(f32[2,16,128]{2,1,0:T(8,128)S(1)} %get-tuple-element.45), channel_id=1, source_target_pairs={{0,96},{1,97},{2,98},{3,99},{4,100},{5,101},{6,102},{7,103},{8,104... | collective-permute-start | bytes 49160 | tf_op jit(solution)/shard_map/ppermute | solution.py:502
  37.2 3.0 %collective-permute-start.8 = (f32[3,16,128]{2,1,0:T(8,128)S(1)}, f32[3,16,128]{2,1,0:T(8,128)S(1)}, u32[]{:S(2)}, u32[]{:S(2)}) collective-permute-start(f32[3,16,128]{2,1,0:T(8,128)S(1)} %join.1), channel_id=1, source_target_pairs={{0,2},{1,3},{2,0},{3,1},{4,6},{5,7},{6,4},{7,5},{8,10},{9,11},{10,... | collective-permute-start | bytes 73736 | tf_op jit(solution)/shard_map/ppermute | solution.py:502
  40.2 6.7 %collective-permute-start.9 = (f32[3,16,128]{2,1,0:T(8,128)S(1)}, f32[3,16,128]{2,1,0:T(8,128)S(1)}, u32[]{:S(2)}, u32[]{:S(2)}) collective-permute-start(f32[3,16,128]{2,1,0:T(8,128)S(1)} %add.9), channel_id=1, source_target_pairs={{0,4},{1,5},{2,6},{3,7},{4,0},{5,1},{6,2},{7,3},{8,12},{9,13},{10,... | collective-permute-start | bytes 73736 | tf_op jit(solution)/shard_map/ppermute | solution.py:502
  43.6 22.5 %collective-permute-start.3 = (f32[2,16,512]{2,1,0:T(8,128)S(1)}, f32[2,16,512]{2,1,0:T(8,128)S(1)}, u32[]{:S(2)}, u32[]{:S(2)}) collective-permute-start(f32[2,16,512]{2,1,0:T(8,128)S(1)} %get-tuple-element.33), channel_id=1, source_target_pairs={{0,16},{1,17},{2,18},{3,19},{4,20},{5,21},{6,22},{7,23},{8,24},{9,... | collective-permute-start | bytes 196616 | tf_op jit(solution)/shard_map/ppermute | solution.py:502
  46.9 2.8 %collective-permute-start.10 = (f32[3,16,128]{2,1,0:T(8,128)S(1)}, f32[3,16,128]{2,1,0:T(8,128)S(1)}, u32[]{:S(2)}, u32[]{:S(2)}) collective-permute-start(f32[3,16,128]{2,1,0:T(8,128)S(1)} %add.10), channel_id=1, source_target_pairs={{0,1},{1,0},{2,3},{3,2},{4,5},{5,4},{6,7},{7,6},{8,9},{9,8},{10,11... | collective-permute-start | bytes 73736 | tf_op jit(solution)/shard_map/ppermute | solution.py:502
  49.7 17.2 %collective-permute-start.11 = (f32[3,16,128]{2,1,0:T(8,128)S(1)}, f32[3,16,128]{2,1,0:T(8,128)S(1)}, u32[]{:S(2)}, u32[]{:S(2)}) collective-permute-start(f32[3,16,128]{2,1,0:T(8,128)S(1)} %add.11.zero), channel_id=1, source_target_pairs={{0,8},{1,9},{2,10},{3,11},{4,12},{5,13},{6,14},{7,15},{8,0},{9,1},... | collective-permute-start | bytes 73736 | tf_op jit(solution)/shard_map/ppermute | solution.py:502
  50.5 16.3 %collective-permute-start.12 = (f32[3,16,128]{2,1,0:T(8,128)S(1)}, f32[3,16,128]{2,1,0:T(8,128)S(1)}, u32[]{:S(2)}, u32[]{:S(2)}) collective-permute-start(f32[3,16,128]{2,1,0:T(8,128)S(1)} %add.11.zero), channel_id=1, source_target_pairs={{0,16},{1,17},{2,18},{3,19},{4,20},{5,21},{6,22},{7,23},{8,24},{9,... | collective-permute-start | bytes 73736 | tf_op jit(solution)/shard_map/ppermute | solution.py:502
  53.9 13.0 %collective-permute-start.13 = (f32[3,16,128]{2,1,0:T(8,128)S(1)}, f32[3,16,128]{2,1,0:T(8,128)S(1)}, u32[]{:S(2)}, u32[]{:S(2)}) collective-permute-start(f32[3,16,128]{2,1,0:T(8,128)S(1)} %add.11.zero), channel_id=1, source_target_pairs={{0,24},{1,25},{2,26},{3,27},{4,28},{5,29},{6,30},{7,31},{8,16},{9,... | collective-permute-start | bytes 73736 | tf_op jit(solution)/shard_map/ppermute | solution.py:502

commit v3 on v2

v3 whole, which is shorter than its diff:
```python
from functools import partial

import jax
import jax.numpy as jnp
from jax import lax
from jax.experimental import pallas as pl
from jax.experimental.pallas import tpu as pltpu
from jax.sharding import PartitionSpec as P


UMAX = 4
CALLS = 4
F32 = jnp.float32
BF16 = jnp.bfloat16
NT = (((1,), (1,)), ((), ()))
NN = (((1,), (0,)), ((), ()))


def split3(value):
    high = value.astype(BF16)
    rest = value - high.astype(F32)
    middle = rest.astype(BF16)
    low = (rest - middle.astype(F32)).astype(BF16)
    return high, middle, low


def three_rows(value):
    return jnp.concatenate(split3(value), axis=0)


def sum_of_three(value):
    size = value.shape[0] // 3
    return (value[2 * size :] + value[size : 2 * size]) + value[:size]


VMEM = pl.BlockSpec(memory_space=pltpu.VMEM)
ANY = pl.BlockSpec(memory_space=pl.ANY)
HBM = pl.BlockSpec(memory_space=pltpu.HBM)
LIMIT = pltpu.CompilerParams(vmem_limit_bytes=30 << 20)
SMEM = pl.BlockSpec(memory_space=pltpu.SMEM)


def near(value):
    return pltpu.with_memory_space_constraint(value, pltpu.VMEM)


def afar(value):
    return pltpu.with_memory_space_constraint(value, pltpu.HBM)


def scalar(value):
    return pltpu.with_memory_space_constraint(value, pltpu.SMEM)


def sides_of(size_x):
    even = lax.axis_index("wide") % 2 == 0
    return jnp.where(even, size_x - 1, 0), jnp.where(even, 0, size_x - 1)


def run_all(copies):
    for copy in copies:
        copy.start()
    for copy in copies:
        copy.wait()


def is_even():
    return lax.axis_index("narrow") % 2 == 0


def faces_kernel(volume, inner, outer, same, cross, sems):
    channels, size_x, size_y, _ = volume.shape
    same_x, cross_x = sides_of(size_x)

    def narrow_copies(even):
        ends = (size_y - 1, 0) if even else (0, size_y - 1)
        return [
            pltpu.make_async_copy(volume.at[:, :, end], target, sems.at[k])
            for k, (end, target) in enumerate(zip(ends, (inner, outer)))
        ]

    def begin(even):
        for copy in narrow_copies(even):
            copy.start()

    pl.when(is_even())(partial(begin, True))
    pl.when(jnp.logical_not(is_even()))(partial(begin, False))
    run_all(
        [
            pltpu.make_async_copy(volume.at[:, same_x], same, sems.at[2]),
            pltpu.make_async_copy(volume.at[:, cross_x], cross.at[pl.ds(0, channels)], sems.at[3]),
        ]
    )
    for copy in narrow_copies(True):
        copy.wait()


def faces(volume):
    channels, size_x, size_y, size_z = volume.shape
    return pl.pallas_call(
        faces_kernel,
        in_specs=[HBM],
        out_specs=[VMEM] * 4,
        out_shape=[
            pltpu.VMEM((channels, size_x, size_z), F32),
            pltpu.VMEM((channels, size_x, size_z), F32),
            pltpu.VMEM((channels, size_y, size_z), F32),
            pltpu.VMEM((channels + 2, size_y, size_z), F32),
        ],
        scratch_shapes=[pltpu.SemaphoreType.DMA((4,))],
        compiler_params=LIMIT,
        name="faces",
    )(afar(volume))


def front_kernel(
    upsample, counts, volume, cells, rows, density, matrix,
    own, one, two, three, count_out, top, sem,
):
    wide = lax.axis_index("wide")
    top_copy = pltpu.make_async_copy(
        volume.at[:, :, :, pl.ds(volume.shape[3] - 128, 128)], top, sem
    )
    top_copy.start()
    channels, _, _, _ = volume.shape
    slots = cells.shape[1]
    cell_count, row_count = count_out.shape
    live = lax.broadcasted_iota(jnp.int32, (1, slots), 1) < counts[0, 0]
    cell_of = jnp.where(live, cells[...], -1)
    cell_hit = lax.broadcasted_iota(jnp.int32, (cell_count, slots), 0) == cell_of
    row_of = (rows[...] ^ (wide * (row_count // 8))).astype(F32)
    row_of = jnp.broadcast_to(row_of, (8, slots)).T[:, :1]
    row_hit = lax.broadcasted_iota(jnp.int32, (slots, row_count), 1).astype(F32) == row_of
    cell_hit = jnp.where(cell_hit, 1.0, 0.0).astype(BF16)
    row_hit = jnp.where(row_hit, 1.0, 0.0).astype(BF16)
    counted = lax.dot_general(cell_hit, row_hit, NN, preferred_element_type=F32).astype(BF16)
    count_out[...] = counted

    blocks = upsample.shape[0]
    width = density.shape[1] // blocks
    group = matrix.shape[2]
    lane = lax.broadcasted_iota(jnp.int32, (channels, width), 1)
    total = jnp.zeros((channels, 2 * group), F32)
    pairs = []
    for block in range(blocks):
        here = density[:, pl.ds(block * width, width)]
        following = jnp.where(lane == width - 1, here, pltpu.roll(here, width - 1, 1))
        factor = upsample[block]
        inverse = jnp.where(
            factor == 1, 1.0, jnp.where(factor == 2, 0.5, jnp.where(factor == 3, 1.0 / 3.0, 0.25))
        )
        pairs.append((here, following, factor, inverse))
    for level in range(UMAX):
        pieces = []
        for here, following, factor, inverse in pairs:
            share = jnp.where(level < factor, inverse, 0.0)
            blend = level * inverse
            fine = ((1.0 - blend) * share) * here + (blend * share) * following
            pieces.append(fine.astype(BF16))
        both = matrix[:, level].reshape(2 * group, matrix.shape[3])
        total = total + lax.dot_general(
            jnp.concatenate(pieces, axis=1), both, NT, preferred_element_type=F32
        )

    top_copy.wait()
    at = lax.broadcasted_iota(jnp.int32, (cell_count, 128), 1)
    tops = jnp.zeros((cell_count, 128), F32)
    for channel in range(channels):
        value = top[channel].reshape(cell_count, 128)
        tops = jnp.where(at == channel, pltpu.roll(value, (channel + 1) % 128, 1), tops)
    traces = sum_of_three(
        lax.dot_general(
            three_rows(tops.T[:channels]), counted, NN, preferred_element_type=F32
        )
    )

    waves = channels // 2
    turned = pltpu.roll(total, group, 1)
    bem = jnp.concatenate(
        [total[:waves] - turned[waves:], total[waves:] + turned[:waves]], axis=0
    )
    for part, target in enumerate((own, one, two, three)):
        target[0] = bem
        target[1] = traces[:channels, part * 128 : (part + 1) * 128]


def front(upsample, counts, volume, density, matrix, cells, rows):
    channels = density.shape[0]
    message = pltpu.VMEM((2, channels, 128), F32)
    return pl.pallas_call(
        front_kernel,
        in_specs=[SMEM, SMEM, HBM] + [VMEM] * 4,
        out_specs=[VMEM] * 5,
        out_shape=[message] * 4 + [pltpu.VMEM((256, 512), BF16)],
        scratch_shapes=[pltpu.VMEM(volume.shape[:3] + (128,), F32), pltpu.SemaphoreType.DMA],
        compiler_params=LIMIT,
        name="front",
    )(
        scalar(upsample),
        scalar(counts),
        afar(volume),
        near(cells),
        near(rows),
        near(density),
        near(matrix),
    )


def edges_kernel(inner, outer, cross_in, corner, cross, sems):
    channels, size_x, _ = inner.shape
    same_x, cross_x = sides_of(size_x)
    high = jnp.where(is_even(), 1, 0)
    copies = []
    for k, (face, end) in enumerate(((inner, high), (outer, 1 - high))):
        copies.append(
            pltpu.make_async_copy(face.at[:, cross_x], cross.at[channels + end], sems.at[0, k])
        )
        copies.append(pltpu.make_async_copy(face.at[:, same_x], corner.at[end], sems.at[1, k]))
    run_all(copies)


def edges_of(inner, outer, cross):
    channels, _, size_z = inner.shape
    return pl.pallas_call(
        edges_kernel,
        in_specs=[VMEM] * 3,
        out_specs=[VMEM] * 2,
        out_shape=[pltpu.VMEM((2, channels, size_z), F32), pltpu.VMEM(cross.shape, F32)],
        scratch_shapes=[pltpu.SemaphoreType.DMA((2, 2))],
        input_output_aliases={2: 1},
        compiler_params=LIMIT,
        name="edges",
    )(near(inner), near(outer), near(cross))


def join_kernel(own, one, two, three, out):
    group = 64
    lane = lax.broadcasted_iota(jnp.int32, own.shape[1:], 1)
    out[0] = jnp.where(lane < group, own[0], pltpu.roll(one[0], group, 1))
    out[1] = jnp.where(lane < group, two[0], pltpu.roll(three[0], group, 1))
    out[2] = (own[1] + one[1]) + (two[1] + three[1])


def join(own, one, two, three):
    return pl.pallas_call(
        join_kernel,
        in_specs=[VMEM] * 4,
        out_specs=VMEM,
        out_shape=pltpu.VMEM((3,) + own.shape[1:], F32),
        compiler_params=LIMIT,
        name="join",
    )(*[near(value) for value in (own, one, two, three)])


def y_sum(value, before, after):
    half = value.shape[0] // 2
    low, high = value[:half], value[half:]
    at = lax.broadcasted_iota(jnp.int32, low.shape, 0)
    low_down, high_down = pltpu.roll(low, 1, 0), pltpu.roll(high, 1, 0)
    low_up, high_up = pltpu.roll(low, half - 1, 0), pltpu.roll(high, half - 1, 0)
    first, final_row = at == 0, at == half - 1
    low_sum = jnp.where(first, before, low_down) + jnp.where(final_row, high_up, low_up)
    high_sum = jnp.where(first, low_down, high_down) + jnp.where(final_row, after, high_up)
    return jnp.concatenate([low_sum, high_sum], axis=0)


def z_sum(value):
    tiles = value.shape[1] // 128
    pieces = [value[:, 128 * k : 128 * (k + 1)] for k in range(tiles)]
    at = lax.broadcasted_iota(jnp.int32, pieces[0].shape, 1)
    first, final_lane = at == 0, at == 127
    down = [pltpu.roll(piece, 1, 1) for piece in pieces]
    up = [pltpu.roll(piece, 127, 1) for piece in pieces]
    sums = []
    for k in range(tiles):
        below = down[k - 1] if k > 0 else 0.0
        above = up[k + 1] if k < tiles - 1 else 0.0
        sums.append(jnp.where(first, below, down[k]) + jnp.where(final_lane, above, up[k]))
    return jnp.concatenate(sums, axis=1)


PLANES = 4


def inside(ref, first, count):
    size_x, size_z = ref.shape[2], ref.shape[4]
    return ref.at[
        :, pl.ds(first, count), pl.ds(1, size_x - 2), :, pl.ds(0, size_z - 128)
    ]


def interior_kernel(volume, given, inner, outer, *refs, first):
    if first == 0:
        result, scales, sums, mixed = refs
    else:
        previous, _, result, out, sums, mixed, sem = refs
        scales = given
    parts, count, size_x, size_y, size_z = result.shape
    waves = volume.shape[1]
    even = is_even()

    if first == 0:

        def prepare(x, carry):
            scale = given[0, x].astype(F32)
            scales[0, x] = scale * (8.0 / 3.0) - given[1, x].astype(F32)
            scales[1, x] = scale * (1.0 / 6.0)
            scales[2, x] = given[2, x].astype(F32)
            return carry

        lax.fori_loop(0, size_x, prepare, 0)
    else:
        writing = pltpu.make_async_copy(
            inside(previous, 0, count), inside(out, first - count, count), sem
        )
        writing.start()
    nothing = jnp.zeros((size_y, size_z), F32)
    for part in range(parts):
        for x in (0, size_x + 1):
            sums[part, x] = nothing
            mixed[part, x] = nothing

    for step in range(count):
        wave = first + step

        def along(group, carry):
            for x in [group * PLANES + k for k in range(PLANES)]:
                for part in range(parts):
                    value = volume[part, wave, x]
                    channel = part * waves + wave
                    row = pl.ds(x, 1)
                    one, two = inner[channel, row, :], outer[channel, row, :]
                    before, after = jnp.where(even, two, one), jnp.where(even, one, two)
                    total = y_sum(value, before, after)
                    sums[part, x + 1] = total
                    mixed[part, x + 1] = 0.5 * total + value
            return carry

        def across(group, carry):
            for x in [group * PLANES + k for k in range(PLANES)]:
                own = []
                for part in range(parts):
                    level = (mixed[part, x] + mixed[part, x + 2]) + sums[part, x + 1]
                    own.append(z_sum(level) + (sums[part, x] + sums[part, x + 2]))
                real, imag = volume[0, wave, x], volume[1, wave, x]
                diagonal, sixth, absorb = scales[0, x], scales[1, x], scales[2, x]
                result[0, step, x] = (diagonal * real - sixth * own[0]) + absorb * imag
                result[1, step, x] = (diagonal * imag - sixth * own[1]) - absorb * real
            return carry

        lax.fori_loop(0, size_x // PLANES, along, 0)
        lax.fori_loop(0, size_x // PLANES, across, 0)
    if first > 0:
        writing.wait()


def interior(volume, given, inner, outer, first, count, previous=None, out=None):
    parts, _, size_x, size_y, size_z = volume.shape
    operands = [near(value) for value in (volume, given, inner, outer)]
    specs = [VMEM] * 4
    work = pltpu.VMEM((parts, size_x + 2, size_y, size_z), F32)
    results = [pltpu.VMEM((parts, count, size_x, size_y, size_z), F32)]
    result_specs = [VMEM]
    scratch = [work, work]
    aliases = {}
    if first == 0:
        results.append(pltpu.VMEM((3, size_x, size_y, size_z), F32))
        result_specs.append(VMEM)
    else:
        operands.append(near(previous))
        specs.append(VMEM)
        scratch.append(pltpu.SemaphoreType.DMA)
        results.append(jax.ShapeDtypeStruct(volume.shape, F32))
        result_specs.append(HBM)
        if out is not None:
            operands.append(out)
            specs.append(HBM)
            aliases = {5: 1}
    return pl.pallas_call(
        partial(interior_kernel if first == 0 or out is not None else first_write, first=first),
        in_specs=specs,
        out_specs=result_specs,
        out_shape=results,
        scratch_shapes=scratch,
        input_output_aliases=aliases,
        compiler_params=LIMIT,
        name="interior",
    )(*operands)


def first_write(volume, given, inner, outer, previous, *refs, first):
    interior_kernel(volume, given, inner, outer, previous, None, *refs, first=first)


def sides_kernel(scales, same_plane, corner, cross_plane, *refs):
    begun = refs[:CALLS]
    _, out, tiles, planes, sems, sem = refs[CALLS:]
    _, channels, _, size_z = (2,) + same_plane.shape
    waves = channels // 2
    count = waves // CALLS
    size_x = scales.shape[1]
    low = size_z - 128
    places = sides_of(size_x)
    writing = pltpu.make_async_copy(
        inside(begun[-1], 0, count), inside(out, waves - count, count), sem
    )
    writing.start()
    copies = []
    for side, (plane, ends) in enumerate(((same_plane, corner), (cross_plane, cross_plane))):
        place = places[side]
        base = ends.shape[0] - 2
        scale = 0.5 * scales[1, place]
        for channel in range(channels):
            part, wave = divmod(channel, waves)
            value = plane[channel]
            before, after = [ends[base + k, pl.ds(channel, 1), :] for k in range(2)]
            total = y_sum(value, before, after)
            nearby = z_sum(total + (value + value)) + (total + total)
            result = begun[wave // count][part, wave % count, place] - scale * nearby
            planes[side, channel] = result[:, :low]
            tiles[side, channel] = result[:, low:]
            copies.append(
                pltpu.make_async_copy(
                    planes.at[side, channel],
                    out.at[part, wave, place, :, pl.ds(0, low)],
                    sems.at[side, channel],
                )
            )
            copies[-1].start()
    for copy in copies + [writing]:
        copy.wait()


def both_sides(scales, same_plane, corner, cross_plane, begun, out):
    channels, size_y, size_z = same_plane.shape
    return pl.pallas_call(
        sides_kernel,
        in_specs=[VMEM] * (4 + CALLS) + [HBM],
        out_specs=[HBM, VMEM],
        out_shape=[
            jax.ShapeDtypeStruct(out.shape, F32),
            pltpu.VMEM((2, channels, size_y, 128), F32),
        ],
        scratch_shapes=[
            pltpu.VMEM((2, channels, size_y, size_z - 128), F32),
            pltpu.SemaphoreType.DMA((2, channels)),
            pltpu.SemaphoreType.DMA,
        ],
        input_output_aliases={4 + CALLS: 0},
        compiler_params=LIMIT,
        name="sides",
    )(*[near(v) for v in (scales, same_plane, corner, cross_plane, *begun)], out)


def final_kernel(tiles, zero, one, two, three, counted, *refs):
    begun = refs[:CALLS]
    out, boundary, tops, sems = refs[CALLS + 1 :]
    narrow = lax.axis_index("narrow")
    _, waves, size_x, size_y, size_z = out.shape
    channels = 2 * waves
    places = sides_of(size_x)
    last = size_x - 1
    low = size_z - 128
    count = waves // CALLS

    group = 64
    lane = lax.broadcasted_iota(jnp.int32, (channels, 128), 1)
    blocks = []
    for pair in range(2):
        close = zero[pair] + one[pair]
        distant = two[pair] + three[pair]
        blocks.append(jnp.where(lane < group, close, pltpu.roll(distant, group, 1)))
        blocks.append(jnp.where(lane < group, pltpu.roll(close, group, 1), distant))
    rows = three_rows(jnp.concatenate(blocks, axis=1))
    added = sum_of_three(
        lax.dot_general(rows, counted[...], NT, preferred_element_type=F32)
    )
    added = jnp.concatenate([added, jnp.zeros((128 - channels, added.shape[1]), F32)], axis=0).T
    at_top = lax.broadcasted_iota(jnp.int32, added.shape, 1) == 127

    copies = []
    same_low = places[0] == 0
    for channel in range(channels):
        part, wave = divmod(channel, waves)
        lifted = jnp.where(at_top, pltpu.roll(added, 127 - channel, 1), 0.0)
        lifted = lifted.reshape(size_x, size_y, 128)
        inner = begun[wave // count][part, wave % count, pl.ds(1, size_x - 2), :, pl.ds(low, 128)]
        tops[channel, pl.ds(1, size_x - 2)] = inner + lifted[1:last]
        same, cross = tiles[0, channel], tiles[1, channel]
        tops[channel, 0] = jnp.where(same_low, same, cross) + lifted[0]
        tops[channel, last] = jnp.where(same_low, cross, same) + lifted[last]
        copies.append(
            pltpu.make_async_copy(
                tops.at[channel], out.at[part, wave, :, :, pl.ds(low, 128)], sems.at[channel]
            )
        )
        copies[-1].start()

    trace = (zero[2] + one[2]) + pltpu.roll(two[2] + three[2], group, 1)
    mine = pltpu.roll(blocks[0] - 0.25 * trace, (128 - narrow * 4) % 128, 1).T
    boundary[0] = mine[:4, :waves]
    boundary[1] = mine[:4, waves:]
    for copy in copies:
        copy.wait()


def final(tiles, messages, counted, begun, out):
    _, waves, size_x, size_y, _ = out.shape
    close = [near(v) for v in (tiles, *messages, counted, *begun)]
    return pl.pallas_call(
        final_kernel,
        in_specs=[VMEM] * len(close) + [HBM],
        out_specs=[HBM, VMEM],
        out_shape=[
            jax.ShapeDtypeStruct(out.shape, F32),
            jax.ShapeDtypeStruct((2, 4, waves), F32),
        ],
        scratch_shapes=[
            pltpu.VMEM((2 * waves, size_x, size_y, 128), F32),
            pltpu.SemaphoreType.DMA((2 * waves,)),
        ],
        input_output_aliases={len(close): 0},
        compiler_params=LIMIT,
        name="final",
    )(*close, out)


N_WIDE = 8
N_NARROW = 16
AXES = ("wide", "narrow")


def moved(value, rule):
    pairs = []
    for wide in range(N_WIDE):
        for narrow in range(N_NARROW):
            target = rule(wide, narrow)
            if target is not None and 0 <= target[0] < N_WIDE and 0 <= target[1] < N_NARROW:
                pairs.append((wide * N_NARROW + narrow, target[0] * N_NARROW + target[1]))
    return lax.ppermute(value, AXES, pairs)


def along_y(step):
    return lambda w, n: (w ^ (step >> 1), n ^ ((step & 1) * 8))


def on_device(
    volume_field,
    coefficients,
    density,
    boundary_matrix,
    upsample,
    trace_cell,
    trace_row,
    slot_counts,
):
    parts, waves, size_x, size_y, size_z = volume_field.shape
    channels = parts * waves
    volume = volume_field.reshape(channels, size_x, size_y, size_z)

    inner_out, outer_out, same_out, cross_out = faces(volume)
    inner = moved(inner_out, lambda w, n: (w, n ^ 1))
    outer = moved(outer_out, lambda w, n: (w, n + (1 if n % 2 else -1)))
    same_plane = moved(same_out, lambda w, n: (w ^ 1, n))

    own, one, two, three, counted = front(
        upsample,
        slot_counts,
        volume,
        density.reshape(channels, density.shape[2]),
        boundary_matrix,
        trace_cell.reshape(1, -1),
        trace_row.reshape(1, -1),
    )
    got = [
        moved(message, lambda w, n, s=step: (w ^ (2 * s), n))
        for step, message in ((1, one), (2, two), (3, three))
    ]
    corner_out, cross_out = edges_of(inner, outer, cross_out)
    corner = moved(corner_out, lambda w, n: (w ^ 1, n))
    cross_plane = moved(cross_out, lambda w, n: (w + (1 if w % 2 else -1), n))

    count = waves // CALLS
    result, scales = interior(volume_field, coefficients, inner, outer, 0, count)
    results, out = [result], None
    small = join(own, *got)
    for call, step in enumerate((2, 4, 1), 1):
        result, out = interior(
            volume_field, scales, inner, outer, call * count, count, results[-1], out
        )
        results.append(result)
        small = small + moved(small, lambda w, n, s=step: (w, n ^ s))
    messages = [small] + [moved(small, along_y(step)) for step in range(1, 4)]
    out, tiles = both_sides(scales, same_plane, corner, cross_plane, results, out)

    volume_out, boundary = final(tiles, messages, counted, results, out)
    return volume_out, boundary.transpose(0, 2, 1)


def solution(mesh):
    return jax.shard_map(
        on_device,
        mesh=mesh,
        in_specs=(
            P(None, None, "wide", "narrow", None),
            P(None, "wide", "narrow", None),
            P(None, None, "narrow"),
            P(None, None, "wide", "narrow"),
            P("narrow"),
            P("wide", "narrow", None),
            P("wide", "narrow", None),
            P("wide", "narrow"),
        ),
        out_specs=(P(None, None, "wide", "narrow", None), P(None, None, ("wide", "narrow"))),
        check_vma=False,
    )
```

time: 70.2 us -> 65.2 us (0.929)
  Pallas kernels: 23.4 us -> 19.5 us
  waiting for transfers between devices: 13.5 us -> 12.1 us
    pallas_call x8 -> x7, Pallas kernels: 21.4 us -> 17.5 us  [the longest x4 9.58 us: interior(): pl.pallas_call(partial(interior_kernel if first == 0 or out is not None e...]
    ppermute x14, waiting for transfers between devices: 13.5 us -> 12.1 us  [moved(): return lax.ppermute(value, AXES, pairs)]
  transfers between devices with their start and end apart: 14 -> 14, of which waited for: 6 -> 5; matrix products, arithmetic and copies ran while one was open for 0% -> 0% of each run, Pallas kernels for 26% -> 23%
where the time goes in v3:
time: 65.2 us; the launch traced here: 65 us
  starting transfers between devices  31.9 us (49%)
  Pallas kernels  19.5 us (30%)
  waiting for transfers between devices  12.1 us (19%)
  between operations  1.53 us (2%)
    ppermute x14, starting transfers between devices, moved(): return lax.ppermute(value, AXES, pairs)  31.9 us
    ppermute x14, waiting for transfers between devices, moved(): return lax.ppermute(value, AXES, pairs)  12.1 us
    pallas_call x4, Pallas kernels, interior(): pl.pallas_call(partial(interior_kernel if first == 0 or out is not None e...  9.58 us
    pallas_call x1, Pallas kernels, front(): pl.pallas_call(front_kernel, in_specs=[SMEM, SMEM, HBM] + [VMEM] * 4, out...  3.66 us
    pallas_call x1, Pallas kernels, final(): pl.pallas_call(final_kernel, in_specs=[VMEM] * len(close) + [HBM], out_sp...  2.61 us
    pallas_call x1, Pallas kernels, faces(): pl.pallas_call(faces_kernel, in_specs=[HBM], out_specs=[VMEM] * 4, out_sh...  1.77 us
    pallas_call x1, Pallas kernels, both_sides(): pl.pallas_call(sides_kernel, in_specs=[VMEM] * (4 + CALLS) + [HBM], out_s...  1.61 us
  transfers between devices with their start and end apart: 14, of which 5 were waited for; matrix products, arithmetic and copies ran while one was open for 0% of the time, Pallas kernels for 23%

profile of v3, /device:TPU:1, one launch (start us, length us, event | category | flops | bytes accessed | tf_op | source)
XLA Modules:
  0.0 65.0 jit_solution(13245077581208644388)
XLA Ops:
  0.7 1.8 %faces.1 = (f32[16,16,512]{2,1,0:T(8,128)S(1)}, f32[16,16,512]{2,1,0:T(8,128)S(1)}, f32[16,16,512]{2,1,0:T(8,128)S(1)}, f32[18,16,512]{2,1,0:T(8,128)S(1)}) custom-call(f32[16,16,16,512]{3,2,1,0:T(8,128)} %bitcast.5), custom_call_target="tpu_custom_call" | custom-call | tf_op jit(solution)/shard_map/faces/pallas_call | solution.py:100
  2.5 1.4 %collective-permute-start = (f32[16,16,512]{2,1,0:T(8,128)S(1)}, f32[16,16,512]{2,1,0:T(8,128)S(1)}, u32[]{:S(2)}, u32[]{:S(2)}) collective-permute-start(f32[16,16,512]{2,1,0:T(8,128)S(1)} %get-tuple-element.25), channel_id=1, source_target_pairs={{0,1},{1,0},{2,3},{3,2},{4,5},{5,4},{6,7},{7,6},{8,9},{9,8},{10,11... | collective-permute-start | bytes 1572872 | tf_op jit(solution)/shard_map/ppermute | solution.py:540
  3.9 3.8 %collective-permute-start.1 = (f32[16,16,512]{2,1,0:T(8,128)S(1)}, f32[16,16,512]{2,1,0:T(8,128)S(1)}, u32[]{:S(2)}, u32[]{:S(2)}) collective-permute-start(f32[16,16,512]{2,1,0:T(8,128)S(1)} %get-tuple-element.26), channel_id=1, source_target_pairs={{1,2},{2,1},{3,4},{4,3},{5,6},{6,5},{7,8},{8,7},{9,10},{10,9},{11,... | collective-permute-start | bytes 1572872 | tf_op jit(solution)/shard_map/ppermute | solution.py:540
  7.8 7.1 %collective-permute-done.1.outer = f32[16,16,512]{2,1,0:T(8,128)S(1)} collective-permute-done((f32[16,16,512]{2,1,0:T(8,128)S(1)}, f32[16,16,512]{2,1,0:T(8,128)S(1)}, u32[]{:S(2)}, u32[]{:S(2)}) %collective-permute-start.1) | collective-permute-done | bytes 524320 | tf_op jit(solution)/shard_map/ppermute | solution.py:540
  15.8 5.4 %collective-permute-start.2 = (f32[16,16,512]{2,1,0:T(8,128)S(1)}, f32[16,16,512]{2,1,0:T(8,128)S(1)}, u32[]{:S(2)}, u32[]{:S(2)}) collective-permute-start(f32[16,16,512]{2,1,0:T(8,128)S(1)} %get-tuple-element.28), channel_id=1, source_target_pairs={{0,16},{1,17},{2,18},{3,19},{4,20},{5,21},{6,22},{7,23},{8,24},{9,... | collective-permute-start | bytes 1572872 | tf_op jit(solution)/shard_map/ppermute | solution.py:540
  21.8 3.7 %front.1 = (f32[2,16,128]{2,1,0:T(8,128)S(1)}, f32[2,16,128]{2,1,0:T(8,128)S(1)}, f32[2,16,128]{2,1,0:T(8,128)S(1)}, f32[2,16,128]{2,1,0:T(8,128)S(1)}, bf16[256,512]{1,0:T(8,128)(2,1)S(1)}) custom-call(s32[8]{0:T(128)S(1)} %copy-done.5, s32[1,1]{1,0:T(1,128)S(6)} %copy.20.counts, f32[16,16,16,512]{3,2,1,0:T(8,128)} %bitcast.6, s32[1,256]{1,0:T(1,128)S(1)} %bitcast.10, ...), custom_call_target="tpu_custom_call" | custom-call | tf_op jit(solution)/shard_map/front/pallas_call | solution.py:190
  25.5 1.3 %collective-permute-start.5 = (f32[2,16,128]{2,1,0:T(8,128)S(1)}, f32[2,16,128]{2,1,0:T(8,128)S(1)}, u32[]{:S(2)}, u32[]{:S(2)}) collective-permute-start(f32[2,16,128]{2,1,0:T(8,128)S(1)} %get-tuple-element.41), channel_id=1, source_target_pairs={{0,32},{1,33},{2,34},{3,35},{4,36},{5,37},{6,38},{7,39},{8,40},{9,... | collective-permute-start | bytes 49160 | tf_op jit(solution)/shard_map/ppermute | solution.py:540
  26.8 1.7 %collective-permute-start.6 = (f32[2,16,128]{2,1,0:T(8,128)S(1)}, f32[2,16,128]{2,1,0:T(8,128)S(1)}, u32[]{:S(2)}, u32[]{:S(2)}) collective-permute-start(f32[2,16,128]{2,1,0:T(8,128)S(1)} %get-tuple-element.42), channel_id=1, source_target_pairs={{0,64},{1,65},{2,66},{3,67},{4,68},{5,69},{6,70},{7,71},{8,72},{9,... | collective-permute-start | bytes 49160 | tf_op jit(solution)/shard_map/ppermute | solution.py:540
  28.6 0.9 %collective-permute-start.7 = (f32[2,16,128]{2,1,0:T(8,128)S(1)}, f32[2,16,128]{2,1,0:T(8,128)S(1)}, u32[]{:S(2)}, u32[]{:S(2)}) collective-permute-start(f32[2,16,128]{2,1,0:T(8,128)S(1)} %get-tuple-element.43), channel_id=1, source_target_pairs={{0,96},{1,97},{2,98},{3,99},{4,100},{5,101},{6,102},{7,103},{8,104... | collective-permute-start | bytes 49160 | tf_op jit(solution)/shard_map/ppermute | solution.py:540
  29.5 1.4 %collective-permute-done.6.two = f32[2,16,128]{2,1,0:T(8,128)S(1)} collective-permute-done((f32[2,16,128]{2,1,0:T(8,128)S(1)}, f32[2,16,128]{2,1,0:T(8,128)S(1)}, u32[]{:S(2)}, u32[]{:S(2)}) %collective-permute-start.6) | collective-permute-done | bytes 16416 | tf_op jit(solution)/shard_map/ppermute | solution.py:540
  30.9 1.4 %collective-permute-done.7.three = f32[2,16,128]{2,1,0:T(8,128)S(1)} collective-permute-done((f32[2,16,128]{2,1,0:T(8,128)S(1)}, f32[2,16,128]{2,1,0:T(8,128)S(1)}, u32[]{:S(2)}, u32[]{:S(2)}) %collective-permute-start.7) | collective-permute-done | bytes 16416 | tf_op jit(solution)/shard_map/ppermute | solution.py:540
  32.4 3.7 %collective-permute-start.8 = (f32[3,16,128]{2,1,0:T(8,128)S(1)}, f32[3,16,128]{2,1,0:T(8,128)S(1)}, u32[]{:S(2)}, u32[]{:S(2)}) collective-permute-start(f32[3,16,128]{2,1,0:T(8,128)S(1)} %join.1), channel_id=1, source_target_pairs={{0,2},{1,3},{2,0},{3,1},{4,6},{5,7},{6,4},{7,5},{8,10},{9,11},{10,... | collective-permute-start | bytes 73736 | tf_op jit(solution)/shard_map/ppermute | solution.py:540
  36.2 1.2 %collective-permute-done.8 = f32[3,16,128]{2,1,0:T(8,128)S(1)} collective-permute-done((f32[3,16,128]{2,1,0:T(8,128)S(1)}, f32[3,16,128]{2,1,0:T(8,128)S(1)}, u32[]{:S(2)}, u32[]{:S(2)}) %collective-permute-start.8) | collective-permute-done | bytes 24608 | tf_op jit(solution)/shard_map/ppermute | solution.py:540
  37.4 4.5 %collective-permute-start.9 = (f32[3,16,128]{2,1,0:T(8,128)S(1)}, f32[3,16,128]{2,1,0:T(8,128)S(1)}, u32[]{:S(2)}, u32[]{:S(2)}) collective-permute-start(f32[3,16,128]{2,1,0:T(8,128)S(1)} %add.9), channel_id=1, source_target_pairs={{0,4},{1,5},{2,6},{3,7},{4,0},{5,1},{6,2},{7,3},{8,12},{9,13},{10,... | collective-permute-start | bytes 73736 | tf_op jit(solution)/shard_map/ppermute | solution.py:540
  41.8 2.7 %collective-permute-start.3 = (f32[2,16,512]{2,1,0:T(8,128)S(1)}, f32[2,16,512]{2,1,0:T(8,128)S(1)}, u32[]{:S(2)}, u32[]{:S(2)}) collective-permute-start(f32[2,16,512]{2,1,0:T(8,128)S(1)} %get-tuple-element.30), channel_id=1, source_target_pairs={{0,16},{1,17},{2,18},{3,19},{4,20},{5,21},{6,22},{7,23},{8,24},{9,... | collective-permute-start | bytes 196616 | tf_op jit(solution)/shard_map/ppermute | solution.py:540
  44.6 1.8 %collective-permute-start.10 = (f32[3,16,128]{2,1,0:T(8,128)S(1)}, f32[3,16,128]{2,1,0:T(8,128)S(1)}, u32[]{:S(2)}, u32[]{:S(2)}) collective-permute-start(f32[3,16,128]{2,1,0:T(8,128)S(1)} %add.10), channel_id=1, source_target_pairs={{0,1},{1,0},{2,3},{3,2},{4,5},{5,4},{6,7},{7,6},{8,9},{9,8},{10,11... | collective-permute-start | bytes 73736 | tf_op jit(solution)/shard_map/ppermute | solution.py:540
  47.2 1.3 %collective-permute-start.11 = (f32[3,16,128]{2,1,0:T(8,128)S(1)}, f32[3,16,128]{2,1,0:T(8,128)S(1)}, u32[]{:S(2)}, u32[]{:S(2)}) collective-permute-start(f32[3,16,128]{2,1,0:T(8,128)S(1)} %add.11.zero), channel_id=1, source_target_pairs={{0,8},{1,9},{2,10},{3,11},{4,12},{5,13},{6,14},{7,15},{8,0},{9,1},... | collective-permute-start | bytes 73736 | tf_op jit(solution)/shard_map/ppermute | solution.py:540
  48.5 2.5 %collective-permute-start.12 = (f32[3,16,128]{2,1,0:T(8,128)S(1)}, f32[3,16,128]{2,1,0:T(8,128)S(1)}, u32[]{:S(2)}, u32[]{:S(2)}) collective-permute-start(f32[3,16,128]{2,1,0:T(8,128)S(1)} %add.11.zero), channel_id=1, source_target_pairs={{0,16},{1,17},{2,18},{3,19},{4,20},{5,21},{6,22},{7,23},{8,24},{9,... | collective-permute-start | bytes 73736 | tf_op jit(solution)/shard_map/ppermute | solution.py:540
  51.1 2.5 %interior.4 = (f32[2,2,16,16,512]{4,3,2,1,0:T(8,128)S(1)}, f32[3,16,16,512]{3,2,1,0:T(8,128)S(1)}) custom-call(f32[2,8,16,16,512]{4,3,2,1,0:T(8,128)S(1)} %bitcast.8, bf16[3,16,16,512]{3,2,1,0:T(8,128)(2,1)S(1)} %copy-done.1, f32[16,16,512]{2,1,0:T(8,128)S(1)} %collective-permute-done.inner, f32[16,16,512]{2,1,0:T(8,128)S(1)} %collective-permute-done.1.outer), custom_call_target="tpu_custom_call" | custom-call | tf_op jit(solution)/shard_map/interior/pallas_call | solution.py:379
  53.7 2.4 %interior.5 = (f32[2,2,16,16,512]{4,3,2,1,0:T(8,128)S(1)}, f32[2,8,16,16,512]{4,3,2,1,0:T(8,128)}) custom-call(f32[2,8,16,16,512]{4,3,2,1,0:T(8,128)S(1)} %bitcast.8, f32[3,16,16,512]{3,2,1,0:T(8,128)S(1)} %get-tuple-element.27.given.scales, f32[16,16,512]{2,1,0:T(8,128)S(1)} %collective-permute-done.inner, f32[16,16,512]{2,1,0:T(8,128)S(1)} %collective-permute-done.1.outer, ...), custom_call_target="tpu_custom_call" | custom-call | tf_op jit(solution)/shard_map/interior/pallas_call | solution.py:379
  56.0 2.4 %interior.6 = (f32[2,2,16,16,512]{4,3,2,1,0:T(8,128)S(1)}, f32[2,8,16,16,512]{4,3,2,1,0:T(8,128)}) custom-call(f32[2,8,16,16,512]{4,3,2,1,0:T(8,128)S(1)} %bitcast.8, f32[3,16,16,512]{3,2,1,0:T(8,128)S(1)} %get-tuple-element.27.given.scales, f32[16,16,512]{2,1,0:T(8,128)S(1)} %collective-permute-done.inner, ...), custom_call_target="tpu_custom_call", output_to_operand_aliasing={{1}: (5, {})} | custom-call | tf_op jit(solution)/shard_map/interior/pallas_call | solution.py:379
  58.4 2.4 %interior.7 = (f32[2,2,16,16,512]{4,3,2,1,0:T(8,128)S(1)}, f32[2,8,16,16,512]{4,3,2,1,0:T(8,128)}) custom-call(f32[2,8,16,16,512]{4,3,2,1,0:T(8,128)S(1)} %bitcast.8, f32[3,16,16,512]{3,2,1,0:T(8,128)S(1)} %get-tuple-element.27.given.scales, f32[16,16,512]{2,1,0:T(8,128)S(1)} %collective-permute-done.inner, ...), custom_call_target="tpu_custom_call", output_to_operand_aliasing={{1}: (5, {})} | custom-call | tf_op jit(solution)/shard_map/interior/pallas_call | solution.py:379
  60.8 1.6 %sides.1 = (f32[2,8,16,16,512]{4,3,2,1,0:T(8,128)}, f32[2,16,16,128]{3,2,1,0:T(8,128)S(1)}) custom-call(f32[3,16,16,512]{3,2,1,0:T(8,128)S(1)} %get-tuple-element.27.given.scales, f32[16,16,512]{2,1,0:T(8,128)S(1)} %collective-permute-done.2.same_plane, f32[2,16,512]{2,1,0:T(8,128)S(1)} %collective-permute-done.3.corner, ...), custom_call_target="tpu_custom_call", output_to_operand_aliasing={{0}: (8, {})} | custom-call | tf_op jit(solution)/shard_map/sides/pallas_call | solution.py:436
  62.4 2.6 %final.1 = (f32[2,8,16,16,512]{4,3,2,1,0:T(8,128)}, f32[2,4,8]{2,1,0:T(4,128)}) custom-call(f32[2,16,16,128]{3,2,1,0:T(8,128)S(1)} %get-tuple-element.39.tiles, f32[3,16,128]{2,1,0:T(8,128)S(1)} %add.11.zero, f32[3,16,128]{2,1,0:T(8,128)S(1)} %collective-permute-done.11.one, ...), custom_call_target="tpu_custom_call", output_to_operand_aliasing={{0}: (10, {})} | custom-call | tf_op jit(solution)/shard_map/final/pallas_call | solution.py:510
  (34 shorter events, 1.9 us)
Async XLA Ops:
  0.6 21.2 %copy-start.3 = (s32[1,1,256]{2,1,0:T(1,128)S(1)}, s32[1,1,256]{2,1,0:T(1,128)}, u32[]{:S(2)}) copy-start(s32[1,1,256]{2,1,0:T(1,128)} %param.13) | copy-start | bytes 3076
  0.6 21.2 %copy-start.4 = (s32[1,1,256]{2,1,0:T(1,128)S(1)}, s32[1,1,256]{2,1,0:T(1,128)}, u32[]{:S(2)}) copy-start(s32[1,1,256]{2,1,0:T(1,128)} %param.14) | copy-start | bytes 3076
  0.7 21.2 %copy-start.2 = (f32[2,8,4096]{2,1,0:T(8,128)S(1)}, f32[2,8,4096]{2,1,0:T(8,128)}, u32[]{:S(2)}) copy-start(f32[2,8,4096]{2,1,0:T(8,128)} %param.10) | copy-start | bytes 786436
  0.7 21.2 %copy-start = (bf16[2,4,64,4096]{3,2,1,0:T(8,128)(2,1)S(1)}, bf16[2,4,64,4096]{3,2,1,0:T(8,128)(2,1)}, u32[]{:S(2)}) copy-start(bf16[2,4,64,4096]{3,2,1,0:T(8,128)(2,1)} %matrix.1) | copy-start | bytes 12582916
  0.7 21.2 %copy-start.5 = (s32[8]{0:T(128)S(1)}, s32[8]{0:T(128)}, u32[]{:S(2)}) copy-start(s32[8]{0:T(128)} %upsample.1) | copy-start | bytes 100
  0.7 50.4 %slice-start = ((s8[8388608]{0:T(1024)(128)(4,1)}), s8[4194304]{0:T(1024)(128)(4,1)S(1)}, s32[]{:S(2)}) async-start(s8[8388608]{0:T(1024)(128)(4,1)} %bitcast.7), calls=%async_computation | async-start | bytes 8388608
  2.5 48.6 %copy-start.1 = (bf16[3,16,16,512]{3,2,1,0:T(8,128)(2,1)S(1)}, bf16[3,16,16,512]{3,2,1,0:T(8,128)(2,1)}, u32[]{:S(2)}) copy-start(bf16[3,16,16,512]{3,2,1,0:T(8,128)(2,1)} %given.1) | copy-start | bytes 2359300
  2.5 5.3 %collective-permute-start = (f32[16,16,512]{2,1,0:T(8,128)S(1)}, f32[16,16,512]{2,1,0:T(8,128)S(1)}, u32[]{:S(2)}, u32[]{:S(2)}) collective-permute-start(f32[16,16,512]{2,1,0:T(8,128)S(1)} %get-tuple-element.25), channel_id=1, source_target_pairs={{0,1},{1,0},{2,3},{3,2},{4,5},{5,4},{6,7},{7,6},{8,9},{9,8},{10,11... | collective-permute-start | bytes 1572872 | tf_op jit(solution)/shard_map/ppermute | solution.py:540
  3.9 11.0 %collective-permute-start.1 = (f32[16,16,512]{2,1,0:T(8,128)S(1)}, f32[16,16,512]{2,1,0:T(8,128)S(1)}, u32[]{:S(2)}, u32[]{:S(2)}) collective-permute-start(f32[16,16,512]{2,1,0:T(8,128)S(1)} %get-tuple-element.26), channel_id=1, source_target_pairs={{1,2},{2,1},{3,4},{4,3},{5,6},{6,5},{7,8},{8,7},{9,10},{10,9},{11,... | collective-permute-start | bytes 1572872 | tf_op jit(solution)/shard_map/ppermute | solution.py:540
  15.1 45.7 %collective-permute-start.4 = (f32[18,16,512]{2,1,0:T(8,128)S(1)}, f32[18,16,512]{2,1,0:T(8,128)S(1)}, u32[]{:S(2)}, u32[]{:S(2)}) collective-permute-start(f32[18,16,512]{2,1,0:T(8,128)S(1)} %get-tuple-element.31), channel_id=1, source_target_pairs={{16,32},{17,33},{18,34},{19,35},{20,36},{21,37},{22,38},{23,39},{2... | collective-permute-start | bytes 1769480 | tf_op jit(solution)/shard_map/ppermute | solution.py:540
  15.8 35.3 %collective-permute-start.2 = (f32[16,16,512]{2,1,0:T(8,128)S(1)}, f32[16,16,512]{2,1,0:T(8,128)S(1)}, u32[]{:S(2)}, u32[]{:S(2)}) collective-permute-start(f32[16,16,512]{2,1,0:T(8,128)S(1)} %get-tuple-element.28), channel_id=1, source_target_pairs={{0,16},{1,17},{2,18},{3,19},{4,20},{5,21},{6,22},{7,23},{8,24},{9,... | collective-permute-start | bytes 1572872 | tf_op jit(solution)/shard_map/ppermute | solution.py:540
  21.8 29.3 %slice-start.1 = ((s8[8388608]{0:T(1024)(128)(4,1)}), s8[4194304]{0:T(1024)(128)(4,1)S(1)}, s32[]{:S(2)}) async-start(s8[8388608]{0:T(1024)(128)(4,1)} %bitcast.7), calls=%async_computation.1 | async-start | bytes 8388608
  25.5 3.9 %collective-permute-start.5 = (f32[2,16,128]{2,1,0:T(8,128)S(1)}, f32[2,16,128]{2,1,0:T(8,128)S(1)}, u32[]{:S(2)}, u32[]{:S(2)}) collective-permute-start(f32[2,16,128]{2,1,0:T(8,128)S(1)} %get-tuple-element.41), channel_id=1, source_target_pairs={{0,32},{1,33},{2,34},{3,35},{4,36},{5,37},{6,38},{7,39},{8,40},{9,... | collective-permute-start | bytes 49160 | tf_op jit(solution)/shard_map/ppermute | solution.py:540
  26.8 4.1 %collective-permute-start.6 = (f32[2,16,128]{2,1,0:T(8,128)S(1)}, f32[2,16,128]{2,1,0:T(8,128)S(1)}, u32[]{:S(2)}, u32[]{:S(2)}) collective-permute-start(f32[2,16,128]{2,1,0:T(8,128)S(1)} %get-tuple-element.42), channel_id=1, source_target_pairs={{0,64},{1,65},{2,66},{3,67},{4,68},{5,69},{6,70},{7,71},{8,72},{9,... | collective-permute-start | bytes 49160 | tf_op jit(solution)/shard_map/ppermute | solution.py:540
  28.6 3.8 %collective-permute-start.7 = (f32[2,16,128]{2,1,0:T(8,128)S(1)}, f32[2,16,128]{2,1,0:T(8,128)S(1)}, u32[]{:S(2)}, u32[]{:S(2)}) collective-permute-start(f32[2,16,128]{2,1,0:T(8,128)S(1)} %get-tuple-element.43), channel_id=1, source_target_pairs={{0,96},{1,97},{2,98},{3,99},{4,100},{5,101},{6,102},{7,103},{8,104... | collective-permute-start | bytes 49160 | tf_op jit(solution)/shard_map/ppermute | solution.py:540
  32.4 5.0 %collective-permute-start.8 = (f32[3,16,128]{2,1,0:T(8,128)S(1)}, f32[3,16,128]{2,1,0:T(8,128)S(1)}, u32[]{:S(2)}, u32[]{:S(2)}) collective-permute-start(f32[3,16,128]{2,1,0:T(8,128)S(1)} %join.1), channel_id=1, source_target_pairs={{0,2},{1,3},{2,0},{3,1},{4,6},{5,7},{6,4},{7,5},{8,10},{9,11},{10,... | collective-permute-start | bytes 73736 | tf_op jit(solution)/shard_map/ppermute | solution.py:540
  37.4 7.2 %collective-permute-start.9 = (f32[3,16,128]{2,1,0:T(8,128)S(1)}, f32[3,16,128]{2,1,0:T(8,128)S(1)}, u32[]{:S(2)}, u32[]{:S(2)}) collective-permute-start(f32[3,16,128]{2,1,0:T(8,128)S(1)} %add.9), channel_id=1, source_target_pairs={{0,4},{1,5},{2,6},{3,7},{4,0},{5,1},{6,2},{7,3},{8,12},{9,13},{10,... | collective-permute-start | bytes 73736 | tf_op jit(solution)/shard_map/ppermute | solution.py:540
  41.8 18.9 %collective-permute-start.3 = (f32[2,16,512]{2,1,0:T(8,128)S(1)}, f32[2,16,512]{2,1,0:T(8,128)S(1)}, u32[]{:S(2)}, u32[]{:S(2)}) collective-permute-start(f32[2,16,512]{2,1,0:T(8,128)S(1)} %get-tuple-element.30), channel_id=1, source_target_pairs={{0,16},{1,17},{2,18},{3,19},{4,20},{5,21},{6,22},{7,23},{8,24},{9,... | collective-permute-start | bytes 196616 | tf_op jit(solution)/shard_map/ppermute | solution.py:540
  44.6 2.7 %collective-permute-start.10 = (f32[3,16,128]{2,1,0:T(8,128)S(1)}, f32[3,16,128]{2,1,0:T(8,128)S(1)}, u32[]{:S(2)}, u32[]{:S(2)}) collective-permute-start(f32[3,16,128]{2,1,0:T(8,128)S(1)} %add.10), channel_id=1, source_target_pairs={{0,1},{1,0},{2,3},{3,2},{4,5},{5,4},{6,7},{7,6},{8,9},{9,8},{10,11... | collective-permute-start | bytes 73736 | tf_op jit(solution)/shard_map/ppermute | solution.py:540
  47.2 15.1 %collective-permute-start.11 = (f32[3,16,128]{2,1,0:T(8,128)S(1)}, f32[3,16,128]{2,1,0:T(8,128)S(1)}, u32[]{:S(2)}, u32[]{:S(2)}) collective-permute-start(f32[3,16,128]{2,1,0:T(8,128)S(1)} %add.11.zero), channel_id=1, source_target_pairs={{0,8},{1,9},{2,10},{3,11},{4,12},{5,13},{6,14},{7,15},{8,0},{9,1},... | collective-permute-start | bytes 73736 | tf_op jit(solution)/shard_map/ppermute | solution.py:540
  48.5 13.8 %collective-permute-start.12 = (f32[3,16,128]{2,1,0:T(8,128)S(1)}, f32[3,16,128]{2,1,0:T(8,128)S(1)}, u32[]{:S(2)}, u32[]{:S(2)}) collective-permute-start(f32[3,16,128]{2,1,0:T(8,128)S(1)} %add.11.zero), channel_id=1, source_target_pairs={{0,16},{1,17},{2,18},{3,19},{4,20},{5,21},{6,22},{7,23},{8,24},{9,... | collective-permute-start | bytes 73736 | tf_op jit(solution)/shard_map/ppermute | solution.py:540
  51.0 11.4 %collective-permute-start.13 = (f32[3,16,128]{2,1,0:T(8,128)S(1)}, f32[3,16,128]{2,1,0:T(8,128)S(1)}, u32[]{:S(2)}, u32[]{:S(2)}) collective-permute-start(f32[3,16,128]{2,1,0:T(8,128)S(1)} %add.11.zero), channel_id=1, source_target_pairs={{0,24},{1,25},{2,26},{3,27},{4,28},{5,29},{6,30},{7,31},{8,16},{9,... | collective-permute-start | bytes 73736 | tf_op jit(solution)/shard_map/ppermute | solution.py:540

commit v4 on v3

--- a/solution.py
+++ b/solution.py
@@ -9,7 +9,6 @@
 
 
 UMAX = 4
-CALLS = 4
 F32 = jnp.float32
 BF16 = jnp.bfloat16
 NT = (((1,), (1,)), ((), ()))
@@ -34,10 +33,9 @@
 
 
 VMEM = pl.BlockSpec(memory_space=pltpu.VMEM)
-ANY = pl.BlockSpec(memory_space=pl.ANY)
+SMEM = pl.BlockSpec(memory_space=pltpu.SMEM)
 HBM = pl.BlockSpec(memory_space=pltpu.HBM)
-LIMIT = pltpu.CompilerParams(vmem_limit_bytes=30 << 20)
-SMEM = pl.BlockSpec(memory_space=pltpu.SMEM)
+LIMIT = pltpu.CompilerParams(vmem_limit_bytes=12 << 20)
 
 
 def near(value):
@@ -46,10 +44,6 @@
 
 def afar(value):
     return pltpu.with_memory_space_constraint(value, pltpu.HBM)
-
-
-def scalar(value):
-    return pltpu.with_memory_space_constraint(value, pltpu.SMEM)
 
 
 def sides_of(size_x):
@@ -123,6 +117,35 @@
     )
     top_copy.start()
     channels, _, _, _ = volume.shape
+    blocks = upsample.shape[1]
+    width = density.shape[1] // blocks
+    group = matrix.shape[2]
+    lane = lax.broadcasted_iota(jnp.int32, (channels, width), 1)
+    total = jnp.zeros((channels, 2 * group), F32)
+    factors = upsample[...]
+    inverses = jnp.where(
+        factors == 1, 1.0, jnp.where(factors == 2, 0.5, jnp.where(factors == 3, 1.0 / 3.0, 0.25))
+    )
+    pairs = []
+    for block in range(blocks):
+        here = density[:, pl.ds(block * width, width)]
+        pairs.append(
+            (here, jnp.where(lane == width - 1, here, pltpu.roll(here, width - 1, 1)))
+        )
+    for level in range(UMAX):
+        shares = jnp.where(level < factors, inverses, 0.0)
+        blends = level * inverses
+        nears, fars = (1.0 - blends) * shares, blends * shares
+        pieces = []
+        for block, (here, following) in enumerate(pairs):
+            at = slice(block, block + 1)
+            fine = nears[:, at] * here + fars[:, at] * following
+            pieces.append(fine.astype(BF16))
+        both = matrix[:, level].reshape(2 * group, matrix.shape[3])
+        total = total + lax.dot_general(
+            jnp.concatenate(pieces, axis=1), both, NT, preferred_element_type=F32
+        )
+
     slots = cells.shape[1]
     cell_count, row_count = count_out.shape
     live = lax.broadcasted_iota(jnp.int32, (1, slots), 1) < counts[0, 0]
@@ -136,32 +159,6 @@
     counted = lax.dot_general(cell_hit, row_hit, NN, preferred_element_type=F32).astype(BF16)
     count_out[...] = counted
 
-    blocks = upsample.shape[0]
-    width = density.shape[1] // blocks
-    group = matrix.shape[2]
-    lane = lax.broadcasted_iota(jnp.int32, (channels, width), 1)
-    total = jnp.zeros((channels, 2 * group), F32)
-    pairs = []
-    for block in range(blocks):
-        here = density[:, pl.ds(block * width, width)]
-        following = jnp.where(lane == width - 1, here, pltpu.roll(here, width - 1, 1))
-        factor = upsample[block]
-        inverse = jnp.where(
-            factor == 1, 1.0, jnp.where(factor == 2, 0.5, jnp.where(factor == 3, 1.0 / 3.0, 0.25))
-        )
-        pairs.append((here, following, factor, inverse))
-    for level in range(UMAX):
-        pieces = []
-        for here, following, factor, inverse in pairs:
-            share = jnp.where(level < factor, inverse, 0.0)
-            blend = level * inverse
-            fine = ((1.0 - blend) * share) * here + (blend * share) * following
-            pieces.append(fine.astype(BF16))
-        both = matrix[:, level].reshape(2 * group, matrix.shape[3])
-        total = total + lax.dot_general(
-            jnp.concatenate(pieces, axis=1), both, NT, preferred_element_type=F32
-        )
-
     top_copy.wait()
     at = lax.broadcasted_iota(jnp.int32, (cell_count, 128), 1)
     tops = jnp.zeros((cell_count, 128), F32)
@@ -189,15 +186,18 @@
     message = pltpu.VMEM((2, channels, 128), F32)
     return pl.pallas_call(
         front_kernel,
-        in_specs=[SMEM, SMEM, HBM] + [VMEM] * 4,
+        in_specs=[VMEM, SMEM, HBM] + [VMEM] * 4,
         out_specs=[VMEM] * 5,
         out_shape=[message] * 4 + [pltpu.VMEM((256, 512), BF16)],
-        scratch_shapes=[pltpu.VMEM(volume.shape[:3] + (128,), F32), pltpu.SemaphoreType.DMA],
+        scratch_shapes=[
+            pltpu.VMEM(volume.shape[:3] + (128,), F32),
+            pltpu.SemaphoreType.DMA,
+        ],
         compiler_params=LIMIT,
         name="front",
     )(
-        scalar(upsample),
-        scalar(counts),
+        near(upsample),
+        counts,
         afar(volume),
         near(cells),
         near(rows),
@@ -282,47 +282,32 @@
 PLANES = 4
 
 
-def inside(ref, first, count):
+def inside(ref, wave):
     size_x, size_z = ref.shape[2], ref.shape[4]
-    return ref.at[
-        :, pl.ds(first, count), pl.ds(1, size_x - 2), :, pl.ds(0, size_z - 128)
-    ]
-
-
-def interior_kernel(volume, given, inner, outer, *refs, first):
-    if first == 0:
-        result, scales, sums, mixed = refs
-    else:
-        previous, _, result, out, sums, mixed, sem = refs
-        scales = given
-    parts, count, size_x, size_y, size_z = result.shape
-    waves = volume.shape[1]
+    return ref.at[:, wave, pl.ds(1, size_x - 2), :, pl.ds(0, size_z - 128)]
+
+
+def interior_kernel(
+    volume, coefficients, inner, outer, result, scales, out, sums, mixed, sems
+):
+    parts, waves, size_x, size_y, size_z = result.shape
     even = is_even()
 
-    if first == 0:
-
-        def prepare(x, carry):
-            scale = given[0, x].astype(F32)
-            scales[0, x] = scale * (8.0 / 3.0) - given[1, x].astype(F32)
-            scales[1, x] = scale * (1.0 / 6.0)
-            scales[2, x] = given[2, x].astype(F32)
-            return carry
-
-        lax.fori_loop(0, size_x, prepare, 0)
-    else:
-        writing = pltpu.make_async_copy(
-            inside(previous, 0, count), inside(out, first - count, count), sem
-        )
-        writing.start()
+    def prepare(x, carry):
+        scale = coefficients[0, x].astype(F32)
+        scales[0, x] = scale * (8.0 / 3.0) - coefficients[1, x].astype(F32)
+        scales[1, x] = scale * (1.0 / 6.0)
+        scales[2, x] = coefficients[2, x].astype(F32)
+        return carry
+
+    lax.fori_loop(0, size_x, prepare, 0)
     nothing = jnp.zeros((size_y, size_z), F32)
     for part in range(parts):
         for x in (0, size_x + 1):
             sums[part, x] = nothing
             mixed[part, x] = nothing
 
-    for step in range(count):
-        wave = first + step
-
+    def one_wave(wave, done):
         def along(group, carry):
             for x in [group * PLANES + k for k in range(PLANES)]:
                 for part in range(parts):
@@ -344,66 +329,51 @@
                     own.append(z_sum(level) + (sums[part, x] + sums[part, x + 2]))
                 real, imag = volume[0, wave, x], volume[1, wave, x]
                 diagonal, sixth, absorb = scales[0, x], scales[1, x], scales[2, x]
-                result[0, step, x] = (diagonal * real - sixth * own[0]) + absorb * imag
-                result[1, step, x] = (diagonal * imag - sixth * own[1]) - absorb * real
+                result[0, wave, x] = (diagonal * real - sixth * own[0]) + absorb * imag
+                result[1, wave, x] = (diagonal * imag - sixth * own[1]) - absorb * real
             return carry
 
         lax.fori_loop(0, size_x // PLANES, along, 0)
         lax.fori_loop(0, size_x // PLANES, across, 0)
-    if first > 0:
-        writing.wait()
-
-
-def interior(volume, given, inner, outer, first, count, previous=None, out=None):
-    parts, _, size_x, size_y, size_z = volume.shape
-    operands = [near(value) for value in (volume, given, inner, outer)]
-    specs = [VMEM] * 4
+
+        @pl.when(wave < waves - 1)
+        def _():
+            pltpu.make_async_copy(inside(result, wave), inside(out, wave), sems.at[wave]).start()
+
+        return done
+
+    lax.fori_loop(0, waves, one_wave, 0)
+    for wave in range(waves - 1):
+        pltpu.make_async_copy(inside(result, wave), inside(out, wave), sems.at[wave]).wait()
+
+
+def interior(volume, coefficients, inner, outer):
+    parts, waves, size_x, size_y, size_z = volume.shape
     work = pltpu.VMEM((parts, size_x + 2, size_y, size_z), F32)
-    results = [pltpu.VMEM((parts, count, size_x, size_y, size_z), F32)]
-    result_specs = [VMEM]
-    scratch = [work, work]
-    aliases = {}
-    if first == 0:
-        results.append(pltpu.VMEM((3, size_x, size_y, size_z), F32))
-        result_specs.append(VMEM)
-    else:
-        operands.append(near(previous))
-        specs.append(VMEM)
-        scratch.append(pltpu.SemaphoreType.DMA)
-        results.append(jax.ShapeDtypeStruct(volume.shape, F32))
-        result_specs.append(HBM)
-        if out is not None:
-            operands.append(out)
-            specs.append(HBM)
-            aliases = {5: 1}
-    return pl.pallas_call(
-        partial(interior_kernel if first == 0 or out is not None else first_write, first=first),
-        in_specs=specs,
-        out_specs=result_specs,
-        out_shape=results,
-        scratch_shapes=scratch,
-        input_output_aliases=aliases,
+    return pl.pallas_call(
+        interior_kernel,
+        in_specs=[VMEM] * 4,
+        out_specs=[VMEM, VMEM, HBM],
+        out_shape=[
+            pltpu.VMEM(volume.shape, F32),
+            pltpu.VMEM((3, size_x, size_y, size_z), F32),
+            jax.ShapeDtypeStruct(volume.shape, F32),
+        ],
+        scratch_shapes=[work, work, pltpu.SemaphoreType.DMA((waves,))],
         compiler_params=LIMIT,
         name="interior",
-    )(*operands)
-
-
-def first_write(volume, given, inner, outer, previous, *refs, first):
-    interior_kernel(volume, given, inner, outer, previous, None, *refs, first=first)
-
-
-def sides_kernel(scales, same_plane, corner, cross_plane, *refs):
-    begun = refs[:CALLS]
-    _, out, tiles, planes, sems, sem = refs[CALLS:]
-    _, channels, _, size_z = (2,) + same_plane.shape
+    )(*[near(value) for value in (volume, coefficients, inner, outer)])
+
+
+def sides_kernel(
+    scales, same_plane, corner, cross_plane, begun, _, out, tiles, planes, sems, sem
+):
+    channels, _, size_z = same_plane.shape
     waves = channels // 2
-    count = waves // CALLS
     size_x = scales.shape[1]
     low = size_z - 128
     places = sides_of(size_x)
-    writing = pltpu.make_async_copy(
-        inside(begun[-1], 0, count), inside(out, waves - count, count), sem
-    )
+    writing = pltpu.make_async_copy(inside(begun, waves - 1), inside(out, waves - 1), sem)
     writing.start()
     copies = []
     for side, (plane, ends) in enumerate(((same_plane, corner), (cross_plane, cross_plane))):
@@ -416,7 +386,7 @@
             before, after = [ends[base + k, pl.ds(channel, 1), :] for k in range(2)]
             total = y_sum(value, before, after)
             nearby = z_sum(total + (value + value)) + (total + total)
-            result = begun[wave // count][part, wave % count, place] - scale * nearby
+            result = begun[part, wave, place] - scale * nearby
             planes[side, channel] = result[:, :low]
             tiles[side, channel] = result[:, low:]
             copies.append(
@@ -435,7 +405,7 @@
     channels, size_y, size_z = same_plane.shape
     return pl.pallas_call(
         sides_kernel,
-        in_specs=[VMEM] * (4 + CALLS) + [HBM],
+        in_specs=[VMEM] * 5 + [HBM],
         out_specs=[HBM, VMEM],
         out_shape=[
             jax.ShapeDtypeStruct(out.shape, F32),
@@ -446,22 +416,21 @@
             pltpu.SemaphoreType.DMA((2, channels)),
             pltpu.SemaphoreType.DMA,
         ],
-        input_output_aliases={4 + CALLS: 0},
+        input_output_aliases={5: 0},
         compiler_params=LIMIT,
         name="sides",
-    )(*[near(v) for v in (scales, same_plane, corner, cross_plane, *begun)], out)
-
-
-def final_kernel(tiles, zero, one, two, three, counted, *refs):
-    begun = refs[:CALLS]
-    out, boundary, tops, sems = refs[CALLS + 1 :]
+    )(*[near(v) for v in (scales, same_plane, corner, cross_plane, begun)], out)
+
+
+def final_kernel(
+    tiles, zero, one, two, three, counted, begun, _, out, boundary, tops, sems
+):
     narrow = lax.axis_index("narrow")
     _, waves, size_x, size_y, size_z = out.shape
     channels = 2 * waves
     places = sides_of(size_x)
     last = size_x - 1
     low = size_z - 128
-    count = waves // CALLS
 
     group = 64
     lane = lax.broadcasted_iota(jnp.int32, (channels, 128), 1)
@@ -484,7 +453,7 @@
         part, wave = divmod(channel, waves)
         lifted = jnp.where(at_top, pltpu.roll(added, 127 - channel, 1), 0.0)
         lifted = lifted.reshape(size_x, size_y, 128)
-        inner = begun[wave // count][part, wave % count, pl.ds(1, size_x - 2), :, pl.ds(low, 128)]
+        inner = begun[part, wave, pl.ds(1, size_x - 2), :, pl.ds(low, 128)]
         tops[channel, pl.ds(1, size_x - 2)] = inner + lifted[1:last]
         same, cross = tiles[0, channel], tiles[1, channel]
         tops[channel, 0] = jnp.where(same_low, same, cross) + lifted[0]
@@ -506,7 +475,7 @@
 
 def final(tiles, messages, counted, begun, out):
     _, waves, size_x, size_y, _ = out.shape
-    close = [near(v) for v in (tiles, *messages, counted, *begun)]
+    close = [near(v) for v in (tiles, *messages, counted, begun)]
     return pl.pallas_call(
         final_kernel,
         in_specs=[VMEM] * len(close) + [HBM],
@@ -564,7 +533,7 @@
     same_plane = moved(same_out, lambda w, n: (w ^ 1, n))
 
     own, one, two, three, counted = front(
-        upsample,
+        upsample.reshape(1, -1),
         slot_counts,
         volume,
         density.reshape(channels, density.shape[2]),
@@ -576,24 +545,17 @@
         moved(message, lambda w, n, s=step: (w ^ (2 * s), n))
         for step, message in ((1, one), (2, two), (3, three))
     ]
+    small = join(own, *got)
+    for step in (2, 4, 1):
+        small = small + moved(small, lambda w, n, s=step: (w, n ^ s))
     corner_out, cross_out = edges_of(inner, outer, cross_out)
     corner = moved(corner_out, lambda w, n: (w ^ 1, n))
     cross_plane = moved(cross_out, lambda w, n: (w + (1 if w % 2 else -1), n))
-
-    count = waves // CALLS
-    result, scales = interior(volume_field, coefficients, inner, outer, 0, count)
-    results, out = [result], None
-    small = join(own, *got)
-    for call, step in enumerate((2, 4, 1), 1):
-        result, out = interior(
-            volume_field, scales, inner, outer, call * count, count, results[-1], out
-        )
-        results.append(result)
-        small = small + moved(small, lambda w, n, s=step: (w, n ^ s))
+    result, scales, out = interior(volume_field, coefficients, inner, outer)
     messages = [small] + [moved(small, along_y(step)) for step in range(1, 4)]
-    out, tiles = both_sides(scales, same_plane, corner, cross_plane, results, out)
-
-    volume_out, boundary = final(tiles, messages, counted, results, out)
+    out, tiles = both_sides(scales, same_plane, corner, cross_plane, result, out)
+
+    volume_out, boundary = final(tiles, messages, counted, result, out)
     return volume_out, boundary.transpose(0, 2, 1)
 
 

time: 65.2 us -> 65.2 us (level)
  Pallas kernels: 19.5 us -> 18.6 us
  starting transfers between devices: 31.9 us -> 32.8 us
    ppermute x14, starting transfers between devices: 31.9 us -> 32.8 us  [moved(): return lax.ppermute(value, AXES, pairs)]
    pallas_call x6 -> x3, Pallas kernels: 14.9 us -> 14 us  [the longest x1 9.75 us: interior(): pl.pallas_call(interior_kernel, in_specs=[VMEM] * 4, out_specs=[VMEM, VME...]
  transfers between devices with their start and end apart: 14 -> 14, of which waited for: 5 -> 6; matrix products, arithmetic and copies ran while one was open for 0% -> 0% of each run, Pallas kernels for 23% -> 22%
where the time goes in v4:
time: 65.2 us; the launch traced here: 65.1 us
  starting transfers between devices  32.8 us (50%)
  Pallas kernels  18.6 us (29%)
  waiting for transfers between devices  12.1 us (19%)
  between operations  1.51 us (2%)
    ppermute x14, starting transfers between devices, moved(): return lax.ppermute(value, AXES, pairs)  32.8 us
    ppermute x14, waiting for transfers between devices, moved(): return lax.ppermute(value, AXES, pairs)  12.1 us
    pallas_call x1, Pallas kernels, interior(): pl.pallas_call(interior_kernel, in_specs=[VMEM] * 4, out_specs=[VMEM, VME...  9.75 us
    pallas_call x1, Pallas kernels, front(): pl.pallas_call(front_kernel, in_specs=[VMEM, SMEM, HBM] + [VMEM] * 4, out...  2.72 us
    pallas_call x1, Pallas kernels, final(): pl.pallas_call(final_kernel, in_specs=[VMEM] * len(close) + [HBM], out_sp...  2.61 us
    pallas_call x1, Pallas kernels, faces(): pl.pallas_call(faces_kernel, in_specs=[HBM], out_specs=[VMEM] * 4, out_sh...  1.77 us
    pallas_call x1, Pallas kernels, both_sides(): pl.pallas_call(sides_kernel, in_specs=[VMEM] * 5 + [HBM], out_specs=[HBM,...  1.54 us
  transfers between devices with their start and end apart: 14, of which 6 were waited for; matrix products, arithmetic and copies ran while one was open for 0% of the time, Pallas kernels for 22%

profile of v4, /device:TPU:1, one launch (start us, length us, event | category | flops | bytes accessed | tf_op | source)
XLA Modules:
  0.0 65.1 jit_solution(8886968519044986642)
XLA Ops:
  0.7 1.8 %faces.1 = (f32[16,16,512]{2,1,0:T(8,128)S(1)}, f32[16,16,512]{2,1,0:T(8,128)S(1)}, f32[16,16,512]{2,1,0:T(8,128)S(1)}, f32[18,16,512]{2,1,0:T(8,128)S(1)}) custom-call(f32[16,16,16,512]{3,2,1,0:T(8,128)} %bitcast.6), custom_call_target="tpu_custom_call" | custom-call | tf_op jit(solution)/shard_map/faces/pallas_call | solution.py:94
  2.5 1.4 %collective-permute-start = (f32[16,16,512]{2,1,0:T(8,128)S(1)}, f32[16,16,512]{2,1,0:T(8,128)S(1)}, u32[]{:S(2)}, u32[]{:S(2)}) collective-permute-start(f32[16,16,512]{2,1,0:T(8,128)S(1)} %get-tuple-element.20), channel_id=1, source_target_pairs={{0,1},{1,0},{2,3},{3,2},{4,5},{5,4},{6,7},{7,6},{8,9},{9,8},{10,11... | collective-permute-start | bytes 1572872 | tf_op jit(solution)/shard_map/ppermute | solution.py:509
  3.9 3.8 %collective-permute-start.1 = (f32[16,16,512]{2,1,0:T(8,128)S(1)}, f32[16,16,512]{2,1,0:T(8,128)S(1)}, u32[]{:S(2)}, u32[]{:S(2)}) collective-permute-start(f32[16,16,512]{2,1,0:T(8,128)S(1)} %get-tuple-element.21), channel_id=1, source_target_pairs={{1,2},{2,1},{3,4},{4,3},{5,6},{6,5},{7,8},{8,7},{9,10},{10,9},{11,... | collective-permute-start | bytes 1572872 | tf_op jit(solution)/shard_map/ppermute | solution.py:509
  7.8 7.1 %collective-permute-done.1.outer = f32[16,16,512]{2,1,0:T(8,128)S(1)} collective-permute-done((f32[16,16,512]{2,1,0:T(8,128)S(1)}, f32[16,16,512]{2,1,0:T(8,128)S(1)}, u32[]{:S(2)}, u32[]{:S(2)}) %collective-permute-start.1) | collective-permute-done | bytes 524320 | tf_op jit(solution)/shard_map/ppermute | solution.py:509
  15.1 0.7 %collective-permute-start.4 = (f32[18,16,512]{2,1,0:T(8,128)S(1)}, f32[18,16,512]{2,1,0:T(8,128)S(1)}, u32[]{:S(2)}, u32[]{:S(2)}) collective-permute-start(f32[18,16,512]{2,1,0:T(8,128)S(1)} %get-tuple-element.26), channel_id=1, source_target_pairs={{16,32},{17,33},{18,34},{19,35},{20,36},{21,37},{22,38},{23,39},{2... | collective-permute-start | bytes 1769480 | tf_op jit(solution)/shard_map/ppermute | solution.py:509
  15.8 5.4 %collective-permute-start.2 = (f32[16,16,512]{2,1,0:T(8,128)S(1)}, f32[16,16,512]{2,1,0:T(8,128)S(1)}, u32[]{:S(2)}, u32[]{:S(2)}) collective-permute-start(f32[16,16,512]{2,1,0:T(8,128)S(1)} %get-tuple-element.23), channel_id=1, source_target_pairs={{0,16},{1,17},{2,18},{3,19},{4,20},{5,21},{6,22},{7,23},{8,24},{9,... | collective-permute-start | bytes 1572872 | tf_op jit(solution)/shard_map/ppermute | solution.py:509
  21.8 2.7 %front.1 = (f32[2,16,128]{2,1,0:T(8,128)S(1)}, f32[2,16,128]{2,1,0:T(8,128)S(1)}, f32[2,16,128]{2,1,0:T(8,128)S(1)}, f32[2,16,128]{2,1,0:T(8,128)S(1)}, bf16[256,512]{1,0:T(8,128)(2,1)S(1)}) custom-call(s32[1,8]{1,0:T(1,128)S(1)} %bitcast.13, s32[1,1]{1,0:T(1,128)S(6)} %copy.16.counts, f32[16,16,16,512]{3,2,1,0:T(8,128)} %bitcast.7, s32[1,256]{1,0:T(1,128)S(1)} %bitcast.11, ...), custom_call_target="tpu_custom_call" | custom-call | tf_op jit(solution)/shard_map/front/pallas_call | solution.py:187
  24.6 1.3 %collective-permute-start.5 = (f32[2,16,128]{2,1,0:T(8,128)S(1)}, f32[2,16,128]{2,1,0:T(8,128)S(1)}, u32[]{:S(2)}, u32[]{:S(2)}) collective-permute-start(f32[2,16,128]{2,1,0:T(8,128)S(1)} %get-tuple-element.31), channel_id=1, source_target_pairs={{0,32},{1,33},{2,34},{3,35},{4,36},{5,37},{6,38},{7,39},{8,40},{9,... | collective-permute-start | bytes 49160 | tf_op jit(solution)/shard_map/ppermute | solution.py:509
  25.9 1.7 %collective-permute-start.6 = (f32[2,16,128]{2,1,0:T(8,128)S(1)}, f32[2,16,128]{2,1,0:T(8,128)S(1)}, u32[]{:S(2)}, u32[]{:S(2)}) collective-permute-start(f32[2,16,128]{2,1,0:T(8,128)S(1)} %get-tuple-element.32), channel_id=1, source_target_pairs={{0,64},{1,65},{2,66},{3,67},{4,68},{5,69},{6,70},{7,71},{8,72},{9,... | collective-permute-start | bytes 49160 | tf_op jit(solution)/shard_map/ppermute | solution.py:509
  27.6 0.9 %collective-permute-start.7 = (f32[2,16,128]{2,1,0:T(8,128)S(1)}, f32[2,16,128]{2,1,0:T(8,128)S(1)}, u32[]{:S(2)}, u32[]{:S(2)}) collective-permute-start(f32[2,16,128]{2,1,0:T(8,128)S(1)} %get-tuple-element.33), channel_id=1, source_target_pairs={{0,96},{1,97},{2,98},{3,99},{4,100},{5,101},{6,102},{7,103},{8,104... | collective-permute-start | bytes 49160 | tf_op jit(solution)/shard_map/ppermute | solution.py:509
  28.7 1.2 %collective-permute-done.6.two = f32[2,16,128]{2,1,0:T(8,128)S(1)} collective-permute-done((f32[2,16,128]{2,1,0:T(8,128)S(1)}, f32[2,16,128]{2,1,0:T(8,128)S(1)}, u32[]{:S(2)}, u32[]{:S(2)}) %collective-permute-start.6) | collective-permute-done | bytes 16416 | tf_op jit(solution)/shard_map/ppermute | solution.py:509
  30.0 1.4 %collective-permute-done.7.three = f32[2,16,128]{2,1,0:T(8,128)S(1)} collective-permute-done((f32[2,16,128]{2,1,0:T(8,128)S(1)}, f32[2,16,128]{2,1,0:T(8,128)S(1)}, u32[]{:S(2)}, u32[]{:S(2)}) %collective-permute-start.7) | collective-permute-done | bytes 16416 | tf_op jit(solution)/shard_map/ppermute | solution.py:509
  31.5 4.7 %collective-permute-start.8 = (f32[3,16,128]{2,1,0:T(8,128)S(1)}, f32[3,16,128]{2,1,0:T(8,128)S(1)}, u32[]{:S(2)}, u32[]{:S(2)}) collective-permute-start(f32[3,16,128]{2,1,0:T(8,128)S(1)} %join.1), channel_id=1, source_target_pairs={{0,2},{1,3},{2,0},{3,1},{4,6},{5,7},{6,4},{7,5},{8,10},{9,11},{10,... | collective-permute-start | bytes 73736 | tf_op jit(solution)/shard_map/ppermute | solution.py:509
  36.2 1.2 %collective-permute-done.8 = f32[3,16,128]{2,1,0:T(8,128)S(1)} collective-permute-done((f32[3,16,128]{2,1,0:T(8,128)S(1)}, f32[3,16,128]{2,1,0:T(8,128)S(1)}, u32[]{:S(2)}, u32[]{:S(2)}) %collective-permute-start.8) | collective-permute-done | bytes 24608 | tf_op jit(solution)/shard_map/ppermute | solution.py:509
  37.4 4.5 %collective-permute-start.9 = (f32[3,16,128]{2,1,0:T(8,128)S(1)}, f32[3,16,128]{2,1,0:T(8,128)S(1)}, u32[]{:S(2)}, u32[]{:S(2)}) collective-permute-start(f32[3,16,128]{2,1,0:T(8,128)S(1)} %add.9), channel_id=1, source_target_pairs={{0,4},{1,5},{2,6},{3,7},{4,0},{5,1},{6,2},{7,3},{8,12},{9,13},{10,... | collective-permute-start | bytes 73736 | tf_op jit(solution)/shard_map/ppermute | solution.py:509
  41.8 2.7 %collective-permute-start.3 = (f32[2,16,512]{2,1,0:T(8,128)S(1)}, f32[2,16,512]{2,1,0:T(8,128)S(1)}, u32[]{:S(2)}, u32[]{:S(2)}) collective-permute-start(f32[2,16,512]{2,1,0:T(8,128)S(1)} %get-tuple-element.25), channel_id=1, source_target_pairs={{0,16},{1,17},{2,18},{3,19},{4,20},{5,21},{6,22},{7,23},{8,24},{9,... | collective-permute-start | bytes 196616 | tf_op jit(solution)/shard_map/ppermute | solution.py:509
  44.6 1.8 %collective-permute-start.10 = (f32[3,16,128]{2,1,0:T(8,128)S(1)}, f32[3,16,128]{2,1,0:T(8,128)S(1)}, u32[]{:S(2)}, u32[]{:S(2)}) collective-permute-start(f32[3,16,128]{2,1,0:T(8,128)S(1)} %add.10), channel_id=1, source_target_pairs={{0,1},{1,0},{2,3},{3,2},{4,5},{5,4},{6,7},{7,6},{8,9},{9,8},{10,11... | collective-permute-start | bytes 73736 | tf_op jit(solution)/shard_map/ppermute | solution.py:509
  46.4 0.8 %collective-permute-done.10 = f32[3,16,128]{2,1,0:T(8,128)S(1)} collective-permute-done((f32[3,16,128]{2,1,0:T(8,128)S(1)}, f32[3,16,128]{2,1,0:T(8,128)S(1)}, u32[]{:S(2)}, u32[]{:S(2)}) %collective-permute-start.10) | collective-permute-done | bytes 24608 | tf_op jit(solution)/shard_map/ppermute | solution.py:509
  47.2 1.3 %collective-permute-start.11 = (f32[3,16,128]{2,1,0:T(8,128)S(1)}, f32[3,16,128]{2,1,0:T(8,128)S(1)}, u32[]{:S(2)}, u32[]{:S(2)}) collective-permute-start(f32[3,16,128]{2,1,0:T(8,128)S(1)} %add.11.zero), channel_id=1, source_target_pairs={{0,8},{1,9},{2,10},{3,11},{4,12},{5,13},{6,14},{7,15},{8,0},{9,1},... | collective-permute-start | bytes 73736 | tf_op jit(solution)/shard_map/ppermute | solution.py:509
  48.5 2.0 %collective-permute-start.12 = (f32[3,16,128]{2,1,0:T(8,128)S(1)}, f32[3,16,128]{2,1,0:T(8,128)S(1)}, u32[]{:S(2)}, u32[]{:S(2)}) collective-permute-start(f32[3,16,128]{2,1,0:T(8,128)S(1)} %add.11.zero), channel_id=1, source_target_pairs={{0,16},{1,17},{2,18},{3,19},{4,20},{5,21},{6,22},{7,23},{8,24},{9,... | collective-permute-start | bytes 73736 | tf_op jit(solution)/shard_map/ppermute | solution.py:509
  50.6 0.5 collective-permute-start.13
  51.1 9.8 %interior.1 = (f32[2,8,16,16,512]{4,3,2,1,0:T(8,128)S(1)}, f32[3,16,16,512]{3,2,1,0:T(8,128)S(1)}, f32[2,8,16,16,512]{4,3,2,1,0:T(8,128)}) custom-call(f32[2,8,16,16,512]{4,3,2,1,0:T(8,128)S(1)} %bitcast.9, bf16[3,16,16,512]{3,2,1,0:T(8,128)(2,1)S(1)} %copy-done.1, f32[16,16,512]{2,1,0:T(8,128)S(1)} %collective-permute-done.inner, ...), custom_call_target="tpu_custom_call" | custom-call | tf_op jit(solution)/shard_map/interior/pallas_call | solution.py:353
  60.9 1.5 %sides.1 = (f32[2,8,16,16,512]{4,3,2,1,0:T(8,128)}, f32[2,16,16,128]{3,2,1,0:T(8,128)S(1)}) custom-call(f32[3,16,16,512]{3,2,1,0:T(8,128)S(1)} %get-tuple-element.22.scales, f32[16,16,512]{2,1,0:T(8,128)S(1)} %collective-permute-done.2.same_plane, f32[2,16,512]{2,1,0:T(8,128)S(1)} %collective-permute-done.3.corner, ...), custom_call_target="tpu_custom_call", output_to_operand_aliasing={{0}: (5, {})} | custom-call | tf_op jit(solution)/shard_map/sides/pallas_call | solution.py:406
  62.5 2.6 %final.1 = (f32[2,8,16,16,512]{4,3,2,1,0:T(8,128)}, f32[2,4,8]{2,1,0:T(4,128)}) custom-call(f32[2,16,16,128]{3,2,1,0:T(8,128)S(1)} %get-tuple-element.29.tiles, f32[3,16,128]{2,1,0:T(8,128)S(1)} %add.11.zero, f32[3,16,128]{2,1,0:T(8,128)S(1)} %collective-permute-done.11.one, ...), custom_call_target="tpu_custom_call", output_to_operand_aliasing={{0}: (7, {})} | custom-call | tf_op jit(solution)/shard_map/final/pallas_call | solution.py:479
  (31 shorter events, 0.5 us)
Async XLA Ops:
  0.6 21.2 %copy-start.5 = (s32[8]{0:T(128)S(1)}, s32[8]{0:T(128)}, u32[]{:S(2)}) copy-start(s32[8]{0:T(128)} %param.12) | copy-start | bytes 100
  0.6 21.2 %copy-start.3 = (s32[1,1,256]{2,1,0:T(1,128)S(1)}, s32[1,1,256]{2,1,0:T(1,128)}, u32[]{:S(2)}) copy-start(s32[1,1,256]{2,1,0:T(1,128)} %param.13) | copy-start | bytes 3076
  0.7 21.2 %copy-start.4 = (s32[1,1,256]{2,1,0:T(1,128)S(1)}, s32[1,1,256]{2,1,0:T(1,128)}, u32[]{:S(2)}) copy-start(s32[1,1,256]{2,1,0:T(1,128)} %param.14) | copy-start | bytes 3076
  0.7 21.2 %copy-start.2 = (f32[2,8,4096]{2,1,0:T(8,128)S(1)}, f32[2,8,4096]{2,1,0:T(8,128)}, u32[]{:S(2)}) copy-start(f32[2,8,4096]{2,1,0:T(8,128)} %param.10) | copy-start | bytes 786436
  0.7 21.2 %copy-start = (bf16[2,4,64,4096]{3,2,1,0:T(8,128)(2,1)S(1)}, bf16[2,4,64,4096]{3,2,1,0:T(8,128)(2,1)}, u32[]{:S(2)}) copy-start(bf16[2,4,64,4096]{3,2,1,0:T(8,128)(2,1)} %matrix.1) | copy-start | bytes 12582916
  0.7 50.4 %slice-start = ((s8[8388608]{0:T(1024)(128)(4,1)}), s8[4194304]{0:T(1024)(128)(4,1)S(1)}, s32[]{:S(2)}) async-start(s8[8388608]{0:T(1024)(128)(4,1)} %bitcast.8), calls=%async_computation | async-start | bytes 8388608
  2.5 48.6 %copy-start.1 = (bf16[3,16,16,512]{3,2,1,0:T(8,128)(2,1)S(1)}, bf16[3,16,16,512]{3,2,1,0:T(8,128)(2,1)}, u32[]{:S(2)}) copy-start(bf16[3,16,16,512]{3,2,1,0:T(8,128)(2,1)} %coefficients.1) | copy-start | bytes 2359300
  2.5 5.3 %collective-permute-start = (f32[16,16,512]{2,1,0:T(8,128)S(1)}, f32[16,16,512]{2,1,0:T(8,128)S(1)}, u32[]{:S(2)}, u32[]{:S(2)}) collective-permute-start(f32[16,16,512]{2,1,0:T(8,128)S(1)} %get-tuple-element.20), channel_id=1, source_target_pairs={{0,1},{1,0},{2,3},{3,2},{4,5},{5,4},{6,7},{7,6},{8,9},{9,8},{10,11... | collective-permute-start | bytes 1572872 | tf_op jit(solution)/shard_map/ppermute | solution.py:509
  3.9 11.0 %collective-permute-start.1 = (f32[16,16,512]{2,1,0:T(8,128)S(1)}, f32[16,16,512]{2,1,0:T(8,128)S(1)}, u32[]{:S(2)}, u32[]{:S(2)}) collective-permute-start(f32[16,16,512]{2,1,0:T(8,128)S(1)} %get-tuple-element.21), channel_id=1, source_target_pairs={{1,2},{2,1},{3,4},{4,3},{5,6},{6,5},{7,8},{8,7},{9,10},{10,9},{11,... | collective-permute-start | bytes 1572872 | tf_op jit(solution)/shard_map/ppermute | solution.py:509
  15.1 45.8 %collective-permute-start.4 = (f32[18,16,512]{2,1,0:T(8,128)S(1)}, f32[18,16,512]{2,1,0:T(8,128)S(1)}, u32[]{:S(2)}, u32[]{:S(2)}) collective-permute-start(f32[18,16,512]{2,1,0:T(8,128)S(1)} %get-tuple-element.26), channel_id=1, source_target_pairs={{16,32},{17,33},{18,34},{19,35},{20,36},{21,37},{22,38},{23,39},{2... | collective-permute-start | bytes 1769480 | tf_op jit(solution)/shard_map/ppermute | solution.py:509
  15.8 34.8 %collective-permute-start.2 = (f32[16,16,512]{2,1,0:T(8,128)S(1)}, f32[16,16,512]{2,1,0:T(8,128)S(1)}, u32[]{:S(2)}, u32[]{:S(2)}) collective-permute-start(f32[16,16,512]{2,1,0:T(8,128)S(1)} %get-tuple-element.23), channel_id=1, source_target_pairs={{0,16},{1,17},{2,18},{3,19},{4,20},{5,21},{6,22},{7,23},{8,24},{9,... | collective-permute-start | bytes 1572872 | tf_op jit(solution)/shard_map/ppermute | solution.py:509
  21.8 29.3 %slice-start.1 = ((s8[8388608]{0:T(1024)(128)(4,1)}), s8[4194304]{0:T(1024)(128)(4,1)S(1)}, s32[]{:S(2)}) async-start(s8[8388608]{0:T(1024)(128)(4,1)} %bitcast.8), calls=%async_computation.1 | async-start | bytes 8388608
  24.6 4.1 %collective-permute-start.5 = (f32[2,16,128]{2,1,0:T(8,128)S(1)}, f32[2,16,128]{2,1,0:T(8,128)S(1)}, u32[]{:S(2)}, u32[]{:S(2)}) collective-permute-start(f32[2,16,128]{2,1,0:T(8,128)S(1)} %get-tuple-element.31), channel_id=1, source_target_pairs={{0,32},{1,33},{2,34},{3,35},{4,36},{5,37},{6,38},{7,39},{8,40},{9,... | collective-permute-start | bytes 49160 | tf_op jit(solution)/shard_map/ppermute | solution.py:509
  25.9 4.1 %collective-permute-start.6 = (f32[2,16,128]{2,1,0:T(8,128)S(1)}, f32[2,16,128]{2,1,0:T(8,128)S(1)}, u32[]{:S(2)}, u32[]{:S(2)}) collective-permute-start(f32[2,16,128]{2,1,0:T(8,128)S(1)} %get-tuple-element.32), channel_id=1, source_target_pairs={{0,64},{1,65},{2,66},{3,67},{4,68},{5,69},{6,70},{7,71},{8,72},{9,... | collective-permute-start | bytes 49160 | tf_op jit(solution)/shard_map/ppermute | solution.py:509
  27.6 3.8 %collective-permute-start.7 = (f32[2,16,128]{2,1,0:T(8,128)S(1)}, f32[2,16,128]{2,1,0:T(8,128)S(1)}, u32[]{:S(2)}, u32[]{:S(2)}) collective-permute-start(f32[2,16,128]{2,1,0:T(8,128)S(1)} %get-tuple-element.33), channel_id=1, source_target_pairs={{0,96},{1,97},{2,98},{3,99},{4,100},{5,101},{6,102},{7,103},{8,104... | collective-permute-start | bytes 49160 | tf_op jit(solution)/shard_map/ppermute | solution.py:509
  31.5 5.9 %collective-permute-start.8 = (f32[3,16,128]{2,1,0:T(8,128)S(1)}, f32[3,16,128]{2,1,0:T(8,128)S(1)}, u32[]{:S(2)}, u32[]{:S(2)}) collective-permute-start(f32[3,16,128]{2,1,0:T(8,128)S(1)} %join.1), channel_id=1, source_target_pairs={{0,2},{1,3},{2,0},{3,1},{4,6},{5,7},{6,4},{7,5},{8,10},{9,11},{10,... | collective-permute-start | bytes 73736 | tf_op jit(solution)/shard_map/ppermute | solution.py:509
  37.4 7.2 %collective-permute-start.9 = (f32[3,16,128]{2,1,0:T(8,128)S(1)}, f32[3,16,128]{2,1,0:T(8,128)S(1)}, u32[]{:S(2)}, u32[]{:S(2)}) collective-permute-start(f32[3,16,128]{2,1,0:T(8,128)S(1)} %add.9), channel_id=1, source_target_pairs={{0,4},{1,5},{2,6},{3,7},{4,0},{5,1},{6,2},{7,3},{8,12},{9,13},{10,... | collective-permute-start | bytes 73736 | tf_op jit(solution)/shard_map/ppermute | solution.py:509
  41.8 19.0 %collective-permute-start.3 = (f32[2,16,512]{2,1,0:T(8,128)S(1)}, f32[2,16,512]{2,1,0:T(8,128)S(1)}, u32[]{:S(2)}, u32[]{:S(2)}) collective-permute-start(f32[2,16,512]{2,1,0:T(8,128)S(1)} %get-tuple-element.25), channel_id=1, source_target_pairs={{0,16},{1,17},{2,18},{3,19},{4,20},{5,21},{6,22},{7,23},{8,24},{9,... | collective-permute-start | bytes 196616 | tf_op jit(solution)/shard_map/ppermute | solution.py:509
  44.6 2.7 %collective-permute-start.10 = (f32[3,16,128]{2,1,0:T(8,128)S(1)}, f32[3,16,128]{2,1,0:T(8,128)S(1)}, u32[]{:S(2)}, u32[]{:S(2)}) collective-permute-start(f32[3,16,128]{2,1,0:T(8,128)S(1)} %add.10), channel_id=1, source_target_pairs={{0,1},{1,0},{2,3},{3,2},{4,5},{5,4},{6,7},{7,6},{8,9},{9,8},{10,11... | collective-permute-start | bytes 73736 | tf_op jit(solution)/shard_map/ppermute | solution.py:509
  47.2 15.2 %collective-permute-start.11 = (f32[3,16,128]{2,1,0:T(8,128)S(1)}, f32[3,16,128]{2,1,0:T(8,128)S(1)}, u32[]{:S(2)}, u32[]{:S(2)}) collective-permute-start(f32[3,16,128]{2,1,0:T(8,128)S(1)} %add.11.zero), channel_id=1, source_target_pairs={{0,8},{1,9},{2,10},{3,11},{4,12},{5,13},{6,14},{7,15},{8,0},{9,1},... | collective-permute-start | bytes 73736 | tf_op jit(solution)/shard_map/ppermute | solution.py:509
  48.5 13.9 %collective-permute-start.12 = (f32[3,16,128]{2,1,0:T(8,128)S(1)}, f32[3,16,128]{2,1,0:T(8,128)S(1)}, u32[]{:S(2)}, u32[]{:S(2)}) collective-permute-start(f32[3,16,128]{2,1,0:T(8,128)S(1)} %add.11.zero), channel_id=1, source_target_pairs={{0,16},{1,17},{2,18},{3,19},{4,20},{5,21},{6,22},{7,23},{8,24},{9,... | collective-permute-start | bytes 73736 | tf_op jit(solution)/shard_map/ppermute | solution.py:509
  50.6 11.9 %collective-permute-start.13 = (f32[3,16,128]{2,1,0:T(8,128)S(1)}, f32[3,16,128]{2,1,0:T(8,128)S(1)}, u32[]{:S(2)}, u32[]{:S(2)}) collective-permute-start(f32[3,16,128]{2,1,0:T(8,128)S(1)} %add.11.zero), channel_id=1, source_target_pairs={{0,24},{1,25},{2,26},{3,27},{4,28},{5,29},{6,30},{7,31},{8,16},{9,... | collective-permute-start | bytes 73736 | tf_op jit(solution)/shard_map/ppermute | solution.py:509
